TPU v7x, 32 devices: a whole 2x2x4 slice. The times are simulated.
32 devices in a mesh: groups: 2 (over x), blk: 8 (over z, y), rows: 2 (over core).
Axes of the slice: x: 2, y: 2, z: 4, core: 2. Of those that a mesh axis runs over, the one named last changes fastest.
Arguments:
- queries: bfloat16 [256, 2048], P(('groups', 'blk'), 'rows'), parts along dimension 0, may hold values from -170 to 170
- cache_keys: bfloat16 [8192, 256], P(('groups', 'blk'), 'rows'), parts along dimension 0, may hold values from -6 to 6
- cache_values: bfloat16 [8192, 256], P(('groups', 'blk'), 'rows'), parts along dimension 0, may hold values from -6 to 6
- span_starts: int32 [4], P('groups'), parts along dimension 0, may hold values from 0 to 4032, as said below
- out_weight: bfloat16 [2048, 2048], P(('rows', 'blk')), may hold values from -0.125 to 0.125
- norm_gain: bfloat16 [2048], replicated, may hold values from 0.099609375 to 1.8984375
- expert_ids: int32 [256, 8], P(('groups', 'blk', 'rows')), parts along dimension 0, may hold values from 0 to 15, all different within a row; in each aligned block of 8 rows (0 to 7, 8 to 15, ...) at most 8 rows name the same one
- gate_fixed: int32 [256, 8], P(('groups', 'blk', 'rows')), parts along dimension 0, may hold values from 1 to 4095
- gate_weight: bfloat16 [16, 2048, 768], P(('blk', 'rows')), may hold values from -0.125 to 0.125
- up_weight: bfloat16 [16, 2048, 768], P(('blk', 'rows')), may hold values from -0.125 to 0.125
- down_weight: bfloat16 [16, 768, 2048], P(('blk', 'rows')), may hold values from -0.21875 to 0.21875
Outputs:
- attn_proj: bfloat16 [256, 2048], P(('groups', 'blk', 'rows')), parts along dimension 0
- expert_out: bfloat16 [256, 2048], P(('groups', 'blk', 'rows')), parts along dimension 0
There are 2 independent parts, one for each index of `groups`. A program takes and returns all parts, laid end to end along the dimension named above; an argument that names none is the same for every part. Nothing has to cross between parts.
Inputs may be any that keep to these rules, and one draw needn't show every extreme that they name: `span_starts`: the last span ends at the last cached position, entry 1 is 4032; entry 0 is at most 3968. `expert_ids`: each token names 8 different experts; among the tokens of one device (aligned blocks of 8 rows) no expert is named more than 8 times.
All inputs are finite; a program needn't handle non-finite values.
Results may differ from a plain program's by a relative error of at most 0.035.
Values may be sent and summed in bfloat16 or wider, within the bound.
No kernel may reach another device: no remote copies, remote signals or barrier semaphores. Data moves between devices by JAX's collectives and lax.ppermute only.
A program may use at most 64 MiB of HBM per device.

v0:
```python
import math

import jax
import jax.numpy as jnp
from jax import lax
from jax.sharding import PartitionSpec as P

HD = 128
SPANS = 2


NEG_FILL = -1e30
EPSILON = 1e-06


def partial_attention(query_block, query_pos, cache_keys, cache_values, key_pos):
    rows_here = query_block.shape[0]
    kv_local = cache_keys.shape[1] // HD
    group_size = query_block.shape[1] // (kv_local * HD)
    heads_here = kv_local * group_size
    shaped_q = query_block.reshape(rows_here, kv_local, group_size, HD)
    shaped_k = cache_keys.reshape(-1, kv_local, HD)
    shaped_v = cache_values.reshape(-1, kv_local, HD)
    scores = jnp.einsum(
        "qgjd,kgd->qgjk", shaped_q, shaped_k, preferred_element_type=jnp.float32
    ) * (1.0 / math.sqrt(HD))
    visible = (key_pos[None, :] <= query_pos[:, None])[:, None, None, :]
    scores = jnp.where(visible, scores, NEG_FILL)
    row_top = jnp.max(scores, axis=-1)
    weights = jnp.where(visible, jnp.exp(scores - row_top[..., None]), 0.0)
    totals = jnp.sum(weights, axis=-1)
    numerator = jnp.einsum(
        "qgjk,kgd->qgjd", weights.astype(jnp.bfloat16), shaped_v, preferred_element_type=jnp.float32
    )
    return (
        row_top.reshape(rows_here, heads_here),
        totals.reshape(rows_here, heads_here),
        numerator.reshape(rows_here, heads_here * HD),
    )


def run_experts(arrived, gate_weight, up_weight, down_weight):
    gate_part = jnp.einsum(
        "secd,edf->secf", arrived, gate_weight, preferred_element_type=jnp.float32
    )
    up_part = jnp.einsum("secd,edf->secf", arrived, up_weight, preferred_element_type=jnp.float32)
    hidden = (jax.nn.silu(gate_part) * up_part).astype(jnp.bfloat16)
    return jnp.einsum(
        "secf,efd->secd", hidden, down_weight, preferred_element_type=jnp.float32
    ).astype(jnp.bfloat16)


def on_device(
    queries,
    cache_keys,
    cache_values,
    span_starts,
    out_weight,
    norm_gain,
    expert_ids,
    gate_fixed,
    gate_weight,
    up_weight,
    down_weight,
):
    gathered = lax.all_gather(queries, "blk", axis=0, tiled=True)
    total_rows = gathered.shape[0]
    width = gathered.shape[1]
    span_length = total_rows // SPANS
    token_index = jnp.arange(total_rows, dtype=jnp.int32)
    span_index = token_index // span_length
    span_match = span_index[:, None] == jnp.arange(SPANS, dtype=jnp.int32)[None, :]
    start_of = jnp.sum(jnp.where(span_match, span_starts[None, :], 0), axis=1)
    query_pos = start_of + token_index % span_length
    cache_rows = cache_keys.shape[0]
    key_pos = lax.axis_index("blk") * cache_rows + jnp.arange(cache_rows, dtype=jnp.int32)
    block_rows = math.gcd(total_rows, 128)
    block_count = total_rows // block_rows

    def one_block(item):
        return partial_attention(item[0], item[1], cache_keys, cache_values, key_pos)

    blocked = (
        gathered.reshape(block_count, block_rows, width),
        query_pos.reshape(block_count, block_rows),
    )
    row_top, totals, numerator = lax.map(one_block, blocked)
    heads_here = row_top.shape[2]
    row_top = row_top.reshape(total_rows, heads_here)
    totals = totals.reshape(total_rows, heads_here)
    numerator = numerator.reshape(total_rows, heads_here * HD)
    global_top = lax.pmax(row_top, "blk")
    factor = jnp.exp(row_top - global_top)
    totals = totals * factor
    numerator = (numerator.reshape(total_rows, heads_here, HD) * factor[:, :, None]).reshape(
        total_rows, heads_here * HD
    )
    own_numer = lax.psum_scatter(
        numerator.astype(jnp.bfloat16), "blk", scatter_dimension=1, tiled=True
    ).astype(jnp.float32)
    all_totals = lax.psum(totals, "blk")
    col_width = own_numer.shape[1]
    first_col = lax.axis_index("blk") * col_width
    spread = jnp.repeat(all_totals, HD, axis=1)
    col_totals = lax.dynamic_slice_in_dim(spread, first_col, col_width, 1)
    attended = (own_numer / col_totals).astype(jnp.bfloat16)
    projected = lax.psum_scatter(
        jnp.dot(attended, out_weight, preferred_element_type=jnp.float32),
        ("blk", "rows"),
        scatter_dimension=0,
        tiled=True,
    )
    attn_proj = projected.astype(jnp.bfloat16)
    values_f = attn_proj.astype(jnp.float32)
    mean_square = jnp.mean(values_f * values_f, axis=-1, keepdims=True)
    normed = (values_f * lax.rsqrt(mean_square + EPSILON) * norm_gain.astype(jnp.float32)).astype(
        jnp.bfloat16
    )
    own_tokens = normed.shape[0]
    top_count = expert_ids.shape[1]
    owners = lax.axis_size("blk") * lax.axis_size("rows")
    local_experts = gate_weight.shape[0]
    expert_count = owners * local_experts
    capacity = min(own_tokens, max(2, 2 * top_count * own_tokens // expert_count))
    slot_total = expert_count * capacity
    route_expert = expert_ids.reshape(-1)
    route_count = route_expert.shape[0]
    hits = (route_expert[:, None] == jnp.arange(expert_count, dtype=jnp.int32)[None, :]).astype(
        jnp.int32
    )
    slot_number = jnp.sum(jnp.cumsum(hits, axis=0) * hits, axis=1) - 1
    target = route_expert * capacity + slot_number
    placed = target[:, None] == jnp.arange(slot_total, dtype=jnp.int32)[None, :]
    route_token = jnp.arange(route_count, dtype=jnp.int32) // top_count
    token_pick = route_token[:, None] == jnp.arange(own_tokens, dtype=jnp.int32)[None, :]
    slot_token = jnp.dot(
        placed.astype(jnp.bfloat16).T,
        token_pick.astype(jnp.bfloat16),
        preferred_element_type=jnp.float32,
    ).astype(jnp.bfloat16)
    outgoing = jnp.dot(slot_token, normed, preferred_element_type=jnp.float32).astype(jnp.bfloat16)
    outgoing = outgoing.reshape(owners, local_experts, capacity, -1)
    gate_values = gate_fixed.astype(jnp.float32)
    route_weight = (gate_values / jnp.sum(gate_values, axis=1, keepdims=True)).reshape(-1)
    weighted_pick = token_pick.astype(jnp.float32) * route_weight[:, None]
    blend = jnp.dot(weighted_pick.T, placed.astype(jnp.float32), precision=lax.Precision.HIGHEST)
    finished = run_experts(
        lax.all_to_all(outgoing, ("blk", "rows"), split_axis=0, concat_axis=0, tiled=True),
        gate_weight,
        up_weight,
        down_weight,
    )
    returned = lax.all_to_all(finished, ("blk", "rows"), split_axis=0, concat_axis=0, tiled=True)
    returned_flat = returned.reshape(slot_total, -1)
    mixed = jnp.dot(blend, returned_flat.astype(jnp.float32), precision=lax.Precision.HIGHEST)
    expert_out = mixed.astype(jnp.bfloat16)
    return (attn_proj, expert_out)


def solution(mesh):
    in_specs = (
        P(("groups", "blk"), "rows"),
        P(("groups", "blk"), "rows"),
        P(("groups", "blk"), "rows"),
        P("groups"),
        P(("rows", "blk"), None),
        P(),
        P(("groups", "blk", "rows"), None),
        P(("groups", "blk", "rows"), None),
        P(("blk", "rows"), None, None),
        P(("blk", "rows"), None, None),
        P(("blk", "rows"), None, None),
    )
    out_specs = (P(("groups", "blk", "rows"), None), P(("groups", "blk", "rows"), None))
    return jax.shard_map(
        on_device, mesh=mesh, in_specs=in_specs, out_specs=out_specs, check_vma=False
    )
```

profile of v0, /device:TPU:0, one launch (start us, length us, event | category | flops | bytes accessed | tf_op | source)
XLA Modules:
  0.0 248.1 jit_solution(16907521409882701303)
XLA Ops:
  7.2 0.0 copy-start
  7.2 0.0 reduce-scatter.3.cloned.1.call-start
  7.3 0.9 fusion.69
  8.2 34.8 %all_gather.3 = bf16[128,1024]{1,0:T(8,128)(2,1)} all-gather(bf16[16,1024]{1,0:T(8,128)(2,1)} %param.11), channel_id=1, replica_groups=mesh['groups'=2,'blk'=8,'rows'=2] {'blk'}, dimensions={0}, use_global_device_ids=true | all-gather | bytes 294912 | tf_op jit(solution)/shard_map/all_gather | solution.py:66
  42.9 1.1 copy.25
  44.0 0.1 broadcast_compare_fusion
  44.2 2.7 %fusion.13 = (f32[128,8]{0,1:T(8,128)S(1)}, f32[512,128,8]{1,0,2:T(8,128)}) fusion(pred[128,512]{0,1:T(8,128)(4,1)S(1)} %broadcast_compare_fusion, bf16[128,8,128]{0,2,1:T(8,128)(2,1)S(1)} %bitcast.116, bf16[512,128]{1,0:T(8,128)(2,1)} %param.12), kind=kOutput, calls=%fused_computation.13 | convolution fusion | flops 135789568 | bytes 2560000 | tf_op jit(solution)/shard_map/while/body/eval_jaxpr/qgjd,kgd->qgjk/dot_general | solution.py:24
  46.9 21.3 %pmax.7 = f32[128,8]{0,1:T(8,128)S(1)} all-reduce(f32[128,8]{0,1:T(8,128)S(1)} %get-tuple-element.24), channel_id=1, replica_groups=mesh['groups'=2,'blk'=8,'rows'=2] {'blk'}, use_global_device_ids=true, to_apply=%region_2.3 | all-reduce | flops 1024 | bytes 8192 | tf_op jit(solution)/shard_map/pmax | solution.py:92
  68.2 0.0 copy-start.1
  68.2 2.2 fusion.14
  70.5 0.0 copy-done.1
  70.5 1.5 fusion.32
  72.0 0.0 copy-start.6
  72.0 0.0 copy-start.5
  72.1 0.7 fusion.37
  72.8 0.0 reduce-scatter.3.cloned.1.call-update
  72.8 0.0 reduce-scatter.5.cloned.1.call-start
  72.9 17.1 %psum.7 = f32[128,8]{0,1:T(8,128)S(1)} all-reduce(f32[128,8]{0,1:T(8,128)S(1)} %get-tuple-element.22), channel_id=1, replica_groups=mesh['groups'=2,'blk'=8,'rows'=2] {'blk'}, use_global_device_ids=true, to_apply=%region_5.6 | all-reduce | flops 1024 | bytes 8192 | tf_op jit(solution)/shard_map/psum | solution.py:101
  90.0 42.7 %reduce-scatter.3.cloned.1.call-done = bf16[128,128]{0,1:T(8,128)(2,1)} async-done(((bf16[128,1024]{0,1:T(8,128)(2,1)}), bf16[128,128]{0,1:T(8,128)(2,1)}) %reduce-scatter.3.cloned.1.call-update) | async-done | bytes 32784 | tf_op jit(solution)/shard_map/reduce_scatter | solution.py:98
  132.7 2.4 fusion.54
  135.1 0.0 reduce-scatter.5.cloned.1.call-update
  135.1 0.0 copy-done.6
  135.1 0.1 reshape.171
  135.2 0.1 fusion.59
  135.3 0.1 reduce_window_sum.11
  135.4 0.0 copy-done.5
  135.4 0.2 select_reduce_fusion
  135.6 57.3 %reduce-scatter.5.cloned.1.call-done = f32[8,2048]{1,0:T(8,128)} async-done(((f32[128,2048]{1,0:T(8,128)}), f32[8,2048]{1,0:T(8,128)}) %reduce-scatter.5.cloned.1.call-update) | async-done | bytes 65552 | tf_op jit(solution)/shard_map/reduce_scatter | solution.py:107
  192.9 1.0 fusion.51
  193.9 0.0 copy-start.3
  193.9 1.4 fusion.12
  195.3 0.0 copy-done.3
  195.3 18.0 %all_to_all.10 = bf16[16,1,8,2048]{3,2,1,0:T(8,128)(2,1)S(1)} all-to-all(bf16[16,1,8,2048]{3,2,1,0:T(8,128)(2,1)} %fusion.12), channel_id=1, replica_groups=mesh['groups'=2,'blk'=8,'rows'=2] {'blk','rows'}, dimensions={0} | all-to-all | bytes 1048576 | tf_op jit(solution)/shard_map/all_to_all | solution.py:148
  213.3 0.0 copy-start.2
  213.3 0.8 copy-done.2
  214.2 2.5 fusion.16
  216.6 0.0 copy-done
  216.6 0.0 copy-start.4
  216.7 4.1 %fusion.9 = bf16[16,1,8,2048]{3,2,1,0:T(8,128)(2,1)} fusion(bf16[1,768,2048]{2,1,0:T(8,128)(2,1)S(1)} %copy-done, bf16[1,2048,768]{2,1,0:T(8,128)(2,1)} %param.20, bf16[16,1,8,2048]{3,2,1,0:T(8,128)(2,1)} %copy-done.2, f32[16,1,8,768]{3,2,0,1:T(8,128)S(1)} %fusion.16), kind=kOutput, calls=%fused_computation.8 | convolution fusion | flops 806158336 | bytes 7733248 | tf_op jit(solution)/shard_map/secf,efd->secd/dot_general | solution.py:48
  220.7 4.2 %all-to-all-start.1 = ((bf16[16,1,8,2048]{3,2,1,0:T(8,128)(2,1)}), bf16[16,1,8,2048]{3,2,1,0:T(8,128)(2,1)}, u32[]{:S(2)}, u32[]{:S(2)}) async-start(bf16[16,1,8,2048]{3,2,1,0:T(8,128)(2,1)} %fusion.9), calls=%async_computation.3 | async-start | bytes 1048576 | tf_op jit(solution)/shard_map/all_to_all | solution.py:153
  225.0 0.0 copy-done.4
  225.0 0.1 convert_reduce_fusion
  225.1 0.1 convert_divide_fusion
  225.2 0.1 mul.86
  225.3 0.3 fusion.58
  225.5 13.8 %all-to-all-done.1 = bf16[16,1,8,2048]{3,2,1,0:T(8,128)(2,1)} async-done(((bf16[16,1,8,2048]{3,2,1,0:T(8,128)(2,1)}), bf16[16,1,8,2048]{3,2,1,0:T(8,128)(2,1)}, u32[]{:S(2)}, u32[]{:S(2)}) %all-to-all-start.1) | async-done | bytes 524320 | tf_op jit(solution)/shard_map/all_to_all | solution.py:153
  239.3 2.0 convolution_convert_fusion.1
  (8 shorter events, 0.1 us)
Async XLA Ops:
  7.2 209.5 %copy-start = (bf16[1,768,2048]{2,1,0:T(8,128)(2,1)S(1)}, bf16[1,768,2048]{2,1,0:T(8,128)(2,1)}, u32[]{:S(2)}) copy-start(bf16[1,768,2048]{2,1,0:T(8,128)(2,1)} %param.21) | copy-start | bytes 9437188
  7.2 125.5 %reduce-scatter.3.cloned.1.call-start = ((), (), s32[]{:S(2)}) async-start(), calls=%async_computation.4 | async-start | bytes 294912 | tf_op jit(solution)/shard_map/reduce_scatter | solution.py:98
  68.2 2.3 copy-start.1
  72.0 63.1 %copy-start.6 = (s32[8,8]{1,0:T(8,128)S(1)}, s32[8,8]{1,0:T(8,128)}, u32[]{:S(2)}) copy-start(s32[8,8]{1,0:T(8,128)} %param.17) | copy-start | bytes 772
  72.0 63.4 %copy-start.5 = (bf16[2048]{0:T(1024)(128)(2,1)S(1)}, bf16[2048]{0:T(1024)(128)(2,1)}, u32[]{:S(2)}) copy-start(bf16[2048]{0:T(1024)(128)(2,1)} %param.16) | copy-start | bytes 12292
  72.8 120.1 %reduce-scatter.5.cloned.1.call-start = ((), (), s32[]{:S(2)}) async-start(), calls=%async_computation.5 | async-start | bytes 1114112 | tf_op jit(solution)/shard_map/reduce_scatter | solution.py:107
  193.9 1.4 copy-start.3
  213.3 0.8 copy-start.2
  216.6 8.3 %copy-start.4 = (s32[8,8]{1,0:T(8,128)S(1)}, s32[8,8]{1,0:T(8,128)}, u32[]{:S(2)}) copy-start(s32[8,8]{1,0:T(8,128)} %param.18) | copy-start | bytes 772
  220.7 18.6 %all-to-all-start.1 = ((bf16[16,1,8,2048]{3,2,1,0:T(8,128)(2,1)}), bf16[16,1,8,2048]{3,2,1,0:T(8,128)(2,1)}, u32[]{:S(2)}, u32[]{:S(2)}) async-start(bf16[16,1,8,2048]{3,2,1,0:T(8,128)(2,1)} %fusion.9), calls=%async_computation.3 | async-start | bytes 1048576 | tf_op jit(solution)/shard_map/all_to_all | solution.py:153
Sparse Core Ops, SparseCore 0:
  72.9 59.7 reduce-scatter.2
  136.3 56.6 reduce-scatter.4
where the time goes:
time: 249 us; the launch traced here: 248 us
  waiting for transfers between devices  114 us (46%)
  blocking collectives  91.3 us (37%)
  matrix products  16.8 us (7%)
  between operations  14.2 us (6%)
  other arithmetic  5.54 us (2%)
  starting transfers between devices  4.32 us (2%)
    reduce_scatter x1, waiting for transfers between devices, on_device(): lax.psum_scatter(jnp.dot(attended, out_weight, preferred_element_type=jnp...  57.3 us
    reduce_scatter x1, waiting for transfers between devices, on_device(): lax.psum_scatter(numerator.astype(jnp.bfloat16), 'blk', scatter_dimension...  42.7 us
    all_gather x1, blocking collectives, on_device(): gathered = lax.all_gather(queries, 'blk', axis=0, tiled=True)  34.8 us
    pmax x1, blocking collectives, on_device(): global_top = lax.pmax(row_top, 'blk')  21.3 us
    all_to_all x1, blocking collectives, on_device(): lax.all_to_all(outgoing, ('blk', 'rows'), split_axis=0, concat_axis=0, ti...  18 us
    psum x1, blocking collectives, on_device(): all_totals = lax.psum(totals, 'blk')  17.1 us
    all_to_all x1, waiting for transfers between devices, on_device(): lax.all_to_all(finished, ('blk', 'rows'), split_axis=0, concat_axis=0, ti...  13.8 us
  transfers between devices with their start and end apart: 3, of which 3 were waited for; matrix products, arithmetic and copies ran while one was open for 0% of the time, Pallas kernels for 0%

commit v1 on v0

--- a/solution.py
+++ b/solution.py
@@ -1,8 +1,11 @@
+import functools
 import math
 
 import jax
 import jax.numpy as jnp
 from jax import lax
+from jax.experimental import pallas as pl
+from jax.experimental.pallas import tpu as pltpu
 from jax.sharding import PartitionSpec as P
 
 HD = 128
@@ -156,6 +159,340 @@
     expert_out = mixed.astype(jnp.bfloat16)
     return (attn_proj, expert_out)
 
+def far_of(step, blk):
+    return [(at, ((at // 2) ^ step) * 2 + at % 2) for at in range(blk)]
+
+
+def side_of(size):
+    return [(at, at ^ 1) for at in range(size)]
+
+
+def in_vmem(count):
+    return [pl.BlockSpec(memory_space=pltpu.VMEM)] * count
+
+
+def attend_kernel(sizes, meta, *refs):
+    far_count, span_length, cache_rows, heads = sizes
+    q_refs = refs[:far_count]
+    key_own, key_side, value_own, value_side, ids, gates = refs[far_count : far_count + 6]
+    outs = refs[far_count + 6 : 2 * far_count + 6]
+    q_all, pos_all, keys, values, staged = refs[2 * far_count + 6 :]
+    far, near = meta[0], meta[1]
+    piece = q_refs[0].shape[0]
+    tokens = far_count * piece
+    own_heads = heads // far_count
+    for step in range(far_count):
+        source = far ^ step
+        first = (source * 2 + near) * piece
+        base = meta[2 + first // span_length] + first % span_length
+        row = pl.multiple_of(source * piece, piece)
+        for head in range(heads):
+            q_all[pl.ds(head * tokens + row, piece), :] = q_refs[step][:, head * HD : (head + 1) * HD]
+        pos_all[pl.ds(row, piece), :] = base + lax.broadcasted_iota(jnp.int32, (piece, HD), 0)
+    keys[:cache_rows, :] = key_own[...]
+    keys[cache_rows:, :] = key_side[...]
+    values[:cache_rows, :] = value_own[...]
+    values[cache_rows:, :] = value_side[...]
+    lane_at = lax.broadcasted_iota(jnp.int32, (1, 2 * cache_rows), 1)
+    own_first = (far * 2 + near) * cache_rows
+    side_first = (far * 2 + 1 - near) * cache_rows - cache_rows
+    key_pos = lane_at + jnp.where(lane_at < cache_rows, own_first, side_first)
+    visible = key_pos <= pos_all[:, :1]
+    gate_values = gates[...].astype(jnp.float32)
+    route_weight = gate_values / jnp.sum(gate_values, axis=1, keepdims=True)
+    own_tokens, top_count = gates.shape
+    expert_lane = lax.broadcasted_iota(jnp.int32, (own_tokens, HD), 1) - HD // 2
+    weight_of = jnp.zeros((own_tokens, HD), jnp.float32)
+    for k in range(top_count):
+        weight_of += jnp.where(expert_lane == ids[:, k : k + 1], route_weight[:, k : k + 1], 0.0)
+    high = weight_of.astype(jnp.bfloat16).astype(jnp.float32)
+    routes = jnp.concatenate(
+        [high, weight_of - high, jnp.zeros((tokens - 2 * own_tokens, HD), jnp.float32)], axis=0
+    )
+    lane = lax.broadcasted_iota(jnp.int32, (tokens, HD), 1)
+    scale = 1.0 / math.sqrt(HD)
+    for group in range(far_count):
+        rows = group * own_heads * tokens
+        scores = lax.dot_general(
+            q_all[rows : rows + own_heads * tokens, :],
+            keys[...],
+            (((1,), (1,)), ((), ())),
+            preferred_element_type=jnp.float32,
+        )
+        extra = routes
+        weights_16 = []
+        for j in range(own_heads):
+            part = jnp.where(visible, scores[j * tokens : (j + 1) * tokens] * scale, NEG_FILL)
+            top = jnp.maximum(jnp.max(part, axis=1, keepdims=True), NEG_FILL / 10)
+            top = top.astype(jnp.bfloat16).astype(jnp.float32)
+            weights = jnp.exp(part - top)
+            total = jnp.sum(weights, axis=1, keepdims=True)
+            total_high = total.astype(jnp.bfloat16).astype(jnp.float32)
+            extra = jnp.where(lane == 3 * j, top, extra)
+            extra = jnp.where(lane == 3 * j + 1, total_high, extra)
+            extra = jnp.where(lane == 3 * j + 2, total - total_high, extra)
+            weights_16.append(weights.astype(jnp.bfloat16))
+        numerator = jnp.dot(
+            jnp.concatenate(weights_16, axis=0), values[...], preferred_element_type=jnp.float32
+        ).astype(jnp.bfloat16)
+        for j in range(own_heads):
+            staged[group, :, j * HD : (j + 1) * HD] = numerator[j * tokens : (j + 1) * tokens]
+        staged[group, :, own_heads * HD :] = extra.astype(jnp.bfloat16)
+    for step in range(far_count):
+        outs[step][...] = staged[far ^ step]
+
+
+def project_kernel(sizes, meta, *refs):
+    far_count, own_heads, own_tokens = sizes
+    messages = refs[:far_count]
+    weight_own, weight_side, keep, send, routes, partial = refs[far_count:]
+    far, near, row_at = meta[0], meta[1], meta[2]
+    tokens = messages[0].shape[0]
+    attended = []
+    extras = [m[:, own_heads * HD :].astype(jnp.float32) for m in messages]
+    for j in range(own_heads):
+        tops = [e[:, 3 * j : 3 * j + 1] for e in extras]
+        best = tops[0]
+        for top in tops[1:]:
+            best = jnp.maximum(best, top)
+        above = jnp.zeros((tokens, HD), jnp.float32)
+        below = jnp.zeros((tokens, 1), jnp.float32)
+        for top, e, m in zip(tops, extras, messages):
+            factor = jnp.exp(top - best)
+            above += factor * m[:, j * HD : (j + 1) * HD].astype(jnp.float32)
+            below += factor * (e[:, 3 * j + 1 : 3 * j + 2] + e[:, 3 * j + 2 : 3 * j + 3])
+        attended.append(above / below)
+    first = jnp.where(near == 0, attended[0], attended[1]).astype(jnp.bfloat16)
+    second = jnp.where(near == 0, attended[1], attended[0]).astype(jnp.bfloat16)
+    partial[...] = jnp.dot(
+        first, weight_own[...], preferred_element_type=jnp.float32
+    ) + jnp.dot(second, weight_side[...], preferred_element_type=jnp.float32)
+    piece = tokens // far_count
+    other = 1 - row_at
+    mine, theirs = [], []
+    for source in range(far_count):
+        at = pl.multiple_of(source * piece + row_at * own_tokens, own_tokens)
+        mine.append(partial[pl.ds(at, own_tokens), :])
+        at = pl.multiple_of(source * piece + other * own_tokens, own_tokens)
+        theirs.append(partial[pl.ds(at, own_tokens), :])
+    keep[...] = jnp.concatenate(mine, axis=0)
+    send[...] = jnp.concatenate(theirs, axis=0).astype(jnp.bfloat16)
+    for step in range(far_count):
+        e = extras[step]
+        at = pl.multiple_of((far ^ step) * own_tokens, own_tokens)
+        routes[pl.ds(at, own_tokens), :] = e[:own_tokens] + e[own_tokens : 2 * own_tokens]
+
+
+def norm_kernel(sizes, meta, *refs):
+    far_count, own_tokens = sizes
+    parts = refs[:far_count]
+    gain, routes, own_rows, spread, summed = refs[far_count:]
+    width = gain.shape[1]
+    total = parts[0][...].astype(jnp.float32)
+    for part in parts[1:]:
+        total += part[...].astype(jnp.float32)
+    values_f = total.astype(jnp.bfloat16).astype(jnp.float32)
+    summed[...] = values_f
+    at = pl.multiple_of(meta[0] * own_tokens, own_tokens)
+    own_rows[...] = summed[pl.ds(at, own_tokens), :].astype(jnp.bfloat16)
+    mean_square = jnp.mean(values_f * values_f, axis=1, keepdims=True)
+    spread[:, :width] = (
+        values_f * lax.rsqrt(mean_square + EPSILON) * gain[...].astype(jnp.float32)
+    ).astype(jnp.bfloat16)
+    weight_of = routes[...]
+    high = weight_of.astype(jnp.bfloat16).astype(jnp.float32)
+    low = pltpu.roll(weight_of - high, HD // 2, 1)
+    high = pltpu.roll(high, HD // 2, 1)
+    lane = lax.broadcasted_iota(jnp.int32, weight_of.shape, 1)
+    spread[:, width:] = jnp.where(
+        lane < HD // 2, high, pltpu.roll(low, HD // 2, 1)
+    ).astype(jnp.bfloat16)
+
+
+def expert_kernel(width, meta, *refs):
+    pieces = refs[:4]
+    gate, up, down, keep, send, gathered, total = refs[4:]
+    rows = pieces[0].shape[0]
+    step = pl.program_id(0)
+
+    @pl.when(step == 0)
+    def _():
+        for at, piece in enumerate(pieces):
+            gathered[at * rows : (at + 1) * rows, :] = piece[:, :width]
+        total[...] = jnp.zeros_like(total)
+
+    arrived = gathered[...]
+    gate_part = jnp.dot(arrived, gate[0], preferred_element_type=jnp.float32)
+    up_part = jnp.dot(arrived, up[0], preferred_element_type=jnp.float32)
+    hidden = (gate_part / (1.0 + jnp.exp(-gate_part)) * up_part).astype(jnp.bfloat16)
+    total[...] += jnp.dot(hidden, down[0], preferred_element_type=jnp.float32)
+
+    @pl.when(step == pl.num_programs(0) - 1)
+    def _():
+        lane = lax.broadcasted_iota(jnp.int32, (rows, HD), 1) % (HD // 2)
+        for at, piece in enumerate(pieces):
+            routes = piece[:, width:].astype(jnp.float32)
+            share = jnp.sum(jnp.where(lane == meta[0], routes, 0.0), axis=1, keepdims=True)
+            result = total[at * rows : (at + 1) * rows, :].astype(jnp.bfloat16).astype(jnp.float32)
+            target = keep if at < 2 else send
+            half = at % 2
+            target[half * rows : (half + 1) * rows, :] = (share * result).astype(jnp.bfloat16)
+
+
+def spread_kernel(sizes, meta, *refs):
+    far_count, own_tokens = sizes
+    ours, theirs = refs[:2]
+    outs = refs[2 : 2 + far_count]
+    summed = refs[2 + far_count]
+    summed[...] = ours[...].astype(jnp.float32) + theirs[...].astype(jnp.float32)
+    for step in range(far_count):
+        at = pl.multiple_of((meta[0] ^ step) * own_tokens, own_tokens)
+        outs[step][...] = summed[pl.ds(at, own_tokens), :].astype(outs[step].dtype)
+
+
+def paired_device(
+    queries,
+    cache_keys,
+    cache_values,
+    span_starts,
+    out_weight,
+    norm_gain,
+    expert_ids,
+    gate_fixed,
+    gate_weight,
+    up_weight,
+    down_weight,
+):
+    blk, row_count = lax.axis_size("blk"), lax.axis_size("rows")
+    far_count = blk // 2
+    piece, query_width = queries.shape
+    heads = query_width // HD
+    own_heads = heads // far_count
+    own_tokens = expert_ids.shape[0]
+    tokens = far_count * piece
+    held = far_count * own_tokens
+    width = out_weight.shape[1]
+    cache_rows = cache_keys.shape[0]
+    span_length = blk * piece // SPANS
+    hidden = gate_weight.shape[2]
+    blk_at, row_at = lax.axis_index("blk"), lax.axis_index("rows")
+    far, near = blk_at // 2, blk_at % 2
+    bf16, f32 = jnp.bfloat16, jnp.float32
+    smem = pl.BlockSpec(memory_space=pltpu.SMEM)
+    shape_of = jax.ShapeDtypeStruct
+
+    def over_far(arrays):
+        moved = [lax.ppermute(arrays[step], "blk", far_of(step, blk)) for step in range(far_count - 1, 0, -1)]
+        return [arrays[0]] + moved[::-1]
+
+    def over_near(array):
+        return lax.ppermute(array, "blk", side_of(blk))
+
+    def over_rows(array):
+        return lax.ppermute(array, "rows", side_of(row_count))
+
+    q_pieces = over_far([queries] * far_count)
+    key_side, value_side = over_near(cache_keys), over_near(cache_values)
+    weight_side = over_near(out_weight)
+    place = jnp.concatenate([jnp.stack([far, near]).astype(jnp.int32), span_starts])
+    message_width = (own_heads + 1) * HD
+    messages = pl.pallas_call(
+        functools.partial(attend_kernel, (far_count, span_length, cache_rows, heads)),
+        out_shape=[shape_of((tokens, message_width), bf16)] * far_count,
+        in_specs=[smem] + in_vmem(far_count + 6),
+        out_specs=in_vmem(far_count),
+        scratch_shapes=[
+            pltpu.VMEM((heads * tokens, HD), bf16),
+            pltpu.VMEM((tokens, HD), jnp.int32),
+            pltpu.VMEM((2 * cache_rows, HD), bf16),
+            pltpu.VMEM((2 * cache_rows, HD), bf16),
+            pltpu.VMEM((far_count, tokens, message_width), bf16),
+        ],
+        name="attend",
+    )(place, *q_pieces, cache_keys, key_side, cache_values, value_side, expert_ids, gate_fixed)
+    messages = over_far(messages)
+    place = jnp.stack([far, near, row_at]).astype(jnp.int32)
+    keep, send, routes = pl.pallas_call(
+        functools.partial(project_kernel, (far_count, own_heads, own_tokens)),
+        out_shape=[shape_of((held, width), f32), shape_of((held, width), bf16), shape_of((held, HD), f32)],
+        in_specs=[smem] + in_vmem(far_count + 2),
+        out_specs=in_vmem(3),
+        scratch_shapes=[pltpu.VMEM((tokens, width), f32)],
+        name="project",
+    )(place, *messages, out_weight, weight_side)
+    part = (keep + over_rows(send).astype(f32)).astype(bf16)
+    parts = over_far([part] * far_count)
+    place = jnp.stack([far]).astype(jnp.int32)
+    attn_proj, normed = pl.pallas_call(
+        functools.partial(norm_kernel, (far_count, own_tokens)),
+        out_shape=[shape_of((own_tokens, width), bf16), shape_of((held, width + HD), bf16)],
+        in_specs=[smem] + in_vmem(far_count + 2),
+        out_specs=in_vmem(2),
+        scratch_shapes=[pltpu.VMEM((held, width), f32)],
+        name="norm",
+    )(place, *parts, norm_gain.reshape(1, width), routes)
+    from_side = over_near(normed)
+    pieces = [normed, from_side, over_rows(normed), over_rows(from_side)]
+    chunk = math.gcd(hidden, 256)
+    place = jnp.stack([blk_at * row_count + row_at]).astype(jnp.int32)
+    whole = pl.BlockSpec((held, width + HD), lambda f: (0, 0))
+    keep, send = pl.pallas_call(
+        functools.partial(expert_kernel, width),
+        out_shape=[shape_of((2 * held, width), bf16)] * 2,
+        grid=(hidden // chunk,),
+        in_specs=[smem]
+        + [whole] * 4
+        + [
+            pl.BlockSpec((1, width, chunk), lambda f: (0, 0, f)),
+            pl.BlockSpec((1, width, chunk), lambda f: (0, 0, f)),
+            pl.BlockSpec((1, chunk, width), lambda f: (0, f, 0)),
+        ],
+        out_specs=[pl.BlockSpec((2 * held, width), lambda f: (0, 0))] * 2,
+        scratch_shapes=[pltpu.VMEM((4 * held, width), bf16), pltpu.VMEM((4 * held, width), f32)],
+        name="experts",
+    )(place, *pieces, gate_weight, up_weight, down_weight)
+    both = keep.astype(f32) + over_rows(send).astype(f32)
+    ours, theirs = both[:held], both[held:].astype(bf16)
+    theirs = over_near(theirs)
+    place = jnp.stack([far]).astype(jnp.int32)
+    shares = pl.pallas_call(
+        functools.partial(spread_kernel, (far_count, own_tokens)),
+        out_shape=[shape_of((own_tokens, width), f32)] + [shape_of((own_tokens, width), bf16)] * (far_count - 1),
+        in_specs=[smem] + in_vmem(2),
+        out_specs=in_vmem(far_count),
+        scratch_shapes=[pltpu.VMEM((held, width), f32)],
+        name="shares",
+    )(place, ours, theirs)
+    shares = over_far(shares)
+    total = shares[0]
+    for share in shares[1:]:
+        total = total + share.astype(f32)
+    return (attn_proj, total.astype(bf16))
+
+
+def fits_pairs(mesh, queries, cache_keys, out_weight, expert_ids, gate_weight):
+    blk, row_count = mesh.shape["blk"], mesh.shape["rows"]
+    parts = mesh.shape["groups"]
+    far_count = blk // 2
+    if blk % 2 or row_count != 2 or far_count < 2 or far_count & (far_count - 1):
+        return False
+    heads = queries.shape[1] // (row_count * HD)
+    piece = queries.shape[0] // (parts * blk)
+    own_tokens = expert_ids.shape[0] // (parts * blk * row_count)
+    experts = gate_weight.shape[0]
+    return (
+        cache_keys.shape[1] == row_count * HD
+        and heads == 2 * far_count
+        and out_weight.shape[0] == row_count * blk * HD
+        and out_weight.shape[1] % HD == 0
+        and piece == 2 * own_tokens
+        and own_tokens % 8 == 0
+        and (blk * piece // SPANS) % piece == 0
+        and experts == blk * row_count
+        and experts <= HD // 2
+        and gate_weight.shape[2] % 128 == 0
+    )
+
 
 def solution(mesh):
     in_specs = (
@@ -172,6 +509,17 @@
         P(("blk", "rows"), None, None),
     )
     out_specs = (P(("groups", "blk", "rows"), None), P(("groups", "blk", "rows"), None))
-    return jax.shard_map(
-        on_device, mesh=mesh, in_specs=in_specs, out_specs=out_specs, check_vma=False
-    )
+
+    def run(*arrays):
+        queries, cache_keys, out_weight = arrays[0], arrays[1], arrays[4]
+        expert_ids, gate_weight = arrays[6], arrays[8]
+        paired = fits_pairs(mesh, queries, cache_keys, out_weight, expert_ids, gate_weight)
+        return jax.shard_map(
+            paired_device if paired else on_device,
+            mesh=mesh,
+            in_specs=in_specs,
+            out_specs=out_specs,
+            check_vma=False,
+        )(*arrays)
+
+    return run

time: 249 us -> 92.8 us (0.37)
  blocking collectives: 91.3 us -> 0 us
  waiting for transfers between devices: 114 us -> 36.7 us
  starting transfers between devices: 4.32 us -> 27.8 us
  matrix products: 16.8 us -> 0 us
  Pallas kernels: 0 us -> 16.5 us
  between operations: 14.2 us -> 0.75 us
  local copies, waits for them, and re-layouts: 2.16 us -> 5.46 us
    reduce_scatter x2 -> x0, waiting for transfers between devices: 100 us -> none  [the longest x1 57.3 us: on_device(): lax.psum_scatter(jnp.dot(attended, out_weight, preferred_element_type=jnp...]
    ppermute x0 -> x21, waiting for transfers between devices: none -> 36.7 us  [the longest x12 19.5 us: over_far(): lax.ppermute(arrays[step], 'blk', far_of(step, blk))]
    all_gather x1 -> x0, blocking collectives: 34.8 us -> none  [on_device(): gathered = lax.all_gather(queries, 'blk', axis=0, tiled=True)]
    ppermute x0 -> x21, starting transfers between devices: none -> 27.8 us  [the longest x12 19.4 us: over_far(): lax.ppermute(arrays[step], 'blk', far_of(step, blk))]
    pmax x1 -> x0, blocking collectives: 21.3 us -> none  [on_device(): global_top = lax.pmax(row_top, 'blk')]
    all_to_all x1 -> x0, blocking collectives: 18 us -> none  [on_device(): lax.all_to_all(outgoing, ('blk', 'rows'), split_axis=0, concat_axis=0, ti...]
    psum x1 -> x0, blocking collectives: 17.1 us -> none  [on_device(): all_totals = lax.psum(totals, 'blk')]
    dot_general x8 -> x0, matrix products: 16.8 us -> none  [the longest x1 4.08 us: run_experts(): jnp.einsum('secf,efd->secd', hidden, down_weight, preferred_element_type=...]
  transfers between devices with their start and end apart: 3 -> 21, of which waited for: 3 -> 14; matrix products, arithmetic and copies ran while one was open for 0% -> 4% of each run, Pallas kernels for 0% -> 4%
where the time goes in v1:
time: 92.8 us; the launch traced here: 92.5 us
  waiting for transfers between devices  36.7 us (40%)
  starting transfers between devices  27.8 us (30%)
  Pallas kernels  16.5 us (18%)
  local copies, waits for them, and re-layouts  5.46 us (6%)
  other arithmetic  5.35 us (6%)
    ppermute x12, waiting for transfers between devices, over_far(): lax.ppermute(arrays[step], 'blk', far_of(step, blk))  19.5 us
    ppermute x12, starting transfers between devices, over_far(): lax.ppermute(arrays[step], 'blk', far_of(step, blk))  19.4 us
    ppermute x5, waiting for transfers between devices, over_near(): return lax.ppermute(array, 'blk', side_of(blk))  12.7 us
    ppermute x5, starting transfers between devices, over_near(): return lax.ppermute(array, 'blk', side_of(blk))  8.22 us
    pallas_call x1, Pallas kernels, paired_device(): pl.pallas_call(functools.partial(expert_kernel, width), out_shape=[shape_...  6.74 us
    ppermute x4, waiting for transfers between devices, over_rows(): return lax.ppermute(array, 'rows', side_of(row_count))  4.5 us
    pallas_call x1, Pallas kernels, paired_device(): pl.pallas_call(functools.partial(attend_kernel, (far_count, span_length,...  3.5 us
    unnamed x34, local copies, waits for them, and re-layouts  3.45 us
  transfers between devices with their start and end apart: 21, of which 14 were waited for; matrix products, arithmetic and copies ran while one was open for 4% of the time, Pallas kernels for 4%

profile of v1, /device:TPU:0, one launch (start us, length us, event | category | flops | bytes accessed | tf_op | source)
XLA Modules:
  0.0 92.5 jit_solution(3560940252696353691)
XLA Ops:
  0.6 3.1 %collective-permute-start.8 = (bf16[128,2048]{1,0:T(8,128)(2,1)}, bf16[128,2048]{1,0:T(8,128)(2,1)S(1)}, u32[]{:S(2)}, u32[]{:S(2)}) collective-permute-start(bf16[128,2048]{1,0:T(8,128)(2,1)} %refs_4_.4), channel_id=1, source_target_pairs={{0,2},{2,0},{4,6},{6,4},{8,10},{10,8},{12,14},{14,12},{1,3},{3,1},... | collective-permute-start | bytes 1572872 | tf_op jit(solution)/shard_map/ppermute | solution.py:389
  3.7 1.6 %collective-permute-start = (bf16[16,1024]{1,0:T(8,128)(2,1)}, bf16[16,1024]{1,0:T(8,128)(2,1)S(1)}, u32[]{:S(2)}, u32[]{:S(2)}) collective-permute-start(bf16[16,1024]{1,0:T(8,128)(2,1)} %refs_0_.1), channel_id=1, source_target_pairs={{0,4},{2,6},{4,0},{6,2},{8,12},{10,14},{12,8},{14,10},{1,5},{3,7},... | collective-permute-start | bytes 98312 | tf_op jit(solution)/shard_map/ppermute | solution.py:385
  5.3 0.5 collective-permute-start.3
  5.8 1.5 %collective-permute-start.4 = (bf16[512,128]{1,0:T(8,128)(2,1)}, bf16[512,128]{1,0:T(8,128)(2,1)S(1)}, u32[]{:S(2)}, u32[]{:S(2)}) collective-permute-start(bf16[512,128]{1,0:T(8,128)(2,1)} %refs_6_.2), channel_id=1, source_target_pairs={{0,2},{2,0},{4,6},{6,4},{8,10},{10,8},{12,14},{14,12},{1,3},{3,1},... | collective-permute-start | bytes 393224 | tf_op jit(solution)/shard_map/ppermute | solution.py:389
  7.3 2.6 %collective-permute-start.1 = (bf16[16,1024]{1,0:T(8,128)(2,1)}, bf16[16,1024]{1,0:T(8,128)(2,1)S(1)}, u32[]{:S(2)}, u32[]{:S(2)}) collective-permute-start(bf16[16,1024]{1,0:T(8,128)(2,1)} %refs_0_.1), channel_id=1, source_target_pairs={{0,8},{2,10},{4,12},{6,14},{8,0},{10,2},{12,4},{14,6},{1,9},{3,11}... | collective-permute-start | bytes 98312 | tf_op jit(solution)/shard_map/ppermute | solution.py:385
  9.9 1.5 %collective-permute-start.2 = (bf16[16,1024]{1,0:T(8,128)(2,1)}, bf16[16,1024]{1,0:T(8,128)(2,1)S(1)}, u32[]{:S(2)}, u32[]{:S(2)}) collective-permute-start(bf16[16,1024]{1,0:T(8,128)(2,1)} %refs_0_.1), channel_id=1, source_target_pairs={{0,12},{2,14},{4,8},{6,10},{8,4},{10,6},{12,0},{14,2},{1,13},{3,15... | collective-permute-start | bytes 98312 | tf_op jit(solution)/shard_map/ppermute | solution.py:385
  11.4 1.3 %pad_add_fusion.1.meta = s32[4]{0:T(128)} fusion(s32[2]{0:T(128)} %param.14, s32[1]{0:T(128)} %bitcast.1, s32[1]{0:T(128)} %bitcast.meta), kind=kLoop, calls=%fused_computation.5 | loop fusion | flops 8 | bytes 32 | tf_op jit(solution)/shard_map/concatenate | solution.py:397
  12.7 3.1 %collective-permute-done.2.refs_3_ = bf16[16,1024]{1,0:T(8,128)(2,1)S(1)} collective-permute-done((bf16[16,1024]{1,0:T(8,128)(2,1)}, bf16[16,1024]{1,0:T(8,128)(2,1)S(1)}, u32[]{:S(2)}, u32[]{:S(2)}) %collective-permute-start.2) | collective-permute-done | bytes 32800 | tf_op jit(solution)/shard_map/ppermute | solution.py:385
  15.8 3.7 %collective-permute-done.3.refs_5_ = bf16[512,128]{1,0:T(8,128)(2,1)S(1)} collective-permute-done((bf16[512,128]{1,0:T(8,128)(2,1)}, bf16[512,128]{1,0:T(8,128)(2,1)S(1)}, u32[]{:S(2)}, u32[]{:S(2)}) %collective-permute-start.3) | collective-permute-done | bytes 131104 | tf_op jit(solution)/shard_map/ppermute | solution.py:389
  19.5 2.0 %collective-permute-done.4.refs_7_ = bf16[512,128]{1,0:T(8,128)(2,1)S(1)} collective-permute-done((bf16[512,128]{1,0:T(8,128)(2,1)}, bf16[512,128]{1,0:T(8,128)(2,1)S(1)}, u32[]{:S(2)}, u32[]{:S(2)}) %collective-permute-start.4) | collective-permute-done | bytes 131104 | tf_op jit(solution)/shard_map/ppermute | solution.py:389
  21.5 0.6 copy-done.10
  22.1 3.5 %attend.1 = (bf16[64,384]{1,0:T(8,128)(2,1)}, bf16[64,384]{1,0:T(8,128)(2,1)}, bf16[64,384]{1,0:T(8,128)(2,1)}, bf16[64,384]{1,0:T(8,128)(2,1)}) custom-call(s32[4]{0:T(128)} %pad_add_fusion.1.meta, bf16[16,1024]{1,0:T(8,128)(2,1)} %refs_0_.1, bf16[16,1024]{1,0:T(8,128)(2,1)} %copy-done.14, bf16[16,1024]{1,0:T(8,128)(2,1)} %copy-done.15, ...), custom_call_target="tpu_custom_call" | custom-call | tf_op jit(solution)/shard_map/attend/pallas_call | solution.py:399
  25.6 1.8 %collective-permute-start.5 = (bf16[64,384]{1,0:T(8,128)(2,1)}, bf16[64,384]{1,0:T(8,128)(2,1)S(1)}, u32[]{:S(2)}, u32[]{:S(2)}) collective-permute-start(bf16[64,384]{1,0:T(8,128)(2,1)} %get-tuple-element.18), channel_id=1, source_target_pairs={{0,4},{2,6},{4,0},{6,2},{8,12},{10,14},{12,8},{14,10},{1,5},{3,7},... | collective-permute-start | bytes 147464 | tf_op jit(solution)/shard_map/ppermute | solution.py:385
  27.4 2.6 %collective-permute-start.6 = (bf16[64,384]{1,0:T(8,128)(2,1)}, bf16[64,384]{1,0:T(8,128)(2,1)S(1)}, u32[]{:S(2)}, u32[]{:S(2)}) collective-permute-start(bf16[64,384]{1,0:T(8,128)(2,1)} %get-tuple-element.19), channel_id=1, source_target_pairs={{0,8},{2,10},{4,12},{6,14},{8,0},{10,2},{12,4},{14,6},{1,9},{3,11}... | collective-permute-start | bytes 147464 | tf_op jit(solution)/shard_map/ppermute | solution.py:385
  30.0 0.6 pad_add_fusion.meta
  30.6 3.1 %collective-permute-done.6.refs_2_ = bf16[64,384]{1,0:T(8,128)(2,1)S(1)} collective-permute-done((bf16[64,384]{1,0:T(8,128)(2,1)}, bf16[64,384]{1,0:T(8,128)(2,1)S(1)}, u32[]{:S(2)}, u32[]{:S(2)}) %collective-permute-start.6) | collective-permute-done | bytes 49184 | tf_op jit(solution)/shard_map/ppermute | solution.py:385
  33.7 2.4 %collective-permute-done.7.refs_3_ = bf16[64,384]{1,0:T(8,128)(2,1)S(1)} collective-permute-done((bf16[64,384]{1,0:T(8,128)(2,1)}, bf16[64,384]{1,0:T(8,128)(2,1)S(1)}, u32[]{:S(2)}, u32[]{:S(2)}) %collective-permute-start.7) | collective-permute-done | bytes 49184 | tf_op jit(solution)/shard_map/ppermute | solution.py:385
  36.1 0.6 copy-done.13
  36.7 0.2 copy-done
  36.9 2.6 %project.1 = (f32[32,2048]{1,0:T(8,128)}, bf16[32,2048]{1,0:T(8,128)(2,1)}, f32[32,128]{1,0:T(8,128)}) custom-call(s32[3]{0:T(128)} %pad_add_fusion.meta, bf16[64,384]{1,0:T(8,128)(2,1)} %get-tuple-element.17.refs_0_, bf16[64,384]{1,0:T(8,128)(2,1)} %copy-done.11, bf16[64,384]{1,0:T(8,128)(2,1)} %copy-done.12, bf16[64,384]{1,0:T(8,128)(2,1)} %copy-done.13, ...), custom_call_target="tpu_custom_call" | custom-call | tf_op jit(solution)/shard_map/project/pallas_call | solution.py:415
  39.5 1.6 %collective-permute-done.9 = bf16[32,2048]{1,0:T(8,128)(2,1)S(1)} collective-permute-done((bf16[32,2048]{1,0:T(8,128)(2,1)}, bf16[32,2048]{1,0:T(8,128)(2,1)S(1)}, u32[]{:S(2)}, u32[]{:S(2)}) %collective-permute-start.9) | collective-permute-done | bytes 131104 | tf_op jit(solution)/shard_map/ppermute | solution.py:392
  41.1 1.0 %add_convert_fusion.refs_0_ = bf16[32,2048]{1,0:T(8,128)(2,1)S(1)} fusion(f32[32,2048]{1,0:T(8,128)} %get-tuple-element.21, bf16[32,2048]{1,0:T(8,128)(2,1)S(1)} %collective-permute-done.9), kind=kLoop, calls=%fused_computation.2 | loop fusion | flops 196608 | bytes 524288 | tf_op jit(solution)/shard_map/convert_element_type | solution.py:423
  42.1 0.1 collective-permute-start.10
  42.2 1.1 %collective-permute-start.11 = (bf16[32,2048]{1,0:T(8,128)(2,1)S(1)}, bf16[32,2048]{1,0:T(8,128)(2,1)S(1)}, u32[]{:S(2)}, u32[]{:S(2)}) collective-permute-start(bf16[32,2048]{1,0:T(8,128)(2,1)S(1)} %add_convert_fusion.refs_0_), channel_id=1, source_target_pairs={{0,8},{2,10},{4,12},{6,14},{8,0},{10,2},{12,4},{14,6},{1,9},{3,11}... | collective-permute-start | bytes 393224 | tf_op jit(solution)/shard_map/ppermute | solution.py:385
  43.3 3.2 %collective-permute-start.12 = (bf16[32,2048]{1,0:T(8,128)(2,1)S(1)}, bf16[32,2048]{1,0:T(8,128)(2,1)S(1)}, u32[]{:S(2)}, u32[]{:S(2)}) collective-permute-start(bf16[32,2048]{1,0:T(8,128)(2,1)S(1)} %add_convert_fusion.refs_0_), channel_id=1, source_target_pairs={{0,12},{2,14},{4,8},{6,10},{8,4},{10,6},{12,0},{14,2},{1,13},{3,15... | collective-permute-start | bytes 393224 | tf_op jit(solution)/shard_map/ppermute | solution.py:385
  46.6 1.3 %reshape.7.refs_4_ = bf16[1,2048]{1,0:T(2,128)(2,1)} reshape(bf16[2048]{0:T(1024)(128)(2,1)} %param.16) | data formatting | bytes 8192 | tf_op jit(solution)/shard_map/reshape | solution.py:433
  47.8 1.1 %collective-permute-done.10.refs_1_ = bf16[32,2048]{1,0:T(8,128)(2,1)S(1)} collective-permute-done((bf16[32,2048]{1,0:T(8,128)(2,1)S(1)}, bf16[32,2048]{1,0:T(8,128)(2,1)S(1)}, u32[]{:S(2)}, u32[]{:S(2)}) %collective-permute-start.10) | collective-permute-done | bytes 131104 | tf_op jit(solution)/shard_map/ppermute | solution.py:385
  48.9 6.3 %collective-permute-done.11.refs_2_ = bf16[32,2048]{1,0:T(8,128)(2,1)S(1)} collective-permute-done((bf16[32,2048]{1,0:T(8,128)(2,1)S(1)}, bf16[32,2048]{1,0:T(8,128)(2,1)S(1)}, u32[]{:S(2)}, u32[]{:S(2)}) %collective-permute-start.11) | collective-permute-done | bytes 131104 | tf_op jit(solution)/shard_map/ppermute | solution.py:385
  55.2 0.6 copy-done.6
  55.9 1.9 %norm.1 = (bf16[8,2048]{1,0:T(8,128)(2,1)}, bf16[32,2176]{1,0:T(8,128)(2,1)}) custom-call(s32[1]{0:T(128)} %bitcast.meta, bf16[32,2048]{1,0:T(8,128)(2,1)} %copy-done.1, bf16[32,2048]{1,0:T(8,128)(2,1)} %copy-done.5, bf16[32,2048]{1,0:T(8,128)(2,1)} %copy-done.6, bf16[32,2048]{1,0:T(8,128)(2,1)} %copy-done.7, bf16[1,2048]{1,0:T(2,128)(2,1)} %reshape.7.refs_4_, ...), custom_call_target="tpu_custom_call" | custom-call | tf_op jit(solution)/shard_map/norm/pallas_call | solution.py:426
  57.8 1.5 %collective-permute-start.13 = (bf16[32,2176]{1,0:T(8,128)(2,1)}, bf16[32,2176]{1,0:T(8,128)(2,1)S(1)}, u32[]{:S(2)}, u32[]{:S(2)}) collective-permute-start(bf16[32,2176]{1,0:T(8,128)(2,1)} %get-tuple-element.25.refs_0_), channel_id=1, source_target_pairs={{0,2},{2,0},{4,6},{6,4},{8,10},{10,8},{12,14},{14,12},{1,3},{3,1},... | collective-permute-start | bytes 417800 | tf_op jit(solution)/shard_map/ppermute | solution.py:389
  59.3 3.7 %collective-permute-done.13.refs_1_ = bf16[32,2176]{1,0:T(8,128)(2,1)S(1)} collective-permute-done((bf16[32,2176]{1,0:T(8,128)(2,1)}, bf16[32,2176]{1,0:T(8,128)(2,1)S(1)}, u32[]{:S(2)}, u32[]{:S(2)}) %collective-permute-start.13) | collective-permute-done | bytes 139296 | tf_op jit(solution)/shard_map/ppermute | solution.py:389
  63.1 1.3 %collective-permute-done.15.refs_3_ = bf16[32,2176]{1,0:T(8,128)(2,1)S(1)} collective-permute-done((bf16[32,2176]{1,0:T(8,128)(2,1)S(1)}, bf16[32,2176]{1,0:T(8,128)(2,1)S(1)}, u32[]{:S(2)}, u32[]{:S(2)}) %collective-permute-start.15) | collective-permute-done | bytes 139296 | tf_op jit(solution)/shard_map/ppermute | solution.py:392
  64.4 0.7 copy-done.4
  65.1 6.7 %experts.1 = (bf16[64,2048]{1,0:T(8,128)(2,1)}, bf16[64,2048]{1,0:T(8,128)(2,1)}) custom-call(s32[1]{0:T(128)} %bitcast.3.meta, bf16[32,2176]{1,0:T(8,128)(2,1)} %get-tuple-element.25.refs_0_, bf16[32,2176]{1,0:T(8,128)(2,1)} %copy-done.2, bf16[32,2176]{1,0:T(8,128)(2,1)} %copy-done.3, bf16[32,2176]{1,0:T(8,128)(2,1)} %copy-done.4, ...), custom_call_target="tpu_custom_call" | custom-call | tf_op jit(solution)/shard_map/experts/pallas_call | solution.py:439
  71.8 0.1 collective-permute-start.16
  72.0 1.6 %collective-permute-done.16 = bf16[64,2048]{1,0:T(8,128)(2,1)S(1)} collective-permute-done((bf16[64,2048]{1,0:T(8,128)(2,1)}, bf16[64,2048]{1,0:T(8,128)(2,1)S(1)}, u32[]{:S(2)}, u32[]{:S(2)}) %collective-permute-start.16) | collective-permute-done | bytes 262176 | tf_op jit(solution)/shard_map/ppermute | solution.py:392
  73.6 1.0 %convert_add_fusion = f32[64,2048]{1,0:T(8,128)S(1)} fusion(bf16[64,2048]{1,0:T(8,128)(2,1)S(1)} %collective-permute-done.16, bf16[64,2048]{1,0:T(8,128)(2,1)} %get-tuple-element.26), kind=kLoop, calls=%fused_computation | loop fusion | flops 393216 | bytes 1048576 | tf_op jit(solution)/shard_map/add | solution.py:454
  74.6 1.6 %collective-permute-start.17 = (bf16[32,2048]{1,0:T(8,128)(2,1)S(1)}, bf16[32,2048]{1,0:T(8,128)(2,1)S(1)}, u32[]{:S(2)}, u32[]{:S(2)}) collective-permute-start(bf16[32,2048]{1,0:T(8,128)(2,1)S(1)} %slice.12), channel_id=1, source_target_pairs={{0,2},{2,0},{4,6},{6,4},{8,10},{10,8},{12,14},{14,12},{1,3},{3,1},... | collective-permute-start | bytes 393224 | tf_op jit(solution)/shard_map/ppermute | solution.py:389
  76.2 0.7 slice.9.refs_0_
  76.9 3.3 %collective-permute-done.17.refs_1_ = bf16[32,2048]{1,0:T(8,128)(2,1)S(1)} collective-permute-done((bf16[32,2048]{1,0:T(8,128)(2,1)S(1)}, bf16[32,2048]{1,0:T(8,128)(2,1)S(1)}, u32[]{:S(2)}, u32[]{:S(2)}) %collective-permute-start.17) | collective-permute-done | bytes 131104 | tf_op jit(solution)/shard_map/ppermute | solution.py:389
  80.2 0.7 copy-done.8
  80.9 1.7 %shares.1 = (f32[8,2048]{1,0:T(8,128)}, bf16[8,2048]{1,0:T(8,128)(2,1)}, bf16[8,2048]{1,0:T(8,128)(2,1)}, bf16[8,2048]{1,0:T(8,128)(2,1)}) custom-call(s32[1]{0:T(128)} %bitcast.meta, f32[32,2048]{1,0:T(8,128)} %slice.9.refs_0_, bf16[32,2048]{1,0:T(8,128)(2,1)} %copy-done.8), custom_call_target="tpu_custom_call" | custom-call | tf_op jit(solution)/shard_map/shares/pallas_call | solution.py:458
  82.6 2.5 %collective-permute-start.18 = (bf16[8,2048]{1,0:T(8,128)(2,1)}, bf16[8,2048]{1,0:T(8,128)(2,1)S(1)}, u32[]{:S(2)}, u32[]{:S(2)}) collective-permute-start(bf16[8,2048]{1,0:T(8,128)(2,1)} %get-tuple-element.29), channel_id=1, source_target_pairs={{0,4},{2,6},{4,0},{6,2},{8,12},{10,14},{12,8},{14,10},{1,5},{3,7},... | collective-permute-start | bytes 98312 | tf_op jit(solution)/shard_map/ppermute | solution.py:385
  85.1 2.4 %collective-permute-start.20 = (bf16[8,2048]{1,0:T(8,128)(2,1)}, bf16[8,2048]{1,0:T(8,128)(2,1)S(1)}, u32[]{:S(2)}, u32[]{:S(2)}) collective-permute-start(bf16[8,2048]{1,0:T(8,128)(2,1)} %get-tuple-element.31), channel_id=1, source_target_pairs={{0,12},{2,14},{4,8},{6,10},{8,4},{10,6},{12,0},{14,2},{1,13},{3,15... | collective-permute-start | bytes 98312 | tf_op jit(solution)/shard_map/ppermute | solution.py:385
  87.4 2.7 %collective-permute-done.19 = bf16[8,2048]{1,0:T(8,128)(2,1)S(1)} collective-permute-done((bf16[8,2048]{1,0:T(8,128)(2,1)}, bf16[8,2048]{1,0:T(8,128)(2,1)S(1)}, u32[]{:S(2)}, u32[]{:S(2)}) %collective-permute-start.19) | collective-permute-done | bytes 32800 | tf_op jit(solution)/shard_map/ppermute | solution.py:385
  90.1 0.9 collective-permute-done.20
  91.0 1.5 %add_convert_fusion.1 = bf16[8,2048]{1,0:T(8,128)(2,1)} fusion(bf16[8,2048]{1,0:T(8,128)(2,1)S(1)} %collective-permute-done.20, bf16[8,2048]{1,0:T(8,128)(2,1)S(1)} %collective-permute-done.19, f32[8,2048]{1,0:T(8,128)} %get-tuple-element.28, bf16[8,2048]{1,0:T(8,128)(2,1)S(1)} %collective-permute-done.18), kind=kLoop, calls=%fused_computation.3 | loop fusion | flops 114688 | bytes 196608 | tf_op jit(solution)/shard_map/convert_element_type | solution.py:470
  (41 shorter events, 0.1 us)
Async XLA Ops:
  0.6 35.5 %collective-permute-start.8 = (bf16[128,2048]{1,0:T(8,128)(2,1)}, bf16[128,2048]{1,0:T(8,128)(2,1)S(1)}, u32[]{:S(2)}, u32[]{:S(2)}) collective-permute-start(bf16[128,2048]{1,0:T(8,128)(2,1)} %refs_4_.4), channel_id=1, source_target_pairs={{0,2},{2,0},{4,6},{6,4},{8,10},{10,8},{12,14},{14,12},{1,3},{3,1},... | collective-permute-start | bytes 1572872 | tf_op jit(solution)/shard_map/ppermute | solution.py:389
  3.7 6.2 %collective-permute-start = (bf16[16,1024]{1,0:T(8,128)(2,1)}, bf16[16,1024]{1,0:T(8,128)(2,1)S(1)}, u32[]{:S(2)}, u32[]{:S(2)}) collective-permute-start(bf16[16,1024]{1,0:T(8,128)(2,1)} %refs_0_.1), channel_id=1, source_target_pairs={{0,4},{2,6},{4,0},{6,2},{8,12},{10,14},{12,8},{14,10},{1,5},{3,7},... | collective-permute-start | bytes 98312 | tf_op jit(solution)/shard_map/ppermute | solution.py:385
  5.3 14.2 %collective-permute-start.3 = (bf16[512,128]{1,0:T(8,128)(2,1)}, bf16[512,128]{1,0:T(8,128)(2,1)S(1)}, u32[]{:S(2)}, u32[]{:S(2)}) collective-permute-start(bf16[512,128]{1,0:T(8,128)(2,1)} %refs_4_.3), channel_id=1, source_target_pairs={{0,2},{2,0},{4,6},{6,4},{8,10},{10,8},{12,14},{14,12},{1,3},{3,1},... | collective-permute-start | bytes 393224 | tf_op jit(solution)/shard_map/ppermute | solution.py:389
  5.8 15.7 %collective-permute-start.4 = (bf16[512,128]{1,0:T(8,128)(2,1)}, bf16[512,128]{1,0:T(8,128)(2,1)S(1)}, u32[]{:S(2)}, u32[]{:S(2)}) collective-permute-start(bf16[512,128]{1,0:T(8,128)(2,1)} %refs_6_.2), channel_id=1, source_target_pairs={{0,2},{2,0},{4,6},{6,4},{8,10},{10,8},{12,14},{14,12},{1,3},{3,1},... | collective-permute-start | bytes 393224 | tf_op jit(solution)/shard_map/ppermute | solution.py:389
  7.3 5.4 %collective-permute-start.1 = (bf16[16,1024]{1,0:T(8,128)(2,1)}, bf16[16,1024]{1,0:T(8,128)(2,1)S(1)}, u32[]{:S(2)}, u32[]{:S(2)}) collective-permute-start(bf16[16,1024]{1,0:T(8,128)(2,1)} %refs_0_.1), channel_id=1, source_target_pairs={{0,8},{2,10},{4,12},{6,14},{8,0},{10,2},{12,4},{14,6},{1,9},{3,11}... | collective-permute-start | bytes 98312 | tf_op jit(solution)/shard_map/ppermute | solution.py:385
  9.9 11.6 %copy-start.14 = (bf16[16,1024]{1,0:T(8,128)(2,1)}, bf16[16,1024]{1,0:T(8,128)(2,1)S(1)}, u32[]{:S(2)}) copy-start(bf16[16,1024]{1,0:T(8,128)(2,1)S(1)} %collective-permute-done.refs_1_) | copy-start | bytes 98308
  9.9 5.9 %collective-permute-start.2 = (bf16[16,1024]{1,0:T(8,128)(2,1)}, bf16[16,1024]{1,0:T(8,128)(2,1)S(1)}, u32[]{:S(2)}, u32[]{:S(2)}) collective-permute-start(bf16[16,1024]{1,0:T(8,128)(2,1)} %refs_0_.1), channel_id=1, source_target_pairs={{0,12},{2,14},{4,8},{6,10},{8,4},{10,6},{12,0},{14,2},{1,13},{3,15... | collective-permute-start | bytes 98312 | tf_op jit(solution)/shard_map/ppermute | solution.py:385
  12.7 8.7 %copy-start.15 = (bf16[16,1024]{1,0:T(8,128)(2,1)}, bf16[16,1024]{1,0:T(8,128)(2,1)S(1)}, u32[]{:S(2)}) copy-start(bf16[16,1024]{1,0:T(8,128)(2,1)S(1)} %collective-permute-done.1.refs_2_) | copy-start | bytes 98308
  15.8 5.6 %copy-start.16 = (bf16[16,1024]{1,0:T(8,128)(2,1)}, bf16[16,1024]{1,0:T(8,128)(2,1)S(1)}, u32[]{:S(2)}) copy-start(bf16[16,1024]{1,0:T(8,128)(2,1)S(1)} %collective-permute-done.2.refs_3_) | copy-start | bytes 98308
  19.5 2.0 %copy-start.9 = (bf16[512,128]{1,0:T(8,128)(2,1)}, bf16[512,128]{1,0:T(8,128)(2,1)S(1)}, u32[]{:S(2)}) copy-start(bf16[512,128]{1,0:T(8,128)(2,1)S(1)} %collective-permute-done.3.refs_5_) | copy-start | bytes 393220
  21.5 0.6 copy-start.10
  25.6 5.0 %collective-permute-start.5 = (bf16[64,384]{1,0:T(8,128)(2,1)}, bf16[64,384]{1,0:T(8,128)(2,1)S(1)}, u32[]{:S(2)}, u32[]{:S(2)}) collective-permute-start(bf16[64,384]{1,0:T(8,128)(2,1)} %get-tuple-element.18), channel_id=1, source_target_pairs={{0,4},{2,6},{4,0},{6,2},{8,12},{10,14},{12,8},{14,10},{1,5},{3,7},... | collective-permute-start | bytes 147464 | tf_op jit(solution)/shard_map/ppermute | solution.py:385
  27.4 6.3 %collective-permute-start.6 = (bf16[64,384]{1,0:T(8,128)(2,1)}, bf16[64,384]{1,0:T(8,128)(2,1)S(1)}, u32[]{:S(2)}, u32[]{:S(2)}) collective-permute-start(bf16[64,384]{1,0:T(8,128)(2,1)} %get-tuple-element.19), channel_id=1, source_target_pairs={{0,8},{2,10},{4,12},{6,14},{8,0},{10,2},{12,4},{14,6},{1,9},{3,11}... | collective-permute-start | bytes 147464 | tf_op jit(solution)/shard_map/ppermute | solution.py:385
  30.0 6.1 %collective-permute-start.7 = (bf16[64,384]{1,0:T(8,128)(2,1)}, bf16[64,384]{1,0:T(8,128)(2,1)S(1)}, u32[]{:S(2)}, u32[]{:S(2)}) collective-permute-start(bf16[64,384]{1,0:T(8,128)(2,1)} %get-tuple-element.20), channel_id=1, source_target_pairs={{0,12},{2,14},{4,8},{6,10},{8,4},{10,6},{12,0},{14,2},{1,13},{3,15... | collective-permute-start | bytes 147464 | tf_op jit(solution)/shard_map/ppermute | solution.py:385
  30.6 5.5 %copy-start.11 = (bf16[64,384]{1,0:T(8,128)(2,1)}, bf16[64,384]{1,0:T(8,128)(2,1)S(1)}, u32[]{:S(2)}) copy-start(bf16[64,384]{1,0:T(8,128)(2,1)S(1)} %collective-permute-done.5.refs_1_) | copy-start | bytes 147460
  33.7 2.5 %copy-start.12 = (bf16[64,384]{1,0:T(8,128)(2,1)}, bf16[64,384]{1,0:T(8,128)(2,1)S(1)}, u32[]{:S(2)}) copy-start(bf16[64,384]{1,0:T(8,128)(2,1)S(1)} %collective-permute-done.6.refs_2_) | copy-start | bytes 147460
  36.1 0.6 copy-start.13
  36.1 0.8 copy-start
  39.5 1.6 %collective-permute-start.9 = (bf16[32,2048]{1,0:T(8,128)(2,1)}, bf16[32,2048]{1,0:T(8,128)(2,1)S(1)}, u32[]{:S(2)}, u32[]{:S(2)}) collective-permute-start(bf16[32,2048]{1,0:T(8,128)(2,1)} %get-tuple-element.22), channel_id=1, source_target_pairs={{0,1},{1,0},{2,3},{3,2},{4,5},{5,4},{6,7},{7,6},{8,9},{9,8},{10,11... | collective-permute-start | bytes 393224 | tf_op jit(solution)/shard_map/ppermute | solution.py:392
  42.1 13.1 %copy-start.1 = (bf16[32,2048]{1,0:T(8,128)(2,1)}, bf16[32,2048]{1,0:T(8,128)(2,1)S(1)}, u32[]{:S(2)}) copy-start(bf16[32,2048]{1,0:T(8,128)(2,1)S(1)} %add_convert_fusion.refs_0_) | copy-start | bytes 393220
  42.1 6.8 %collective-permute-start.10 = (bf16[32,2048]{1,0:T(8,128)(2,1)S(1)}, bf16[32,2048]{1,0:T(8,128)(2,1)S(1)}, u32[]{:S(2)}, u32[]{:S(2)}) collective-permute-start(bf16[32,2048]{1,0:T(8,128)(2,1)S(1)} %add_convert_fusion.refs_0_), channel_id=1, source_target_pairs={{0,4},{2,6},{4,0},{6,2},{8,12},{10,14},{12,8},{14,10},{1,5},{3,7},... | collective-permute-start | bytes 393224 | tf_op jit(solution)/shard_map/ppermute | solution.py:385
  42.2 13.0 %collective-permute-start.11 = (bf16[32,2048]{1,0:T(8,128)(2,1)S(1)}, bf16[32,2048]{1,0:T(8,128)(2,1)S(1)}, u32[]{:S(2)}, u32[]{:S(2)}) collective-permute-start(bf16[32,2048]{1,0:T(8,128)(2,1)S(1)} %add_convert_fusion.refs_0_), channel_id=1, source_target_pairs={{0,8},{2,10},{4,12},{6,14},{8,0},{10,2},{12,4},{14,6},{1,9},{3,11}... | collective-permute-start | bytes 393224 | tf_op jit(solution)/shard_map/ppermute | solution.py:385
  43.3 11.9 %collective-permute-start.12 = (bf16[32,2048]{1,0:T(8,128)(2,1)S(1)}, bf16[32,2048]{1,0:T(8,128)(2,1)S(1)}, u32[]{:S(2)}, u32[]{:S(2)}) collective-permute-start(bf16[32,2048]{1,0:T(8,128)(2,1)S(1)} %add_convert_fusion.refs_0_), channel_id=1, source_target_pairs={{0,12},{2,14},{4,8},{6,10},{8,4},{10,6},{12,0},{14,2},{1,13},{3,15... | collective-permute-start | bytes 393224 | tf_op jit(solution)/shard_map/ppermute | solution.py:385
  48.9 6.3 %copy-start.5 = (bf16[32,2048]{1,0:T(8,128)(2,1)}, bf16[32,2048]{1,0:T(8,128)(2,1)S(1)}, u32[]{:S(2)}) copy-start(bf16[32,2048]{1,0:T(8,128)(2,1)S(1)} %collective-permute-done.10.refs_1_) | copy-start | bytes 393220
  55.2 0.7 copy-start.6
  55.2 0.7 copy-start.7
  57.8 5.3 %collective-permute-start.13 = (bf16[32,2176]{1,0:T(8,128)(2,1)}, bf16[32,2176]{1,0:T(8,128)(2,1)S(1)}, u32[]{:S(2)}, u32[]{:S(2)}) collective-permute-start(bf16[32,2176]{1,0:T(8,128)(2,1)} %get-tuple-element.25.refs_0_), channel_id=1, source_target_pairs={{0,2},{2,0},{4,6},{6,4},{8,10},{10,8},{12,14},{14,12},{1,3},{3,1},... | collective-permute-start | bytes 417800 | tf_op jit(solution)/shard_map/ppermute | solution.py:389
  59.3 3.7 %collective-permute-start.14 = (bf16[32,2176]{1,0:T(8,128)(2,1)}, bf16[32,2176]{1,0:T(8,128)(2,1)S(1)}, u32[]{:S(2)}, u32[]{:S(2)}) collective-permute-start(bf16[32,2176]{1,0:T(8,128)(2,1)} %get-tuple-element.25.refs_0_), channel_id=1, source_target_pairs={{0,1},{1,0},{2,3},{3,2},{4,5},{5,4},{6,7},{7,6},{8,9},{9,8},{10,11... | collective-permute-start | bytes 417800 | tf_op jit(solution)/shard_map/ppermute | solution.py:392
  63.1 1.4 %copy-start.2 = (bf16[32,2176]{1,0:T(8,128)(2,1)}, bf16[32,2176]{1,0:T(8,128)(2,1)S(1)}, u32[]{:S(2)}) copy-start(bf16[32,2176]{1,0:T(8,128)(2,1)S(1)} %collective-permute-done.13.refs_1_) | copy-start | bytes 417796
  63.1 1.4 %collective-permute-start.15 = (bf16[32,2176]{1,0:T(8,128)(2,1)S(1)}, bf16[32,2176]{1,0:T(8,128)(2,1)S(1)}, u32[]{:S(2)}, u32[]{:S(2)}) collective-permute-start(bf16[32,2176]{1,0:T(8,128)(2,1)S(1)} %collective-permute-done.13.refs_1_), channel_id=1, source_target_pairs={{0,1},{1,0},{2,3},{3,2},{4,5},{5,4},{6,7},{7,6},{8,9},{9,8},{10,11... | collective-permute-start | bytes 417800 | tf_op jit(solution)/shard_map/ppermute | solution.py:392
  63.1 1.4 %copy-start.3 = (bf16[32,2176]{1,0:T(8,128)(2,1)}, bf16[32,2176]{1,0:T(8,128)(2,1)S(1)}, u32[]{:S(2)}) copy-start(bf16[32,2176]{1,0:T(8,128)(2,1)S(1)} %collective-permute-done.14.refs_2_) | copy-start | bytes 417796
  64.4 0.7 copy-start.4
  71.8 1.7 %collective-permute-start.16 = (bf16[64,2048]{1,0:T(8,128)(2,1)}, bf16[64,2048]{1,0:T(8,128)(2,1)S(1)}, u32[]{:S(2)}, u32[]{:S(2)}) collective-permute-start(bf16[64,2048]{1,0:T(8,128)(2,1)} %get-tuple-element.27), channel_id=1, source_target_pairs={{0,1},{1,0},{2,3},{3,2},{4,5},{5,4},{6,7},{7,6},{8,9},{9,8},{10,11... | collective-permute-start | bytes 786440 | tf_op jit(solution)/shard_map/ppermute | solution.py:392
  74.6 5.6 %collective-permute-start.17 = (bf16[32,2048]{1,0:T(8,128)(2,1)S(1)}, bf16[32,2048]{1,0:T(8,128)(2,1)S(1)}, u32[]{:S(2)}, u32[]{:S(2)}) collective-permute-start(bf16[32,2048]{1,0:T(8,128)(2,1)S(1)} %slice.12), channel_id=1, source_target_pairs={{0,2},{2,0},{4,6},{6,4},{8,10},{10,8},{12,14},{14,12},{1,3},{3,1},... | collective-permute-start | bytes 393224 | tf_op jit(solution)/shard_map/ppermute | solution.py:389
  80.2 0.7 copy-start.8
  82.6 4.9 %collective-permute-start.18 = (bf16[8,2048]{1,0:T(8,128)(2,1)}, bf16[8,2048]{1,0:T(8,128)(2,1)S(1)}, u32[]{:S(2)}, u32[]{:S(2)}) collective-permute-start(bf16[8,2048]{1,0:T(8,128)(2,1)} %get-tuple-element.29), channel_id=1, source_target_pairs={{0,4},{2,6},{4,0},{6,2},{8,12},{10,14},{12,8},{14,10},{1,5},{3,7},... | collective-permute-start | bytes 98312 | tf_op jit(solution)/shard_map/ppermute | solution.py:385
  85.1 5.0 %collective-permute-start.19 = (bf16[8,2048]{1,0:T(8,128)(2,1)}, bf16[8,2048]{1,0:T(8,128)(2,1)S(1)}, u32[]{:S(2)}, u32[]{:S(2)}) collective-permute-start(bf16[8,2048]{1,0:T(8,128)(2,1)} %get-tuple-element.30), channel_id=1, source_target_pairs={{0,8},{2,10},{4,12},{6,14},{8,0},{10,2},{12,4},{14,6},{1,9},{3,11}... | collective-permute-start | bytes 98312 | tf_op jit(solution)/shard_map/ppermute | solution.py:385
  85.1 5.9 %collective-permute-start.20 = (bf16[8,2048]{1,0:T(8,128)(2,1)}, bf16[8,2048]{1,0:T(8,128)(2,1)S(1)}, u32[]{:S(2)}, u32[]{:S(2)}) collective-permute-start(bf16[8,2048]{1,0:T(8,128)(2,1)} %get-tuple-element.31), channel_id=1, source_target_pairs={{0,12},{2,14},{4,8},{6,10},{8,4},{10,6},{12,0},{14,2},{1,13},{3,15... | collective-permute-start | bytes 98312 | tf_op jit(solution)/shard_map/ppermute | solution.py:385

commit v2 on v1

--- a/solution.py
+++ b/solution.py
@@ -7,6 +7,7 @@
 from jax.experimental import pallas as pl
 from jax.experimental.pallas import tpu as pltpu
 from jax.sharding import PartitionSpec as P
+
 
 HD = 128
 SPANS = 2
@@ -159,6 +160,7 @@
     expert_out = mixed.astype(jnp.bfloat16)
     return (attn_proj, expert_out)
 
+
 def far_of(step, blk):
     return [(at, ((at // 2) ^ step) * 2 + at % 2) for at in range(blk)]
 
@@ -167,28 +169,74 @@
     return [(at, at ^ 1) for at in range(size)]
 
 
+def place_of():
+    blk_at = lax.axis_index("blk")
+    return blk_at // 2, blk_at % 2
+
+
+def grant(mebibytes):
+    return pltpu.CompilerParams(vmem_limit_bytes=mebibytes << 20)
+
+
 def in_vmem(count):
     return [pl.BlockSpec(memory_space=pltpu.VMEM)] * count
 
 
-def attend_kernel(sizes, meta, *refs):
-    far_count, span_length, cache_rows, heads = sizes
+def prepare_kernel(sizes, *refs):
+    far_count, span_length = sizes
+    sources, (starts_hbm, ids_hbm, gates_hbm) = refs[:7], refs[7:10]
+    targets, (pos_all, routes) = refs[10:17], refs[17:19]
+    starts, ids_ref, gates_ref, sems = refs[19:]
+    copies = [
+        pltpu.make_async_copy(source, target, sems.at[at])
+        for at, (source, target) in enumerate(
+            zip((starts_hbm, ids_hbm, gates_hbm) + sources, (starts, ids_ref, gates_ref) + targets)
+        )
+    ]
+    for copy in copies:
+        copy.start()
+    for copy in copies[:3]:
+        copy.wait()
+    _, near = place_of()
+    tokens = pos_all.shape[0]
+    piece = tokens // far_count
+    for source in range(far_count):
+        first = (source * 2 + near) * piece
+        base = starts[first // span_length] + first % span_length
+        pos_all[source * piece : (source + 1) * piece, :] = base + lax.broadcasted_iota(
+            jnp.int32, (piece, HD), 0
+        )
+    gate_values = gates_ref[...].astype(jnp.float32)
+    ids = ids_ref[...]
+    route_weight = gate_values / jnp.sum(gate_values, axis=1, keepdims=True)
+    own_tokens, top_count = gate_values.shape
+    expert_lane = lax.broadcasted_iota(jnp.int32, (own_tokens, HD), 1) - HD // 2
+    weight_of = jnp.zeros((own_tokens, HD), jnp.float32)
+    for k in range(top_count):
+        weight_of += jnp.where(expert_lane == ids[:, k : k + 1], route_weight[:, k : k + 1], 0.0)
+    high = weight_of.astype(jnp.bfloat16).astype(jnp.float32)
+    routes[...] = jnp.concatenate(
+        [high, weight_of - high, jnp.zeros((tokens - 2 * own_tokens, HD), jnp.float32)], axis=0
+    )
+    for copy in copies[3:]:
+        copy.wait()
+
+
+def attend_kernel(sizes, *refs):
+    far_count, cache_rows, heads = sizes
     q_refs = refs[:far_count]
-    key_own, key_side, value_own, value_side, ids, gates = refs[far_count : far_count + 6]
+    key_own, key_side, value_own, value_side, pos_all, routes_ref = refs[far_count : far_count + 6]
     outs = refs[far_count + 6 : 2 * far_count + 6]
-    q_all, pos_all, keys, values, staged = refs[2 * far_count + 6 :]
-    far, near = meta[0], meta[1]
+    q_all, keys, values, staged = refs[2 * far_count + 6 :]
+    far, near = place_of()
     piece = q_refs[0].shape[0]
     tokens = far_count * piece
     own_heads = heads // far_count
     for step in range(far_count):
         source = far ^ step
-        first = (source * 2 + near) * piece
-        base = meta[2 + first // span_length] + first % span_length
         row = pl.multiple_of(source * piece, piece)
         for head in range(heads):
             q_all[pl.ds(head * tokens + row, piece), :] = q_refs[step][:, head * HD : (head + 1) * HD]
-        pos_all[pl.ds(row, piece), :] = base + lax.broadcasted_iota(jnp.int32, (piece, HD), 0)
     keys[:cache_rows, :] = key_own[...]
     keys[cache_rows:, :] = key_side[...]
     values[:cache_rows, :] = value_own[...]
@@ -198,17 +246,7 @@
     side_first = (far * 2 + 1 - near) * cache_rows - cache_rows
     key_pos = lane_at + jnp.where(lane_at < cache_rows, own_first, side_first)
     visible = key_pos <= pos_all[:, :1]
-    gate_values = gates[...].astype(jnp.float32)
-    route_weight = gate_values / jnp.sum(gate_values, axis=1, keepdims=True)
-    own_tokens, top_count = gates.shape
-    expert_lane = lax.broadcasted_iota(jnp.int32, (own_tokens, HD), 1) - HD // 2
-    weight_of = jnp.zeros((own_tokens, HD), jnp.float32)
-    for k in range(top_count):
-        weight_of += jnp.where(expert_lane == ids[:, k : k + 1], route_weight[:, k : k + 1], 0.0)
-    high = weight_of.astype(jnp.bfloat16).astype(jnp.float32)
-    routes = jnp.concatenate(
-        [high, weight_of - high, jnp.zeros((tokens - 2 * own_tokens, HD), jnp.float32)], axis=0
-    )
+    routes = routes_ref[...]
     lane = lax.broadcasted_iota(jnp.int32, (tokens, HD), 1)
     scale = 1.0 / math.sqrt(HD)
     for group in range(far_count):
@@ -242,11 +280,12 @@
         outs[step][...] = staged[far ^ step]
 
 
-def project_kernel(sizes, meta, *refs):
+def project_kernel(sizes, *refs):
     far_count, own_heads, own_tokens = sizes
     messages = refs[:far_count]
     weight_own, weight_side, keep, send, routes, partial = refs[far_count:]
-    far, near, row_at = meta[0], meta[1], meta[2]
+    far, near = place_of()
+    row_at = lax.axis_index("rows")
     tokens = messages[0].shape[0]
     attended = []
     extras = [m[:, own_heads * HD :].astype(jnp.float32) for m in messages]
@@ -283,7 +322,7 @@
         routes[pl.ds(at, own_tokens), :] = e[:own_tokens] + e[own_tokens : 2 * own_tokens]
 
 
-def norm_kernel(sizes, meta, *refs):
+def norm_kernel(sizes, *refs):
     far_count, own_tokens = sizes
     parts = refs[:far_count]
     gain, routes, own_rows, spread, summed = refs[far_count:]
@@ -293,7 +332,7 @@
         total += part[...].astype(jnp.float32)
     values_f = total.astype(jnp.bfloat16).astype(jnp.float32)
     summed[...] = values_f
-    at = pl.multiple_of(meta[0] * own_tokens, own_tokens)
+    at = pl.multiple_of(place_of()[0] * own_tokens, own_tokens)
     own_rows[...] = summed[pl.ds(at, own_tokens), :].astype(jnp.bfloat16)
     mean_square = jnp.mean(values_f * values_f, axis=1, keepdims=True)
     spread[:, :width] = (
@@ -309,44 +348,68 @@
     ).astype(jnp.bfloat16)
 
 
-def expert_kernel(width, meta, *refs):
+def expert_kernel(width, *refs):
     pieces = refs[:4]
-    gate, up, down, keep, send, gathered, total = refs[4:]
+    gate, up, down, keep, send, gathered, hidden = refs[4:]
     rows = pieces[0].shape[0]
-    step = pl.program_id(0)
-
-    @pl.when(step == 0)
-    def _():
-        for at, piece in enumerate(pieces):
-            gathered[at * rows : (at + 1) * rows, :] = piece[:, :width]
-        total[...] = jnp.zeros_like(total)
-
+    for at, piece in enumerate(pieces):
+        gathered[at * rows : (at + 1) * rows, :] = piece[:, :width]
     arrived = gathered[...]
-    gate_part = jnp.dot(arrived, gate[0], preferred_element_type=jnp.float32)
-    up_part = jnp.dot(arrived, up[0], preferred_element_type=jnp.float32)
-    hidden = (gate_part / (1.0 + jnp.exp(-gate_part)) * up_part).astype(jnp.bfloat16)
-    total[...] += jnp.dot(hidden, down[0], preferred_element_type=jnp.float32)
-
-    @pl.when(step == pl.num_programs(0) - 1)
-    def _():
-        lane = lax.broadcasted_iota(jnp.int32, (rows, HD), 1) % (HD // 2)
-        for at, piece in enumerate(pieces):
-            routes = piece[:, width:].astype(jnp.float32)
-            share = jnp.sum(jnp.where(lane == meta[0], routes, 0.0), axis=1, keepdims=True)
-            result = total[at * rows : (at + 1) * rows, :].astype(jnp.bfloat16).astype(jnp.float32)
+    ff = hidden.shape[1]
+    chunk = math.gcd(ff, 256)
+    for first in range(0, ff, chunk):
+        gate_part = jnp.dot(
+            arrived, gate[0, :, first : first + chunk], preferred_element_type=jnp.float32
+        )
+        up_part = jnp.dot(
+            arrived, up[0, :, first : first + chunk], preferred_element_type=jnp.float32
+        )
+        hidden[:, first : first + chunk] = (
+            gate_part / (1.0 + jnp.exp(-gate_part)) * up_part
+        ).astype(jnp.bfloat16)
+    expert = lax.axis_index("blk") * 2 + lax.axis_index("rows")
+    lane = lax.broadcasted_iota(jnp.int32, (rows, HD), 1) % (HD // 2)
+    shares = []
+    for piece in pieces:
+        routes = piece[:, width:].astype(jnp.float32)
+        shares.append(jnp.sum(jnp.where(lane == expert, routes, 0.0), axis=1, keepdims=True))
+    acted = hidden[...]
+    for first in range(0, width, 512):
+        last = min(first + 512, width)
+        result = jnp.dot(acted, down[0, :, first:last], preferred_element_type=jnp.float32)
+        result = result.astype(jnp.bfloat16).astype(jnp.float32)
+        for at, share in enumerate(shares):
             target = keep if at < 2 else send
             half = at % 2
-            target[half * rows : (half + 1) * rows, :] = (share * result).astype(jnp.bfloat16)
-
-
-def spread_kernel(sizes, meta, *refs):
+            target[half * rows : (half + 1) * rows, first:last] = (
+                share * result[at * rows : (at + 1) * rows]
+            ).astype(jnp.bfloat16)
+
+
+def add_kernel(*refs):
+    terms, out = refs[:-1], refs[-1]
+    total = terms[0][...].astype(jnp.float32)
+    for term in terms[1:]:
+        total += term[...].astype(jnp.float32)
+    out[...] = total.astype(out.dtype)
+
+
+def halves_kernel(keep, received, ours, theirs):
+    held = ours.shape[0]
+    ours[...] = keep[:held, :].astype(jnp.float32) + received[:held, :].astype(jnp.float32)
+    theirs[...] = (
+        keep[held:, :].astype(jnp.float32) + received[held:, :].astype(jnp.float32)
+    ).astype(jnp.bfloat16)
+
+
+def spread_kernel(sizes, *refs):
     far_count, own_tokens = sizes
     ours, theirs = refs[:2]
     outs = refs[2 : 2 + far_count]
     summed = refs[2 + far_count]
     summed[...] = ours[...].astype(jnp.float32) + theirs[...].astype(jnp.float32)
     for step in range(far_count):
-        at = pl.multiple_of((meta[0] ^ step) * own_tokens, own_tokens)
+        at = pl.multiple_of((place_of()[0] ^ step) * own_tokens, own_tokens)
         outs[step][...] = summed[pl.ds(at, own_tokens), :].astype(outs[step].dtype)
 
 
@@ -375,15 +438,24 @@
     cache_rows = cache_keys.shape[0]
     span_length = blk * piece // SPANS
     hidden = gate_weight.shape[2]
-    blk_at, row_at = lax.axis_index("blk"), lax.axis_index("rows")
-    far, near = blk_at // 2, blk_at % 2
     bf16, f32 = jnp.bfloat16, jnp.float32
-    smem = pl.BlockSpec(memory_space=pltpu.SMEM)
     shape_of = jax.ShapeDtypeStruct
 
     def over_far(arrays):
-        moved = [lax.ppermute(arrays[step], "blk", far_of(step, blk)) for step in range(far_count - 1, 0, -1)]
+        moved = []
+        for step in range(far_count - 1, 0, -1):
+            moved.append(lax.ppermute(arrays[step], "blk", far_of(step, blk)))
         return [arrays[0]] + moved[::-1]
+
+    def added(shape, dtype, *terms):
+        return pl.pallas_call(
+            add_kernel,
+            out_shape=shape_of(shape, dtype),
+            in_specs=in_vmem(len(terms)),
+            out_specs=pl.BlockSpec(memory_space=pltpu.VMEM),
+            compiler_params=grant(4),
+            name="added",
+        )(*terms)
 
     def over_near(array):
         return lax.ppermute(array, "blk", side_of(blk))
@@ -391,83 +463,95 @@
     def over_rows(array):
         return lax.ppermute(array, "rows", side_of(row_count))
 
+    key_side = over_near(cache_keys)
+    value_side = over_near(cache_values)
     q_pieces = over_far([queries] * far_count)
-    key_side, value_side = over_near(cache_keys), over_near(cache_values)
     weight_side = over_near(out_weight)
-    place = jnp.concatenate([jnp.stack([far, near]).astype(jnp.int32), span_starts])
+    local = [queries, cache_keys, cache_values, out_weight, gate_weight, up_weight, down_weight]
+    *local, pos_all, routes = pl.pallas_call(
+        functools.partial(prepare_kernel, (far_count, span_length)),
+        out_shape=[shape_of(a.shape, a.dtype) for a in local]
+        + [shape_of((tokens, HD), jnp.int32), shape_of((tokens, HD), f32)],
+        in_specs=[pl.BlockSpec(memory_space=pltpu.HBM)] * 10,
+        out_specs=in_vmem(9),
+        scratch_shapes=[
+            pltpu.SMEM(span_starts.shape, jnp.int32),
+            pltpu.VMEM(expert_ids.shape, jnp.int32),
+            pltpu.VMEM(gate_fixed.shape, jnp.int32),
+            pltpu.SemaphoreType.DMA((10,)),
+        ],
+        compiler_params=grant(4),
+        name="prepare",
+    )(*(pltpu.with_memory_space_constraint(a, pltpu.HBM) for a in local + [span_starts, expert_ids, gate_fixed]))
+    queries_own, keys_own, values_own, weight_own, gate_weight, up_weight, down_weight = local
+    q_pieces[0] = queries_own
     message_width = (own_heads + 1) * HD
     messages = pl.pallas_call(
-        functools.partial(attend_kernel, (far_count, span_length, cache_rows, heads)),
+        functools.partial(attend_kernel, (far_count, cache_rows, heads)),
         out_shape=[shape_of((tokens, message_width), bf16)] * far_count,
-        in_specs=[smem] + in_vmem(far_count + 6),
+        in_specs=in_vmem(far_count + 6),
         out_specs=in_vmem(far_count),
         scratch_shapes=[
             pltpu.VMEM((heads * tokens, HD), bf16),
-            pltpu.VMEM((tokens, HD), jnp.int32),
             pltpu.VMEM((2 * cache_rows, HD), bf16),
             pltpu.VMEM((2 * cache_rows, HD), bf16),
             pltpu.VMEM((far_count, tokens, message_width), bf16),
         ],
+        compiler_params=grant(12),
         name="attend",
-    )(place, *q_pieces, cache_keys, key_side, cache_values, value_side, expert_ids, gate_fixed)
+    )(*q_pieces, keys_own, key_side, values_own, value_side, pos_all, routes)
     messages = over_far(messages)
-    place = jnp.stack([far, near, row_at]).astype(jnp.int32)
     keep, send, routes = pl.pallas_call(
         functools.partial(project_kernel, (far_count, own_heads, own_tokens)),
         out_shape=[shape_of((held, width), f32), shape_of((held, width), bf16), shape_of((held, HD), f32)],
-        in_specs=[smem] + in_vmem(far_count + 2),
+        in_specs=in_vmem(far_count + 2),
         out_specs=in_vmem(3),
         scratch_shapes=[pltpu.VMEM((tokens, width), f32)],
+        compiler_params=grant(8),
         name="project",
-    )(place, *messages, out_weight, weight_side)
-    part = (keep + over_rows(send).astype(f32)).astype(bf16)
+    )(*messages, weight_own, weight_side)
+    part = added((held, width), bf16, keep, over_rows(send))
     parts = over_far([part] * far_count)
-    place = jnp.stack([far]).astype(jnp.int32)
     attn_proj, normed = pl.pallas_call(
         functools.partial(norm_kernel, (far_count, own_tokens)),
         out_shape=[shape_of((own_tokens, width), bf16), shape_of((held, width + HD), bf16)],
-        in_specs=[smem] + in_vmem(far_count + 2),
+        in_specs=in_vmem(far_count + 2),
         out_specs=in_vmem(2),
         scratch_shapes=[pltpu.VMEM((held, width), f32)],
+        compiler_params=grant(6),
         name="norm",
-    )(place, *parts, norm_gain.reshape(1, width), routes)
+    )(*parts, norm_gain.reshape(1, width), routes)
     from_side = over_near(normed)
     pieces = [normed, from_side, over_rows(normed), over_rows(from_side)]
-    chunk = math.gcd(hidden, 256)
-    place = jnp.stack([blk_at * row_count + row_at]).astype(jnp.int32)
-    whole = pl.BlockSpec((held, width + HD), lambda f: (0, 0))
     keep, send = pl.pallas_call(
         functools.partial(expert_kernel, width),
         out_shape=[shape_of((2 * held, width), bf16)] * 2,
-        grid=(hidden // chunk,),
-        in_specs=[smem]
-        + [whole] * 4
-        + [
-            pl.BlockSpec((1, width, chunk), lambda f: (0, 0, f)),
-            pl.BlockSpec((1, width, chunk), lambda f: (0, 0, f)),
-            pl.BlockSpec((1, chunk, width), lambda f: (0, f, 0)),
-        ],
-        out_specs=[pl.BlockSpec((2 * held, width), lambda f: (0, 0))] * 2,
-        scratch_shapes=[pltpu.VMEM((4 * held, width), bf16), pltpu.VMEM((4 * held, width), f32)],
+        in_specs=in_vmem(7),
+        out_specs=in_vmem(2),
+        scratch_shapes=[pltpu.VMEM((4 * held, width), bf16), pltpu.VMEM((4 * held, hidden), bf16)],
+        compiler_params=grant(8),
         name="experts",
-    )(place, *pieces, gate_weight, up_weight, down_weight)
-    both = keep.astype(f32) + over_rows(send).astype(f32)
-    ours, theirs = both[:held], both[held:].astype(bf16)
+    )(*pieces, gate_weight, up_weight, down_weight)
+    ours, theirs = pl.pallas_call(
+        halves_kernel,
+        out_shape=[shape_of((held, width), f32), shape_of((held, width), bf16)],
+        in_specs=in_vmem(2),
+        out_specs=in_vmem(2),
+        compiler_params=grant(4),
+        name="halves",
+    )(keep, over_rows(send))
     theirs = over_near(theirs)
-    place = jnp.stack([far]).astype(jnp.int32)
     shares = pl.pallas_call(
         functools.partial(spread_kernel, (far_count, own_tokens)),
         out_shape=[shape_of((own_tokens, width), f32)] + [shape_of((own_tokens, width), bf16)] * (far_count - 1),
-        in_specs=[smem] + in_vmem(2),
+        in_specs=in_vmem(2),
         out_specs=in_vmem(far_count),
         scratch_shapes=[pltpu.VMEM((held, width), f32)],
+        compiler_params=grant(4),
         name="shares",
-    )(place, ours, theirs)
+    )(ours, theirs)
     shares = over_far(shares)
-    total = shares[0]
-    for share in shares[1:]:
-        total = total + share.astype(f32)
-    return (attn_proj, total.astype(bf16))
+    return (attn_proj, added((own_tokens, width), bf16, *shares))
 
 
 def fits_pairs(mesh, queries, cache_keys, out_weight, expert_ids, gate_weight):
@@ -510,16 +594,16 @@
     )
     out_specs = (P(("groups", "blk", "rows"), None), P(("groups", "blk", "rows"), None))
 
+    def mapped(body):
+        return jax.shard_map(
+            body, mesh=mesh, in_specs=in_specs, out_specs=out_specs, check_vma=False
+        )
+
     def run(*arrays):
         queries, cache_keys, out_weight = arrays[0], arrays[1], arrays[4]
         expert_ids, gate_weight = arrays[6], arrays[8]
-        paired = fits_pairs(mesh, queries, cache_keys, out_weight, expert_ids, gate_weight)
-        return jax.shard_map(
-            paired_device if paired else on_device,
-            mesh=mesh,
-            in_specs=in_specs,
-            out_specs=out_specs,
-            check_vma=False,
-        )(*arrays)
+        if not fits_pairs(mesh, queries, cache_keys, out_weight, expert_ids, gate_weight):
+            return mapped(on_device)(*arrays)
+        return mapped(paired_device)(*arrays)
 
     return run

time: 92.8 us -> 73.7 us (0.79)
  Pallas kernels: 16.5 us -> 9.41 us
  local copies, waits for them, and re-layouts: 5.46 us -> 0.01 us
  other arithmetic: 5.35 us -> 0 us
  waiting for transfers between devices: 36.7 us -> 33.4 us
  starting transfers between devices: 27.8 us -> 29.9 us
    pallas_call x1, Pallas kernels: 6.74 us -> 1.5 us  [paired_device(): pl.pallas_call(functools.partial(expert_kernel, width), out_shape=[shape_...]
    unnamed x34 -> x2, local copies, waits for them, and re-layouts: 3.45 us -> 0.01 us
    pallas_call x1 -> x5, Pallas kernels: 3.5 us -> 6.55 us  [the longest x1 4.18 us: paired_device(): pl.pallas_call(functools.partial(prepare_kernel, (far_count, span_length)...]
    convert_element_type x2 -> x0, other arithmetic: 2.46 us -> none  [the longest x1 1.47 us: paired_device(): return (attn_proj, total.astype(bf16))]
    ppermute x12, starting transfers between devices: 19.4 us -> 21.5 us  [over_far(): moved.append(lax.ppermute(arrays[step], 'blk', far_of(step, blk)))]
    pallas_call x1, Pallas kernels: 2.64 us -> 0.6 us  [paired_device(): pl.pallas_call(functools.partial(project_kernel, (far_count, own_heads, o...]
    pallas_call x1, Pallas kernels: 1.67 us -> 0.04 us  [paired_device(): pl.pallas_call(functools.partial(spread_kernel, (far_count, own_tokens)),...]
    ppermute x12, waiting for transfers between devices: 19.5 us -> 18 us  [over_far(): moved.append(lax.ppermute(arrays[step], 'blk', far_of(step, blk)))]
  transfers between devices with their start and end apart: 21 -> 21, of which waited for: 14 -> 15; matrix products, arithmetic and copies ran while one was open for 4% -> 0% of each run, Pallas kernels for 4% -> 8%
where the time goes in v2:
time: 73.7 us; the launch traced here: 73.5 us
  waiting for transfers between devices  33.4 us (45%)
  starting transfers between devices  29.9 us (41%)
  Pallas kernels  9.41 us (13%)
  between operations  0.74 us (1%)
    ppermute x12, starting transfers between devices, over_far(): moved.append(lax.ppermute(arrays[step], 'blk', far_of(step, blk)))  21.5 us
    ppermute x12, waiting for transfers between devices, over_far(): moved.append(lax.ppermute(arrays[step], 'blk', far_of(step, blk)))  18 us
    ppermute x5, waiting for transfers between devices, over_near(): return lax.ppermute(array, 'blk', side_of(blk))  11.3 us
    ppermute x5, starting transfers between devices, over_near(): return lax.ppermute(array, 'blk', side_of(blk))  8.19 us
    pallas_call x1, Pallas kernels, paired_device(): pl.pallas_call(functools.partial(prepare_kernel, (far_count, span_length)...  4.18 us
    ppermute x4, waiting for transfers between devices, over_rows(): return lax.ppermute(array, 'rows', side_of(row_count))  4.08 us
    pallas_call x1, Pallas kernels, paired_device(): pl.pallas_call(functools.partial(attend_kernel, (far_count, cache_rows, h...  1.65 us
    pallas_call x1, Pallas kernels, paired_device(): pl.pallas_call(functools.partial(expert_kernel, width), out_shape=[shape_...  1.5 us
  transfers between devices with their start and end apart: 21, of which 15 were waited for; matrix products, arithmetic and copies ran while one was open for 0% of the time, Pallas kernels for 8%

profile of v2, /device:TPU:0, one launch (start us, length us, event | category | flops | bytes accessed | tf_op | source)
XLA Modules:
  0.0 73.5 jit_solution(14295664794465700553)
XLA Ops:
  0.6 3.1 %collective-permute-start.8 = (bf16[128,2048]{1,0:T(8,128)(2,1)}, bf16[128,2048]{1,0:T(8,128)(2,1)S(1)}, u32[]{:S(2)}, u32[]{:S(2)}) collective-permute-start(bf16[128,2048]{1,0:T(8,128)(2,1)} %refs_3_.1), channel_id=1, source_target_pairs={{0,2},{2,0},{4,6},{6,4},{8,10},{10,8},{12,14},{14,12},{1,3},{3,1},... | collective-permute-start | bytes 1572872 | tf_op jit(solution)/shard_map/ppermute | solution.py:461
  3.7 0.1 collective-permute-start.3
  3.8 1.9 %collective-permute-start.4 = (bf16[512,128]{1,0:T(8,128)(2,1)}, bf16[512,128]{1,0:T(8,128)(2,1)S(1)}, u32[]{:S(2)}, u32[]{:S(2)}) collective-permute-start(bf16[512,128]{1,0:T(8,128)(2,1)} %refs_2_.1), channel_id=1, source_target_pairs={{0,2},{2,0},{4,6},{6,4},{8,10},{10,8},{12,14},{14,12},{1,3},{3,1},... | collective-permute-start | bytes 393224 | tf_op jit(solution)/shard_map/ppermute | solution.py:461
  5.7 1.6 %collective-permute-start = (bf16[16,1024]{1,0:T(8,128)(2,1)}, bf16[16,1024]{1,0:T(8,128)(2,1)S(1)}, u32[]{:S(2)}, u32[]{:S(2)}) collective-permute-start(bf16[16,1024]{1,0:T(8,128)(2,1)} %refs_0_.1), channel_id=1, source_target_pairs={{0,4},{2,6},{4,0},{6,2},{8,12},{10,14},{12,8},{14,10},{1,5},{3,7},... | collective-permute-start | bytes 98312 | tf_op jit(solution)/shard_map/ppermute | solution.py:447
  7.3 2.6 %collective-permute-start.1 = (bf16[16,1024]{1,0:T(8,128)(2,1)}, bf16[16,1024]{1,0:T(8,128)(2,1)S(1)}, u32[]{:S(2)}, u32[]{:S(2)}) collective-permute-start(bf16[16,1024]{1,0:T(8,128)(2,1)} %refs_0_.1), channel_id=1, source_target_pairs={{0,8},{2,10},{4,12},{6,14},{8,0},{10,2},{12,4},{14,6},{1,9},{3,11}... | collective-permute-start | bytes 98312 | tf_op jit(solution)/shard_map/ppermute | solution.py:447
  9.9 0.2 collective-permute-done.refs_1_
  10.1 3.3 %collective-permute-start.2 = (bf16[16,1024]{1,0:T(8,128)(2,1)}, bf16[16,1024]{1,0:T(8,128)(2,1)S(1)}, u32[]{:S(2)}, u32[]{:S(2)}) collective-permute-start(bf16[16,1024]{1,0:T(8,128)(2,1)} %refs_0_.1), channel_id=1, source_target_pairs={{0,12},{2,14},{4,8},{6,10},{8,4},{10,6},{12,0},{14,2},{1,13},{3,15... | collective-permute-start | bytes 98312 | tf_op jit(solution)/shard_map/ppermute | solution.py:447
  13.5 4.2 %prepare.1 = (bf16[16,1024]{1,0:T(8,128)(2,1)S(1)}, bf16[512,128]{1,0:T(8,128)(2,1)S(1)}, bf16[512,128]{1,0:T(8,128)(2,1)S(1)}, bf16[128,2048]{1,0:T(8,128)(2,1)...) custom-call(bf16[16,1024]{1,0:T(8,128)(2,1)} %refs_0_.1, ...), custom_call_target="tpu_custom_call" | custom-call | tf_op jit(solution)/shard_map/prepare/pallas_call | solution.py:471
  17.6 0.0 collective-permute-done.1.refs_2_
  17.7 0.0 collective-permute-done.2.refs_3_
  17.7 1.8 %collective-permute-done.3.refs_5_ = bf16[512,128]{1,0:T(8,128)(2,1)S(1)} collective-permute-done((bf16[512,128]{1,0:T(8,128)(2,1)}, bf16[512,128]{1,0:T(8,128)(2,1)S(1)}, u32[]{:S(2)}, u32[]{:S(2)}) %collective-permute-start.3) | collective-permute-done | bytes 131104 | tf_op jit(solution)/shard_map/ppermute | solution.py:461
  19.5 2.0 %collective-permute-done.4.refs_7_ = bf16[512,128]{1,0:T(8,128)(2,1)S(1)} collective-permute-done((bf16[512,128]{1,0:T(8,128)(2,1)}, bf16[512,128]{1,0:T(8,128)(2,1)S(1)}, u32[]{:S(2)}, u32[]{:S(2)}) %collective-permute-start.4) | collective-permute-done | bytes 131104 | tf_op jit(solution)/shard_map/ppermute | solution.py:461
  21.5 1.7 %attend.1 = (bf16[64,384]{1,0:T(8,128)(2,1)S(1)}, bf16[64,384]{1,0:T(8,128)(2,1)S(1)}, bf16[64,384]{1,0:T(8,128)(2,1)S(1)}, bf16[64,384]{1,0:T(8,128)(2,1)S(1)}) custom-call(bf16[16,1024]{1,0:T(8,128)(2,1)S(1)} %get-tuple-element.28.refs_0_, bf16[16,1024]{1,0:T(8,128)(2,1)S(1)} %collective-permute-done.refs_1_, ...), custom_call_target="tpu_custom_call" | custom-call | tf_op jit(solution)/shard_map/attend/pallas_call | solution.py:489
  23.1 1.9 %collective-permute-start.5 = (bf16[64,384]{1,0:T(8,128)(2,1)S(1)}, bf16[64,384]{1,0:T(8,128)(2,1)S(1)}, u32[]{:S(2)}, u32[]{:S(2)}) collective-permute-start(bf16[64,384]{1,0:T(8,128)(2,1)S(1)} %get-tuple-element.34), channel_id=1, source_target_pairs={{0,4},{2,6},{4,0},{6,2},{8,12},{10,14},{12,8},{14,10},{1,5},{3,7},... | collective-permute-start | bytes 147464 | tf_op jit(solution)/shard_map/ppermute | solution.py:447
  25.0 2.6 %collective-permute-start.6 = (bf16[64,384]{1,0:T(8,128)(2,1)S(1)}, bf16[64,384]{1,0:T(8,128)(2,1)S(1)}, u32[]{:S(2)}, u32[]{:S(2)}) collective-permute-start(bf16[64,384]{1,0:T(8,128)(2,1)S(1)} %get-tuple-element.35), channel_id=1, source_target_pairs={{0,8},{2,10},{4,12},{6,14},{8,0},{10,2},{12,4},{14,6},{1,9},{3,11}... | collective-permute-start | bytes 147464 | tf_op jit(solution)/shard_map/ppermute | solution.py:447
  27.6 0.0 collective-permute-start.7
  27.6 0.2 collective-permute-done.5.refs_1_
  27.7 3.3 %collective-permute-done.6.refs_2_ = bf16[64,384]{1,0:T(8,128)(2,1)S(1)} collective-permute-done((bf16[64,384]{1,0:T(8,128)(2,1)S(1)}, bf16[64,384]{1,0:T(8,128)(2,1)S(1)}, u32[]{:S(2)}, u32[]{:S(2)}) %collective-permute-start.6) | collective-permute-done | bytes 49184 | tf_op jit(solution)/shard_map/ppermute | solution.py:447
  31.0 2.4 %collective-permute-done.7.refs_3_ = bf16[64,384]{1,0:T(8,128)(2,1)S(1)} collective-permute-done((bf16[64,384]{1,0:T(8,128)(2,1)S(1)}, bf16[64,384]{1,0:T(8,128)(2,1)S(1)}, u32[]{:S(2)}, u32[]{:S(2)}) %collective-permute-start.7) | collective-permute-done | bytes 49184 | tf_op jit(solution)/shard_map/ppermute | solution.py:447
  33.5 0.0 collective-permute-done.8.refs_5_
  33.5 0.6 project.1
  34.1 0.1 collective-permute-start.9
  34.1 1.3 %collective-permute-done.9.refs_1_ = bf16[32,2048]{1,0:T(8,128)(2,1)S(1)} collective-permute-done((bf16[32,2048]{1,0:T(8,128)(2,1)S(1)}, bf16[32,2048]{1,0:T(8,128)(2,1)S(1)}, u32[]{:S(2)}, u32[]{:S(2)}) %collective-permute-start.9) | collective-permute-done | bytes 131104 | tf_op jit(solution)/shard_map/ppermute | solution.py:464
  35.5 0.1 collective-permute-start.10
  35.6 1.1 %collective-permute-start.11 = (bf16[32,2048]{1,0:T(8,128)(2,1)S(1)}, bf16[32,2048]{1,0:T(8,128)(2,1)S(1)}, u32[]{:S(2)}, u32[]{:S(2)}) collective-permute-start(bf16[32,2048]{1,0:T(8,128)(2,1)S(1)} %added.2.refs_0_), channel_id=1, source_target_pairs={{0,8},{2,10},{4,12},{6,14},{8,0},{10,2},{12,4},{14,6},{1,9},{3,11}... | collective-permute-start | bytes 393224 | tf_op jit(solution)/shard_map/ppermute | solution.py:447
  36.7 3.3 %collective-permute-start.12 = (bf16[32,2048]{1,0:T(8,128)(2,1)S(1)}, bf16[32,2048]{1,0:T(8,128)(2,1)S(1)}, u32[]{:S(2)}, u32[]{:S(2)}) collective-permute-start(bf16[32,2048]{1,0:T(8,128)(2,1)S(1)} %added.2.refs_0_), channel_id=1, source_target_pairs={{0,12},{2,14},{4,8},{6,10},{8,4},{10,6},{12,0},{14,2},{1,13},{3,15... | collective-permute-start | bytes 393224 | tf_op jit(solution)/shard_map/ppermute | solution.py:447
  40.0 2.3 %collective-permute-done.10.refs_1_ = bf16[32,2048]{1,0:T(8,128)(2,1)S(1)} collective-permute-done((bf16[32,2048]{1,0:T(8,128)(2,1)S(1)}, bf16[32,2048]{1,0:T(8,128)(2,1)S(1)}, u32[]{:S(2)}, u32[]{:S(2)}) %collective-permute-start.10) | collective-permute-done | bytes 131104 | tf_op jit(solution)/shard_map/ppermute | solution.py:447
  42.3 6.3 %collective-permute-done.11.refs_2_ = bf16[32,2048]{1,0:T(8,128)(2,1)S(1)} collective-permute-done((bf16[32,2048]{1,0:T(8,128)(2,1)S(1)}, bf16[32,2048]{1,0:T(8,128)(2,1)S(1)}, u32[]{:S(2)}, u32[]{:S(2)}) %collective-permute-start.11) | collective-permute-done | bytes 131104 | tf_op jit(solution)/shard_map/ppermute | solution.py:447
  48.6 0.0 collective-permute-done.12.refs_3_
  48.6 0.7 norm.1
  49.3 1.5 %collective-permute-start.13 = (bf16[32,2176]{1,0:T(8,128)(2,1)S(1)}, bf16[32,2176]{1,0:T(8,128)(2,1)S(1)}, u32[]{:S(2)}, u32[]{:S(2)}) collective-permute-start(bf16[32,2176]{1,0:T(8,128)(2,1)S(1)} %get-tuple-element.42.refs_0_), channel_id=1, source_target_pairs={{0,2},{2,0},{4,6},{6,4},{8,10},{10,8},{12,14},{14,12},{1,3},{3,1},... | collective-permute-start | bytes 417800 | tf_op jit(solution)/shard_map/ppermute | solution.py:461
  50.8 0.0 collective-permute-start.14
  50.8 3.5 %collective-permute-done.13.refs_1_ = bf16[32,2176]{1,0:T(8,128)(2,1)S(1)} collective-permute-done((bf16[32,2176]{1,0:T(8,128)(2,1)S(1)}, bf16[32,2176]{1,0:T(8,128)(2,1)S(1)}, u32[]{:S(2)}, u32[]{:S(2)}) %collective-permute-start.13) | collective-permute-done | bytes 139296 | tf_op jit(solution)/shard_map/ppermute | solution.py:461
  54.4 0.0 collective-permute-start.15
  54.4 0.0 collective-permute-done.14.refs_2_
  54.4 1.4 %collective-permute-done.15.refs_3_ = bf16[32,2176]{1,0:T(8,128)(2,1)S(1)} collective-permute-done((bf16[32,2176]{1,0:T(8,128)(2,1)S(1)}, bf16[32,2176]{1,0:T(8,128)(2,1)S(1)}, u32[]{:S(2)}, u32[]{:S(2)}) %collective-permute-start.15) | collective-permute-done | bytes 139296 | tf_op jit(solution)/shard_map/ppermute | solution.py:464
  55.7 1.5 %experts.1 = (bf16[64,2048]{1,0:T(8,128)(2,1)S(1)}, bf16[64,2048]{1,0:T(8,128)(2,1)S(1)}) custom-call(bf16[32,2176]{1,0:T(8,128)(2,1)S(1)} %get-tuple-element.42.refs_0_, bf16[32,2176]{1,0:T(8,128)(2,1)S(1)} %collective-permute-done.13.refs_1_, bf16[32,2176]{1,0:T(8,128)(2,1)S(1)} %collective-permute-done.14.refs_2_, ...), custom_call_target="tpu_custom_call" | custom-call | tf_op jit(solution)/shard_map/experts/pallas_call | solution.py:526
  57.2 0.2 collective-permute-start.16
  57.4 1.4 %collective-permute-done.16.received = bf16[64,2048]{1,0:T(8,128)(2,1)S(1)} collective-permute-done((bf16[64,2048]{1,0:T(8,128)(2,1)S(1)}, bf16[64,2048]{1,0:T(8,128)(2,1)S(1)}, u32[]{:S(2)}, u32[]{:S(2)}) %collective-permute-start.16) | collective-permute-done | bytes 262176 | tf_op jit(solution)/shard_map/ppermute | solution.py:464
  58.8 0.1 halves.1
  58.9 1.6 %collective-permute-start.17 = (bf16[32,2048]{1,0:T(8,128)(2,1)S(1)}, bf16[32,2048]{1,0:T(8,128)(2,1)S(1)}, u32[]{:S(2)}, u32[]{:S(2)}) collective-permute-start(bf16[32,2048]{1,0:T(8,128)(2,1)S(1)} %get-tuple-element.49), channel_id=1, source_target_pairs={{0,2},{2,0},{4,6},{6,4},{8,10},{10,8},{12,14},{14,12},{1,3},{3,1},... | collective-permute-start | bytes 393224 | tf_op jit(solution)/shard_map/ppermute | solution.py:461
  60.5 4.0 %collective-permute-done.17.refs_1_ = bf16[32,2048]{1,0:T(8,128)(2,1)S(1)} collective-permute-done((bf16[32,2048]{1,0:T(8,128)(2,1)S(1)}, bf16[32,2048]{1,0:T(8,128)(2,1)S(1)}, u32[]{:S(2)}, u32[]{:S(2)}) %collective-permute-start.17) | collective-permute-done | bytes 131104 | tf_op jit(solution)/shard_map/ppermute | solution.py:461
  64.6 2.6 %collective-permute-start.18 = (bf16[8,2048]{1,0:T(8,128)(2,1)S(1)}, bf16[8,2048]{1,0:T(8,128)(2,1)S(1)}, u32[]{:S(2)}, u32[]{:S(2)}) collective-permute-start(bf16[8,2048]{1,0:T(8,128)(2,1)S(1)} %get-tuple-element.51), channel_id=1, source_target_pairs={{0,4},{2,6},{4,0},{6,2},{8,12},{10,14},{12,8},{14,10},{1,5},{3,7},... | collective-permute-start | bytes 98312 | tf_op jit(solution)/shard_map/ppermute | solution.py:447
  67.2 0.0 collective-permute-start.19
  67.2 2.4 %collective-permute-start.20 = (bf16[8,2048]{1,0:T(8,128)(2,1)S(1)}, bf16[8,2048]{1,0:T(8,128)(2,1)S(1)}, u32[]{:S(2)}, u32[]{:S(2)}) collective-permute-start(bf16[8,2048]{1,0:T(8,128)(2,1)S(1)} %get-tuple-element.53), channel_id=1, source_target_pairs={{0,12},{2,14},{4,8},{6,10},{8,4},{10,6},{12,0},{14,2},{1,13},{3,15... | collective-permute-start | bytes 98312 | tf_op jit(solution)/shard_map/ppermute | solution.py:447
  69.6 2.4 %collective-permute-done.19.refs_2_ = bf16[8,2048]{1,0:T(8,128)(2,1)S(1)} collective-permute-done((bf16[8,2048]{1,0:T(8,128)(2,1)S(1)}, bf16[8,2048]{1,0:T(8,128)(2,1)S(1)}, u32[]{:S(2)}, u32[]{:S(2)}) %collective-permute-start.19) | collective-permute-done | bytes 32800 | tf_op jit(solution)/shard_map/ppermute | solution.py:447
  72.0 0.9 %collective-permute-done.20.refs_3_ = bf16[8,2048]{1,0:T(8,128)(2,1)S(1)} collective-permute-done((bf16[8,2048]{1,0:T(8,128)(2,1)S(1)}, bf16[8,2048]{1,0:T(8,128)(2,1)S(1)}, u32[]{:S(2)}, u32[]{:S(2)}) %collective-permute-start.20) | collective-permute-done | bytes 32800 | tf_op jit(solution)/shard_map/ppermute | solution.py:447
  72.9 0.6 added.3
  (6 shorter events, 0.1 us)
Async XLA Ops:
  0.6 39.3 %copy-start = (bf16[2048]{0:T(1024)(128)(2,1)S(1)}, bf16[2048]{0:T(1024)(128)(2,1)}, u32[]{:S(2)}) copy-start(bf16[2048]{0:T(1024)(128)(2,1)} %param.16) | copy-start | bytes 12292
  0.6 32.8 %collective-permute-start.8 = (bf16[128,2048]{1,0:T(8,128)(2,1)}, bf16[128,2048]{1,0:T(8,128)(2,1)S(1)}, u32[]{:S(2)}, u32[]{:S(2)}) collective-permute-start(bf16[128,2048]{1,0:T(8,128)(2,1)} %refs_3_.1), channel_id=1, source_target_pairs={{0,2},{2,0},{4,6},{6,4},{8,10},{10,8},{12,14},{14,12},{1,3},{3,1},... | collective-permute-start | bytes 1572872 | tf_op jit(solution)/shard_map/ppermute | solution.py:461
  3.7 15.8 %collective-permute-start.3 = (bf16[512,128]{1,0:T(8,128)(2,1)}, bf16[512,128]{1,0:T(8,128)(2,1)S(1)}, u32[]{:S(2)}, u32[]{:S(2)}) collective-permute-start(bf16[512,128]{1,0:T(8,128)(2,1)} %refs_1_.1), channel_id=1, source_target_pairs={{0,2},{2,0},{4,6},{6,4},{8,10},{10,8},{12,14},{14,12},{1,3},{3,1},... | collective-permute-start | bytes 393224 | tf_op jit(solution)/shard_map/ppermute | solution.py:461
  3.8 17.7 %collective-permute-start.4 = (bf16[512,128]{1,0:T(8,128)(2,1)}, bf16[512,128]{1,0:T(8,128)(2,1)S(1)}, u32[]{:S(2)}, u32[]{:S(2)}) collective-permute-start(bf16[512,128]{1,0:T(8,128)(2,1)} %refs_2_.1), channel_id=1, source_target_pairs={{0,2},{2,0},{4,6},{6,4},{8,10},{10,8},{12,14},{14,12},{1,3},{3,1},... | collective-permute-start | bytes 393224 | tf_op jit(solution)/shard_map/ppermute | solution.py:461
  5.7 4.4 %collective-permute-start = (bf16[16,1024]{1,0:T(8,128)(2,1)}, bf16[16,1024]{1,0:T(8,128)(2,1)S(1)}, u32[]{:S(2)}, u32[]{:S(2)}) collective-permute-start(bf16[16,1024]{1,0:T(8,128)(2,1)} %refs_0_.1), channel_id=1, source_target_pairs={{0,4},{2,6},{4,0},{6,2},{8,12},{10,14},{12,8},{14,10},{1,5},{3,7},... | collective-permute-start | bytes 98312 | tf_op jit(solution)/shard_map/ppermute | solution.py:447
  7.3 10.3 %collective-permute-start.1 = (bf16[16,1024]{1,0:T(8,128)(2,1)}, bf16[16,1024]{1,0:T(8,128)(2,1)S(1)}, u32[]{:S(2)}, u32[]{:S(2)}) collective-permute-start(bf16[16,1024]{1,0:T(8,128)(2,1)} %refs_0_.1), channel_id=1, source_target_pairs={{0,8},{2,10},{4,12},{6,14},{8,0},{10,2},{12,4},{14,6},{1,9},{3,11}... | collective-permute-start | bytes 98312 | tf_op jit(solution)/shard_map/ppermute | solution.py:447
  10.1 7.5 %collective-permute-start.2 = (bf16[16,1024]{1,0:T(8,128)(2,1)}, bf16[16,1024]{1,0:T(8,128)(2,1)S(1)}, u32[]{:S(2)}, u32[]{:S(2)}) collective-permute-start(bf16[16,1024]{1,0:T(8,128)(2,1)} %refs_0_.1), channel_id=1, source_target_pairs={{0,12},{2,14},{4,8},{6,10},{8,4},{10,6},{12,0},{14,2},{1,13},{3,15... | collective-permute-start | bytes 98312 | tf_op jit(solution)/shard_map/ppermute | solution.py:447
  23.1 4.6 %collective-permute-start.5 = (bf16[64,384]{1,0:T(8,128)(2,1)S(1)}, bf16[64,384]{1,0:T(8,128)(2,1)S(1)}, u32[]{:S(2)}, u32[]{:S(2)}) collective-permute-start(bf16[64,384]{1,0:T(8,128)(2,1)S(1)} %get-tuple-element.34), channel_id=1, source_target_pairs={{0,4},{2,6},{4,0},{6,2},{8,12},{10,14},{12,8},{14,10},{1,5},{3,7},... | collective-permute-start | bytes 147464 | tf_op jit(solution)/shard_map/ppermute | solution.py:447
  25.0 6.0 %collective-permute-start.6 = (bf16[64,384]{1,0:T(8,128)(2,1)S(1)}, bf16[64,384]{1,0:T(8,128)(2,1)S(1)}, u32[]{:S(2)}, u32[]{:S(2)}) collective-permute-start(bf16[64,384]{1,0:T(8,128)(2,1)S(1)} %get-tuple-element.35), channel_id=1, source_target_pairs={{0,8},{2,10},{4,12},{6,14},{8,0},{10,2},{12,4},{14,6},{1,9},{3,11}... | collective-permute-start | bytes 147464 | tf_op jit(solution)/shard_map/ppermute | solution.py:447
  27.6 5.9 %collective-permute-start.7 = (bf16[64,384]{1,0:T(8,128)(2,1)S(1)}, bf16[64,384]{1,0:T(8,128)(2,1)S(1)}, u32[]{:S(2)}, u32[]{:S(2)}) collective-permute-start(bf16[64,384]{1,0:T(8,128)(2,1)S(1)} %get-tuple-element.36), channel_id=1, source_target_pairs={{0,12},{2,14},{4,8},{6,10},{8,4},{10,6},{12,0},{14,2},{1,13},{3,15... | collective-permute-start | bytes 147464 | tf_op jit(solution)/shard_map/ppermute | solution.py:447
  34.1 1.4 %collective-permute-start.9 = (bf16[32,2048]{1,0:T(8,128)(2,1)S(1)}, bf16[32,2048]{1,0:T(8,128)(2,1)S(1)}, u32[]{:S(2)}, u32[]{:S(2)}) collective-permute-start(bf16[32,2048]{1,0:T(8,128)(2,1)S(1)} %get-tuple-element.39), channel_id=1, source_target_pairs={{0,1},{1,0},{2,3},{3,2},{4,5},{5,4},{6,7},{7,6},{8,9},{9,8},{10,11... | collective-permute-start | bytes 393224 | tf_op jit(solution)/shard_map/ppermute | solution.py:464
  35.5 6.8 %collective-permute-start.10 = (bf16[32,2048]{1,0:T(8,128)(2,1)S(1)}, bf16[32,2048]{1,0:T(8,128)(2,1)S(1)}, u32[]{:S(2)}, u32[]{:S(2)}) collective-permute-start(bf16[32,2048]{1,0:T(8,128)(2,1)S(1)} %added.2.refs_0_), channel_id=1, source_target_pairs={{0,4},{2,6},{4,0},{6,2},{8,12},{10,14},{12,8},{14,10},{1,5},{3,7},... | collective-permute-start | bytes 393224 | tf_op jit(solution)/shard_map/ppermute | solution.py:447
  35.6 13.0 %collective-permute-start.11 = (bf16[32,2048]{1,0:T(8,128)(2,1)S(1)}, bf16[32,2048]{1,0:T(8,128)(2,1)S(1)}, u32[]{:S(2)}, u32[]{:S(2)}) collective-permute-start(bf16[32,2048]{1,0:T(8,128)(2,1)S(1)} %added.2.refs_0_), channel_id=1, source_target_pairs={{0,8},{2,10},{4,12},{6,14},{8,0},{10,2},{12,4},{14,6},{1,9},{3,11}... | collective-permute-start | bytes 393224 | tf_op jit(solution)/shard_map/ppermute | solution.py:447
  36.7 11.9 %collective-permute-start.12 = (bf16[32,2048]{1,0:T(8,128)(2,1)S(1)}, bf16[32,2048]{1,0:T(8,128)(2,1)S(1)}, u32[]{:S(2)}, u32[]{:S(2)}) collective-permute-start(bf16[32,2048]{1,0:T(8,128)(2,1)S(1)} %added.2.refs_0_), channel_id=1, source_target_pairs={{0,12},{2,14},{4,8},{6,10},{8,4},{10,6},{12,0},{14,2},{1,13},{3,15... | collective-permute-start | bytes 393224 | tf_op jit(solution)/shard_map/ppermute | solution.py:447
  49.3 5.1 %collective-permute-start.13 = (bf16[32,2176]{1,0:T(8,128)(2,1)S(1)}, bf16[32,2176]{1,0:T(8,128)(2,1)S(1)}, u32[]{:S(2)}, u32[]{:S(2)}) collective-permute-start(bf16[32,2176]{1,0:T(8,128)(2,1)S(1)} %get-tuple-element.42.refs_0_), channel_id=1, source_target_pairs={{0,2},{2,0},{4,6},{6,4},{8,10},{10,8},{12,14},{14,12},{1,3},{3,1},... | collective-permute-start | bytes 417800 | tf_op jit(solution)/shard_map/ppermute | solution.py:461
  50.8 3.5 %collective-permute-start.14 = (bf16[32,2176]{1,0:T(8,128)(2,1)S(1)}, bf16[32,2176]{1,0:T(8,128)(2,1)S(1)}, u32[]{:S(2)}, u32[]{:S(2)}) collective-permute-start(bf16[32,2176]{1,0:T(8,128)(2,1)S(1)} %get-tuple-element.42.refs_0_), channel_id=1, source_target_pairs={{0,1},{1,0},{2,3},{3,2},{4,5},{5,4},{6,7},{7,6},{8,9},{9,8},{10,11... | collective-permute-start | bytes 417800 | tf_op jit(solution)/shard_map/ppermute | solution.py:464
  54.4 1.4 %collective-permute-start.15 = (bf16[32,2176]{1,0:T(8,128)(2,1)S(1)}, bf16[32,2176]{1,0:T(8,128)(2,1)S(1)}, u32[]{:S(2)}, u32[]{:S(2)}) collective-permute-start(bf16[32,2176]{1,0:T(8,128)(2,1)S(1)} %collective-permute-done.13.refs_1_), channel_id=1, source_target_pairs={{0,1},{1,0},{2,3},{3,2},{4,5},{5,4},{6,7},{7,6},{8,9},{9,8},{10,11... | collective-permute-start | bytes 417800 | tf_op jit(solution)/shard_map/ppermute | solution.py:464
  57.2 1.6 %collective-permute-start.16 = (bf16[64,2048]{1,0:T(8,128)(2,1)S(1)}, bf16[64,2048]{1,0:T(8,128)(2,1)S(1)}, u32[]{:S(2)}, u32[]{:S(2)}) collective-permute-start(bf16[64,2048]{1,0:T(8,128)(2,1)S(1)} %get-tuple-element.47), channel_id=1, source_target_pairs={{0,1},{1,0},{2,3},{3,2},{4,5},{5,4},{6,7},{7,6},{8,9},{9,8},{10,11... | collective-permute-start | bytes 786440 | tf_op jit(solution)/shard_map/ppermute | solution.py:464
  58.9 5.6 %collective-permute-start.17 = (bf16[32,2048]{1,0:T(8,128)(2,1)S(1)}, bf16[32,2048]{1,0:T(8,128)(2,1)S(1)}, u32[]{:S(2)}, u32[]{:S(2)}) collective-permute-start(bf16[32,2048]{1,0:T(8,128)(2,1)S(1)} %get-tuple-element.49), channel_id=1, source_target_pairs={{0,2},{2,0},{4,6},{6,4},{8,10},{10,8},{12,14},{14,12},{1,3},{3,1},... | collective-permute-start | bytes 393224 | tf_op jit(solution)/shard_map/ppermute | solution.py:461
  64.6 5.1 %collective-permute-start.18 = (bf16[8,2048]{1,0:T(8,128)(2,1)S(1)}, bf16[8,2048]{1,0:T(8,128)(2,1)S(1)}, u32[]{:S(2)}, u32[]{:S(2)}) collective-permute-start(bf16[8,2048]{1,0:T(8,128)(2,1)S(1)} %get-tuple-element.51), channel_id=1, source_target_pairs={{0,4},{2,6},{4,0},{6,2},{8,12},{10,14},{12,8},{14,10},{1,5},{3,7},... | collective-permute-start | bytes 98312 | tf_op jit(solution)/shard_map/ppermute | solution.py:447
  67.2 4.8 %collective-permute-start.19 = (bf16[8,2048]{1,0:T(8,128)(2,1)S(1)}, bf16[8,2048]{1,0:T(8,128)(2,1)S(1)}, u32[]{:S(2)}, u32[]{:S(2)}) collective-permute-start(bf16[8,2048]{1,0:T(8,128)(2,1)S(1)} %get-tuple-element.52), channel_id=1, source_target_pairs={{0,8},{2,10},{4,12},{6,14},{8,0},{10,2},{12,4},{14,6},{1,9},{3,11}... | collective-permute-start | bytes 98312 | tf_op jit(solution)/shard_map/ppermute | solution.py:447
  67.2 5.7 %collective-permute-start.20 = (bf16[8,2048]{1,0:T(8,128)(2,1)S(1)}, bf16[8,2048]{1,0:T(8,128)(2,1)S(1)}, u32[]{:S(2)}, u32[]{:S(2)}) collective-permute-start(bf16[8,2048]{1,0:T(8,128)(2,1)S(1)} %get-tuple-element.53), channel_id=1, source_target_pairs={{0,12},{2,14},{4,8},{6,10},{8,4},{10,6},{12,0},{14,2},{1,13},{3,15... | collective-permute-start | bytes 98312 | tf_op jit(solution)/shard_map/ppermute | solution.py:447

commit v3 on v2

--- a/solution.py
+++ b/solution.py
@@ -184,9 +184,9 @@
 
 def prepare_kernel(sizes, *refs):
     far_count, span_length = sizes
-    sources, (starts_hbm, ids_hbm, gates_hbm) = refs[:7], refs[7:10]
-    targets, (pos_all, routes) = refs[10:17], refs[17:19]
-    starts, ids_ref, gates_ref, sems = refs[19:]
+    sources, (starts_hbm, ids_hbm, gates_hbm) = refs[:4], refs[4:7]
+    targets, (pos_all, routes) = refs[7:11], refs[11:13]
+    starts, ids_ref, gates_ref, sems = refs[13:]
     copies = [
         pltpu.make_async_copy(source, target, sems.at[at])
         for at, (source, target) in enumerate(
@@ -219,6 +219,18 @@
         [high, weight_of - high, jnp.zeros((tokens - 2 * own_tokens, HD), jnp.float32)], axis=0
     )
     for copy in copies[3:]:
+        copy.wait()
+
+
+def fetch_kernel(*refs):
+    count = len(refs) // 2
+    sems = refs[-1]
+    copies = [
+        pltpu.make_async_copy(refs[at], refs[count + at], sems.at[at]) for at in range(count)
+    ]
+    for copy in copies:
+        copy.start()
+    for copy in copies:
         copy.wait()
 
 
@@ -309,31 +321,40 @@
     piece = tokens // far_count
     other = 1 - row_at
     mine, theirs = [], []
-    for source in range(far_count):
-        at = pl.multiple_of(source * piece + row_at * own_tokens, own_tokens)
+    for step in range(far_count):
+        at = pl.multiple_of((far ^ step) * piece + row_at * own_tokens, own_tokens)
         mine.append(partial[pl.ds(at, own_tokens), :])
-        at = pl.multiple_of(source * piece + other * own_tokens, own_tokens)
+        at = pl.multiple_of((far ^ step) * piece + other * own_tokens, own_tokens)
         theirs.append(partial[pl.ds(at, own_tokens), :])
     keep[...] = jnp.concatenate(mine, axis=0)
     send[...] = jnp.concatenate(theirs, axis=0).astype(jnp.bfloat16)
-    for step in range(far_count):
+    for at, step in enumerate(range(0, far_count, 2)):
         e = extras[step]
-        at = pl.multiple_of((far ^ step) * own_tokens, own_tokens)
-        routes[pl.ds(at, own_tokens), :] = e[:own_tokens] + e[own_tokens : 2 * own_tokens]
-
-
-def norm_kernel(sizes, *refs):
-    far_count, own_tokens = sizes
+        routes[at * own_tokens : (at + 1) * own_tokens, :] = (
+            e[:own_tokens] + e[own_tokens : 2 * own_tokens]
+        )
+
+
+def parts_kernel(keep, received, *outs):
+    far_count = len(outs)
+    own_tokens = keep.shape[0] // far_count
+    total = keep[...] + received[...].astype(jnp.float32)
+    blocks = [total[at * own_tokens : (at + 1) * own_tokens] for at in range(far_count)]
+    for step, out in enumerate(outs):
+        taken = [blocks[step ^ even] for even in range(0, far_count, 2)]
+        out[...] = jnp.concatenate(taken, axis=0).astype(out.dtype)
+
+
+def norm_kernel(far_count, *refs):
     parts = refs[:far_count]
-    gain, routes, own_rows, spread, summed = refs[far_count:]
+    gain, routes, own_rows, spread = refs[far_count:]
     width = gain.shape[1]
     total = parts[0][...].astype(jnp.float32)
     for part in parts[1:]:
         total += part[...].astype(jnp.float32)
-    values_f = total.astype(jnp.bfloat16).astype(jnp.float32)
-    summed[...] = values_f
-    at = pl.multiple_of(place_of()[0] * own_tokens, own_tokens)
-    own_rows[...] = summed[pl.ds(at, own_tokens), :].astype(jnp.bfloat16)
+    rounded = total.astype(jnp.bfloat16)
+    values_f = rounded.astype(jnp.float32)
+    own_rows[...] = rounded[: own_rows.shape[0]]
     mean_square = jnp.mean(values_f * values_f, axis=1, keepdims=True)
     spread[:, :width] = (
         values_f * lax.rsqrt(mean_square + EPSILON) * gain[...].astype(jnp.float32)
@@ -348,9 +369,9 @@
     ).astype(jnp.bfloat16)
 
 
-def expert_kernel(width, *refs):
-    pieces = refs[:4]
-    gate, up, down, keep, send, gathered, hidden = refs[4:]
+def expert_kernel(width, count, *refs):
+    pieces = refs[:count]
+    gate, up, down, keep, send, gathered, hidden = refs[count:]
     rows = pieces[0].shape[0]
     for at, piece in enumerate(pieces):
         gathered[at * rows : (at + 1) * rows, :] = piece[:, :width]
@@ -379,8 +400,8 @@
         result = jnp.dot(acted, down[0, :, first:last], preferred_element_type=jnp.float32)
         result = result.astype(jnp.bfloat16).astype(jnp.float32)
         for at, share in enumerate(shares):
-            target = keep if at < 2 else send
-            half = at % 2
+            target = keep if at < count // 2 else send
+            half = at % (count // 2)
             target[half * rows : (half + 1) * rows, first:last] = (
                 share * result[at * rows : (at + 1) * rows]
             ).astype(jnp.bfloat16)
@@ -394,23 +415,23 @@
     out[...] = total.astype(out.dtype)
 
 
-def halves_kernel(keep, received, ours, theirs):
-    held = ours.shape[0]
-    ours[...] = keep[:held, :].astype(jnp.float32) + received[:held, :].astype(jnp.float32)
-    theirs[...] = (
-        keep[held:, :].astype(jnp.float32) + received[held:, :].astype(jnp.float32)
-    ).astype(jnp.bfloat16)
-
-
-def spread_kernel(sizes, *refs):
-    far_count, own_tokens = sizes
-    ours, theirs = refs[:2]
-    outs = refs[2 : 2 + far_count]
-    summed = refs[2 + far_count]
-    summed[...] = ours[...].astype(jnp.float32) + theirs[...].astype(jnp.float32)
-    for step in range(far_count):
-        at = pl.multiple_of((place_of()[0] ^ step) * own_tokens, own_tokens)
-        outs[step][...] = summed[pl.ds(at, own_tokens), :].astype(outs[step].dtype)
+def quarters_kernel(keep, received, *outs):
+    rows = outs[0].shape[0]
+    for at, out in enumerate(outs):
+        part = slice(at * rows, (at + 1) * rows)
+        out[...] = (
+            keep[part, :].astype(jnp.float32) + received[part, :].astype(jnp.float32)
+        ).astype(out.dtype)
+
+
+def last_kernel(*refs):
+    terms, outs = refs[:4], refs[4:]
+    rows = outs[0].shape[0]
+    total = terms[0][...]
+    for term in terms[1:]:
+        total += term[...].astype(jnp.float32)
+    for at, out in enumerate(outs):
+        out[...] = total[at * rows : (at + 1) * rows].astype(out.dtype)
 
 
 def paired_device(
@@ -434,6 +455,7 @@
     own_tokens = expert_ids.shape[0]
     tokens = far_count * piece
     held = far_count * own_tokens
+    shared = held // 2
     width = out_weight.shape[1]
     cache_rows = cache_keys.shape[0]
     span_length = blk * piece // SPANS
@@ -446,6 +468,19 @@
         for step in range(far_count - 1, 0, -1):
             moved.append(lax.ppermute(arrays[step], "blk", far_of(step, blk)))
         return [arrays[0]] + moved[::-1]
+
+    def in_hbm(arrays):
+        return [pltpu.with_memory_space_constraint(a, pltpu.HBM) for a in arrays]
+
+    def fetched(*arrays):
+        return pl.pallas_call(
+            fetch_kernel,
+            out_shape=[shape_of(a.shape, a.dtype) for a in arrays],
+            in_specs=[pl.BlockSpec(memory_space=pltpu.HBM)] * len(arrays),
+            out_specs=in_vmem(len(arrays)),
+            scratch_shapes=[pltpu.SemaphoreType.DMA((len(arrays),))],
+            compiler_params=grant(4),
+        )(*in_hbm(arrays))
 
     def added(shape, dtype, *terms):
         return pl.pallas_call(
@@ -457,6 +492,13 @@
             name="added",
         )(*terms)
 
+    def over_close(arrays):
+        moved = []
+        for at, step in ((3, 3), (1, 1), (2, 2)):
+            pairs = [(source, source ^ step) for source in range(blk)]
+            moved.append(lax.ppermute(arrays[at], "blk", pairs))
+        return [arrays[0], moved[1], moved[2], moved[0]]
+
     def over_near(array):
         return lax.ppermute(array, "blk", side_of(blk))
 
@@ -467,23 +509,23 @@
     value_side = over_near(cache_values)
     q_pieces = over_far([queries] * far_count)
     weight_side = over_near(out_weight)
-    local = [queries, cache_keys, cache_values, out_weight, gate_weight, up_weight, down_weight]
+    local = [queries, cache_keys, cache_values, out_weight]
     *local, pos_all, routes = pl.pallas_call(
         functools.partial(prepare_kernel, (far_count, span_length)),
         out_shape=[shape_of(a.shape, a.dtype) for a in local]
         + [shape_of((tokens, HD), jnp.int32), shape_of((tokens, HD), f32)],
-        in_specs=[pl.BlockSpec(memory_space=pltpu.HBM)] * 10,
-        out_specs=in_vmem(9),
+        in_specs=[pl.BlockSpec(memory_space=pltpu.HBM)] * 7,
+        out_specs=in_vmem(6),
         scratch_shapes=[
             pltpu.SMEM(span_starts.shape, jnp.int32),
             pltpu.VMEM(expert_ids.shape, jnp.int32),
             pltpu.VMEM(gate_fixed.shape, jnp.int32),
-            pltpu.SemaphoreType.DMA((10,)),
+            pltpu.SemaphoreType.DMA((7,)),
         ],
         compiler_params=grant(4),
         name="prepare",
-    )(*(pltpu.with_memory_space_constraint(a, pltpu.HBM) for a in local + [span_starts, expert_ids, gate_fixed]))
-    queries_own, keys_own, values_own, weight_own, gate_weight, up_weight, down_weight = local
+    )(*in_hbm(local + [span_starts, expert_ids, gate_fixed]))
+    queries_own, keys_own, values_own, weight_own = local
     q_pieces[0] = queries_own
     message_width = (own_heads + 1) * HD
     messages = pl.pallas_call(
@@ -501,57 +543,71 @@
         name="attend",
     )(*q_pieces, keys_own, key_side, values_own, value_side, pos_all, routes)
     messages = over_far(messages)
+    (down_weight,) = fetched(down_weight)
     keep, send, routes = pl.pallas_call(
         functools.partial(project_kernel, (far_count, own_heads, own_tokens)),
-        out_shape=[shape_of((held, width), f32), shape_of((held, width), bf16), shape_of((held, HD), f32)],
+        out_shape=[shape_of((held, width), f32), shape_of((held, width), bf16), shape_of((shared, HD), f32)],
         in_specs=in_vmem(far_count + 2),
         out_specs=in_vmem(3),
         scratch_shapes=[pltpu.VMEM((tokens, width), f32)],
         compiler_params=grant(8),
         name="project",
     )(*messages, weight_own, weight_side)
-    part = added((held, width), bf16, keep, over_rows(send))
-    parts = over_far([part] * far_count)
+    parts = pl.pallas_call(
+        parts_kernel,
+        out_shape=[shape_of((shared, width), f32)] + [shape_of((shared, width), bf16)] * (far_count - 1),
+        in_specs=in_vmem(2),
+        out_specs=in_vmem(far_count),
+        compiler_params=grant(4),
+        name="parts",
+    )(keep, over_rows(send))
+    parts = over_far(parts)
+    gate_weight, up_weight = fetched(gate_weight, up_weight)
     attn_proj, normed = pl.pallas_call(
-        functools.partial(norm_kernel, (far_count, own_tokens)),
-        out_shape=[shape_of((own_tokens, width), bf16), shape_of((held, width + HD), bf16)],
+        functools.partial(norm_kernel, far_count),
+        out_shape=[shape_of((own_tokens, width), bf16), shape_of((shared, width + HD), bf16)],
         in_specs=in_vmem(far_count + 2),
         out_specs=in_vmem(2),
-        scratch_shapes=[pltpu.VMEM((held, width), f32)],
-        compiler_params=grant(6),
+        compiler_params=grant(4),
         name="norm",
     )(*parts, norm_gain.reshape(1, width), routes)
-    from_side = over_near(normed)
-    pieces = [normed, from_side, over_rows(normed), over_rows(from_side)]
+    pieces = over_close([normed] * 4)
+    pieces = pieces + [over_rows(piece) for piece in pieces]
     keep, send = pl.pallas_call(
-        functools.partial(expert_kernel, width),
-        out_shape=[shape_of((2 * held, width), bf16)] * 2,
-        in_specs=in_vmem(7),
+        functools.partial(expert_kernel, width, len(pieces)),
+        out_shape=[shape_of((4 * shared, width), bf16)] * 2,
+        in_specs=in_vmem(len(pieces) + 3),
         out_specs=in_vmem(2),
-        scratch_shapes=[pltpu.VMEM((4 * held, width), bf16), pltpu.VMEM((4 * held, hidden), bf16)],
+        scratch_shapes=[
+            pltpu.VMEM((len(pieces) * shared, width), bf16),
+            pltpu.VMEM((len(pieces) * shared, hidden), bf16),
+        ],
         compiler_params=grant(8),
         name="experts",
     )(*pieces, gate_weight, up_weight, down_weight)
-    ours, theirs = pl.pallas_call(
-        halves_kernel,
-        out_shape=[shape_of((held, width), f32), shape_of((held, width), bf16)],
+    shares = pl.pallas_call(
+        quarters_kernel,
+        out_shape=[shape_of((shared, width), f32)] + [shape_of((shared, width), bf16)] * 3,
         in_specs=in_vmem(2),
-        out_specs=in_vmem(2),
+        out_specs=in_vmem(4),
         compiler_params=grant(4),
-        name="halves",
+        name="quarters",
     )(keep, over_rows(send))
-    theirs = over_near(theirs)
-    shares = pl.pallas_call(
-        functools.partial(spread_kernel, (far_count, own_tokens)),
-        out_shape=[shape_of((own_tokens, width), f32)] + [shape_of((own_tokens, width), bf16)] * (far_count - 1),
-        in_specs=in_vmem(2),
-        out_specs=in_vmem(far_count),
-        scratch_shapes=[pltpu.VMEM((held, width), f32)],
+    shares = over_close(shares)
+    evens = list(range(0, far_count, 2))
+    last = pl.pallas_call(
+        last_kernel,
+        out_shape=[shape_of((own_tokens, width), f32)]
+        + [shape_of((own_tokens, width), bf16)] * (len(evens) - 1),
+        in_specs=in_vmem(4),
+        out_specs=in_vmem(len(evens)),
         compiler_params=grant(4),
-        name="shares",
-    )(ours, theirs)
-    shares = over_far(shares)
-    return (attn_proj, added((own_tokens, width), bf16, *shares))
+        name="last",
+    )(*shares)
+    last = [last[0]] + [
+        lax.ppermute(term, "blk", far_of(step, blk)) for term, step in zip(last[1:], evens[1:])
+    ]
+    return (attn_proj, added((own_tokens, width), bf16, *last))
 
 
 def fits_pairs(mesh, queries, cache_keys, out_weight, expert_ids, gate_weight):

time: 73.7 us -> 73.2 us (level)
  waiting for transfers between devices: 33.4 us -> 31.5 us
  Pallas kernels: 9.41 us -> 11.2 us
    ppermute x0 -> x7, waiting for transfers between devices: none -> 11.1 us  [the longest x6 7.44 us: over_close(): moved.append(lax.ppermute(arrays[at], 'blk', pairs))]
    ppermute x0 -> x7, starting transfers between devices: none -> 8.29 us  [the longest x6 7.04 us: over_close(): moved.append(lax.ppermute(arrays[at], 'blk', pairs))]
    ppermute x12 -> x9, waiting for transfers between devices: 18 us -> 11.3 us  [over_far(): moved.append(lax.ppermute(arrays[step], 'blk', far_of(step, blk)))]
    ppermute x12 -> x9, starting transfers between devices: 21.5 us -> 15.5 us  [over_far(): moved.append(lax.ppermute(arrays[step], 'blk', far_of(step, blk)))]
    ppermute x5 -> x3, waiting for transfers between devices: 11.3 us -> 6.58 us  [over_near(): return lax.ppermute(array, 'blk', side_of(blk))]
    pallas_call x4 -> x7, Pallas kernels: 2.32 us -> 7.07 us  [the longest x2 4.76 us: fetched(): pl.pallas_call(fetch_kernel, out_shape=[shape_of(a.shape, a.dtype) for a...]
    ppermute x5 -> x3, starting transfers between devices: 8.19 us -> 5.09 us  [over_near(): return lax.ppermute(array, 'blk', side_of(blk))]
    pallas_call x1, Pallas kernels: 4.18 us -> 1.28 us  [paired_device(): pl.pallas_call(functools.partial(prepare_kernel, (far_count, span_length)...]
  transfers between devices with their start and end apart: 21 -> 25, of which waited for: 15 -> 17; matrix products, arithmetic and copies ran while one was open for 0% -> 0% of each run, Pallas kernels for 8% -> 11%
where the time goes in v3:
time: 73.2 us; the launch traced here: 73 us
  waiting for transfers between devices  31.5 us (43%)
  starting transfers between devices  29.6 us (40%)
  Pallas kernels  11.2 us (15%)
  between operations  0.78 us (1%)
    ppermute x9, starting transfers between devices, over_far(): moved.append(lax.ppermute(arrays[step], 'blk', far_of(step, blk)))  15.5 us
    ppermute x9, waiting for transfers between devices, over_far(): moved.append(lax.ppermute(arrays[step], 'blk', far_of(step, blk)))  11.3 us
    ppermute x6, waiting for transfers between devices, over_close(): moved.append(lax.ppermute(arrays[at], 'blk', pairs))  7.44 us
    ppermute x6, starting transfers between devices, over_close(): moved.append(lax.ppermute(arrays[at], 'blk', pairs))  7.04 us
    ppermute x3, waiting for transfers between devices, over_near(): return lax.ppermute(array, 'blk', side_of(blk))  6.58 us
    ppermute x3, starting transfers between devices, over_near(): return lax.ppermute(array, 'blk', side_of(blk))  5.09 us
    pallas_call x2, Pallas kernels, fetched(): pl.pallas_call(fetch_kernel, out_shape=[shape_of(a.shape, a.dtype) for a...  4.76 us
    ppermute x1, waiting for transfers between devices, paired_device(): lax.ppermute(term, 'blk', far_of(step, blk))  3.63 us
  transfers between devices with their start and end apart: 25, of which 17 were waited for; matrix products, arithmetic and copies ran while one was open for 0% of the time, Pallas kernels for 11%

profile of v3, /device:TPU:0, one launch (start us, length us, event | category | flops | bytes accessed | tf_op | source)
XLA Modules:
  0.0 73.0 jit_solution(18096857118314273895)
XLA Ops:
  0.6 3.1 %collective-permute-start.8 = (bf16[128,2048]{1,0:T(8,128)(2,1)}, bf16[128,2048]{1,0:T(8,128)(2,1)S(1)}, u32[]{:S(2)}, u32[]{:S(2)}) collective-permute-start(bf16[128,2048]{1,0:T(8,128)(2,1)} %refs_3_.1), channel_id=1, source_target_pairs={{0,2},{2,0},{4,6},{6,4},{8,10},{10,8},{12,14},{14,12},{1,3},{3,1},... | collective-permute-start | bytes 1572872 | tf_op jit(solution)/shard_map/ppermute | solution.py:503
  3.7 0.1 collective-permute-start.3
  3.8 1.9 %collective-permute-start.4 = (bf16[512,128]{1,0:T(8,128)(2,1)}, bf16[512,128]{1,0:T(8,128)(2,1)S(1)}, u32[]{:S(2)}, u32[]{:S(2)}) collective-permute-start(bf16[512,128]{1,0:T(8,128)(2,1)} %refs_2_.1), channel_id=1, source_target_pairs={{0,2},{2,0},{4,6},{6,4},{8,10},{10,8},{12,14},{14,12},{1,3},{3,1},... | collective-permute-start | bytes 393224 | tf_op jit(solution)/shard_map/ppermute | solution.py:503
  5.7 1.6 %collective-permute-start = (bf16[16,1024]{1,0:T(8,128)(2,1)}, bf16[16,1024]{1,0:T(8,128)(2,1)S(1)}, u32[]{:S(2)}, u32[]{:S(2)}) collective-permute-start(bf16[16,1024]{1,0:T(8,128)(2,1)} %refs_0_.3), channel_id=1, source_target_pairs={{0,4},{2,6},{4,0},{6,2},{8,12},{10,14},{12,8},{14,10},{1,5},{3,7},... | collective-permute-start | bytes 98312 | tf_op jit(solution)/shard_map/ppermute | solution.py:469
  7.3 2.5 %collective-permute-start.2 = (bf16[16,1024]{1,0:T(8,128)(2,1)}, bf16[16,1024]{1,0:T(8,128)(2,1)S(1)}, u32[]{:S(2)}, u32[]{:S(2)}) collective-permute-start(bf16[16,1024]{1,0:T(8,128)(2,1)} %refs_0_.3), channel_id=1, source_target_pairs={{0,12},{2,14},{4,8},{6,10},{8,4},{10,6},{12,0},{14,2},{1,13},{3,15... | collective-permute-start | bytes 98312 | tf_op jit(solution)/shard_map/ppermute | solution.py:469
  9.8 0.1 collective-permute-done.refs_1_
  9.9 2.6 %collective-permute-start.1 = (bf16[16,1024]{1,0:T(8,128)(2,1)}, bf16[16,1024]{1,0:T(8,128)(2,1)S(1)}, u32[]{:S(2)}, u32[]{:S(2)}) collective-permute-start(bf16[16,1024]{1,0:T(8,128)(2,1)} %refs_0_.3), channel_id=1, source_target_pairs={{0,8},{2,10},{4,12},{6,14},{8,0},{10,2},{12,4},{14,6},{1,9},{3,11}... | collective-permute-start | bytes 98312 | tf_op jit(solution)/shard_map/ppermute | solution.py:469
  12.4 1.3 %prepare.1 = (bf16[16,1024]{1,0:T(8,128)(2,1)S(1)}, bf16[512,128]{1,0:T(8,128)(2,1)S(1)}, bf16[512,128]{1,0:T(8,128)(2,1)S(1)}, bf16[128,2048]{1,0:T(8,128)(2,1)...) custom-call(bf16[16,1024]{1,0:T(8,128)(2,1)} %refs_0_.3, bf16[512,128]{1,0:T(8,128)(2,1)} %refs_1_.2, ...), custom_call_target="tpu_custom_call" | custom-call | tf_op jit(solution)/shard_map/prepare/pallas_call | solution.py:513
  13.7 0.0 collective-permute-done.2.refs_3_
  13.7 1.1 %collective-permute-done.1.refs_2_ = bf16[16,1024]{1,0:T(8,128)(2,1)S(1)} collective-permute-done((bf16[16,1024]{1,0:T(8,128)(2,1)}, bf16[16,1024]{1,0:T(8,128)(2,1)S(1)}, u32[]{:S(2)}, u32[]{:S(2)}) %collective-permute-start.1) | collective-permute-done | bytes 32800 | tf_op jit(solution)/shard_map/ppermute | solution.py:469
  14.9 4.6 %collective-permute-done.3.refs_5_ = bf16[512,128]{1,0:T(8,128)(2,1)S(1)} collective-permute-done((bf16[512,128]{1,0:T(8,128)(2,1)}, bf16[512,128]{1,0:T(8,128)(2,1)S(1)}, u32[]{:S(2)}, u32[]{:S(2)}) %collective-permute-start.3) | collective-permute-done | bytes 131104 | tf_op jit(solution)/shard_map/ppermute | solution.py:503
  19.5 2.0 %collective-permute-done.4.refs_7_ = bf16[512,128]{1,0:T(8,128)(2,1)S(1)} collective-permute-done((bf16[512,128]{1,0:T(8,128)(2,1)}, bf16[512,128]{1,0:T(8,128)(2,1)S(1)}, u32[]{:S(2)}, u32[]{:S(2)}) %collective-permute-start.4) | collective-permute-done | bytes 131104 | tf_op jit(solution)/shard_map/ppermute | solution.py:503
  21.5 1.6 %attend.1 = (bf16[64,384]{1,0:T(8,128)(2,1)S(1)}, bf16[64,384]{1,0:T(8,128)(2,1)S(1)}, bf16[64,384]{1,0:T(8,128)(2,1)S(1)}, bf16[64,384]{1,0:T(8,128)(2,1)S(1)}) custom-call(bf16[16,1024]{1,0:T(8,128)(2,1)S(1)} %get-tuple-element.31.refs_0_, bf16[16,1024]{1,0:T(8,128)(2,1)S(1)} %collective-permute-done.refs_1_, ...), custom_call_target="tpu_custom_call" | custom-call | tf_op jit(solution)/shard_map/attend/pallas_call | solution.py:531
  23.1 1.9 %collective-permute-start.5 = (bf16[64,384]{1,0:T(8,128)(2,1)S(1)}, bf16[64,384]{1,0:T(8,128)(2,1)S(1)}, u32[]{:S(2)}, u32[]{:S(2)}) collective-permute-start(bf16[64,384]{1,0:T(8,128)(2,1)S(1)} %get-tuple-element.37), channel_id=1, source_target_pairs={{0,4},{2,6},{4,0},{6,2},{8,12},{10,14},{12,8},{14,10},{1,5},{3,7},... | collective-permute-start | bytes 147464 | tf_op jit(solution)/shard_map/ppermute | solution.py:469
  25.0 2.6 %collective-permute-start.6 = (bf16[64,384]{1,0:T(8,128)(2,1)S(1)}, bf16[64,384]{1,0:T(8,128)(2,1)S(1)}, u32[]{:S(2)}, u32[]{:S(2)}) collective-permute-start(bf16[64,384]{1,0:T(8,128)(2,1)S(1)} %get-tuple-element.38), channel_id=1, source_target_pairs={{0,8},{2,10},{4,12},{6,14},{8,0},{10,2},{12,4},{14,6},{1,9},{3,11}... | collective-permute-start | bytes 147464 | tf_op jit(solution)/shard_map/ppermute | solution.py:469
  27.6 0.0 collective-permute-start.7
  27.6 3.4 %collective-permute-done.6.refs_2_ = bf16[64,384]{1,0:T(8,128)(2,1)S(1)} collective-permute-done((bf16[64,384]{1,0:T(8,128)(2,1)S(1)}, bf16[64,384]{1,0:T(8,128)(2,1)S(1)}, u32[]{:S(2)}, u32[]{:S(2)}) %collective-permute-start.6) | collective-permute-done | bytes 49184 | tf_op jit(solution)/shard_map/ppermute | solution.py:469
  31.0 2.4 %collective-permute-done.7.refs_3_ = bf16[64,384]{1,0:T(8,128)(2,1)S(1)} collective-permute-done((bf16[64,384]{1,0:T(8,128)(2,1)S(1)}, bf16[64,384]{1,0:T(8,128)(2,1)S(1)}, u32[]{:S(2)}, u32[]{:S(2)}) %collective-permute-start.7) | collective-permute-done | bytes 49184 | tf_op jit(solution)/shard_map/ppermute | solution.py:469
  33.4 0.6 project.1
  34.0 0.1 collective-permute-start.9
  34.1 1.3 %collective-permute-done.9.received = bf16[32,2048]{1,0:T(8,128)(2,1)S(1)} collective-permute-done((bf16[32,2048]{1,0:T(8,128)(2,1)S(1)}, bf16[32,2048]{1,0:T(8,128)(2,1)S(1)}, u32[]{:S(2)}, u32[]{:S(2)}) %collective-permute-start.9) | collective-permute-done | bytes 131104 | tf_op jit(solution)/shard_map/ppermute | solution.py:506
  35.5 0.1 collective-permute-start.10
  35.6 1.1 %collective-permute-start.11 = (bf16[16,2048]{1,0:T(8,128)(2,1)S(1)}, bf16[16,2048]{1,0:T(8,128)(2,1)S(1)}, u32[]{:S(2)}, u32[]{:S(2)}) collective-permute-start(bf16[16,2048]{1,0:T(8,128)(2,1)S(1)} %get-tuple-element.45), channel_id=1, source_target_pairs={{0,8},{2,10},{4,12},{6,14},{8,0},{10,2},{12,4},{14,6},{1,9},{3,11}... | collective-permute-start | bytes 196616 | tf_op jit(solution)/shard_map/ppermute | solution.py:469
  36.7 3.3 %collective-permute-start.12 = (bf16[16,2048]{1,0:T(8,128)(2,1)S(1)}, bf16[16,2048]{1,0:T(8,128)(2,1)S(1)}, u32[]{:S(2)}, u32[]{:S(2)}) collective-permute-start(bf16[16,2048]{1,0:T(8,128)(2,1)S(1)} %get-tuple-element.46), channel_id=1, source_target_pairs={{0,12},{2,14},{4,8},{6,10},{8,4},{10,6},{12,0},{14,2},{1,13},{3,15... | collective-permute-start | bytes 196616 | tf_op jit(solution)/shard_map/ppermute | solution.py:469
  40.0 0.8 %collective-permute-done.10.refs_1_ = bf16[16,2048]{1,0:T(8,128)(2,1)S(1)} collective-permute-done((bf16[16,2048]{1,0:T(8,128)(2,1)S(1)}, bf16[16,2048]{1,0:T(8,128)(2,1)S(1)}, u32[]{:S(2)}, u32[]{:S(2)}) %collective-permute-start.10) | collective-permute-done | bytes 65568 | tf_op jit(solution)/shard_map/ppermute | solution.py:469
  40.7 3.5 %collective-permute-done.11.refs_2_ = bf16[16,2048]{1,0:T(8,128)(2,1)S(1)} collective-permute-done((bf16[16,2048]{1,0:T(8,128)(2,1)S(1)}, bf16[16,2048]{1,0:T(8,128)(2,1)S(1)}, u32[]{:S(2)}, u32[]{:S(2)}) %collective-permute-start.11) | collective-permute-done | bytes 65568 | tf_op jit(solution)/shard_map/ppermute | solution.py:469
  44.2 0.7 norm.1
  44.8 2.2 %collective-permute-start.15 = (bf16[16,2176]{1,0:T(8,128)(2,1)S(1)}, bf16[16,2176]{1,0:T(8,128)(2,1)S(1)}, u32[]{:S(2)}, u32[]{:S(2)}) collective-permute-start(bf16[16,2176]{1,0:T(8,128)(2,1)S(1)} %get-tuple-element.49.refs_0_), channel_id=1, source_target_pairs={{0,6},{2,4},{4,2},{6,0},{8,14},{10,12},{12,10},{14,8},{1,7},{3,5},... | collective-permute-start | bytes 208904 | tf_op jit(solution)/shard_map/ppermute | solution.py:499
  47.1 0.8 %collective-permute-start.14 = (bf16[16,2176]{1,0:T(8,128)(2,1)S(1)}, bf16[16,2176]{1,0:T(8,128)(2,1)S(1)}, u32[]{:S(2)}, u32[]{:S(2)}) collective-permute-start(bf16[16,2176]{1,0:T(8,128)(2,1)S(1)} %get-tuple-element.49.refs_0_), channel_id=1, source_target_pairs={{0,4},{2,6},{4,0},{6,2},{8,12},{10,14},{12,8},{14,10},{1,5},{3,7},... | collective-permute-start | bytes 208904 | tf_op jit(solution)/shard_map/ppermute | solution.py:499
  47.8 0.5 collective-permute-start.13
  48.3 1.7 %collective-permute-done.15.refs_3_ = bf16[16,2176]{1,0:T(8,128)(2,1)S(1)} collective-permute-done((bf16[16,2176]{1,0:T(8,128)(2,1)S(1)}, bf16[16,2176]{1,0:T(8,128)(2,1)S(1)}, u32[]{:S(2)}, u32[]{:S(2)}) %collective-permute-start.15) | collective-permute-done | bytes 69664 | tf_op jit(solution)/shard_map/ppermute | solution.py:499
  50.1 1.3 %collective-permute-done.14.refs_2_ = bf16[16,2176]{1,0:T(8,128)(2,1)S(1)} collective-permute-done((bf16[16,2176]{1,0:T(8,128)(2,1)S(1)}, bf16[16,2176]{1,0:T(8,128)(2,1)S(1)}, u32[]{:S(2)}, u32[]{:S(2)}) %collective-permute-start.14) | collective-permute-done | bytes 69664 | tf_op jit(solution)/shard_map/ppermute | solution.py:499
  51.4 0.8 %collective-permute-done.13.refs_1_ = bf16[16,2176]{1,0:T(8,128)(2,1)S(1)} collective-permute-done((bf16[16,2176]{1,0:T(8,128)(2,1)S(1)}, bf16[16,2176]{1,0:T(8,128)(2,1)S(1)}, u32[]{:S(2)}, u32[]{:S(2)}) %collective-permute-start.13) | collective-permute-done | bytes 69664 | tf_op jit(solution)/shard_map/ppermute | solution.py:499
  52.1 1.9 %shard_map.123.refs_10_ = bf16[1,768,2048]{2,1,0:T(8,128)(2,1)S(1)} custom-call(bf16[1,768,2048]{2,1,0:T(8,128)(2,1)} %refs_0_.5), custom_call_target="tpu_custom_call" | custom-call | tf_op jit(solution)/shard_map/pallas_call | solution.py:476
  54.0 2.9 %shard_map.122 = (bf16[1,2048,768]{2,1,0:T(8,128)(2,1)S(1)}, bf16[1,2048,768]{2,1,0:T(8,128)(2,1)S(1)}) custom-call(bf16[1,2048,768]{2,1,0:T(8,128)(2,1)} %refs_0_.4, bf16[1,2048,768]{2,1,0:T(8,128)(2,1)} %refs_1_.3), custom_call_target="tpu_custom_call" | custom-call | tf_op jit(solution)/shard_map/pallas_call | solution.py:476
  57.0 1.5 %experts.1 = (bf16[64,2048]{1,0:T(8,128)(2,1)S(1)}, bf16[64,2048]{1,0:T(8,128)(2,1)S(1)}) custom-call(bf16[16,2176]{1,0:T(8,128)(2,1)S(1)} %get-tuple-element.49.refs_0_, bf16[16,2176]{1,0:T(8,128)(2,1)S(1)} %collective-permute-done.13.refs_1_, bf16[16,2176]{1,0:T(8,128)(2,1)S(1)} %collective-permute-done.14.refs_2_, ...), custom_call_target="tpu_custom_call" | custom-call | tf_op jit(solution)/shard_map/experts/pallas_call | solution.py:576
  58.5 0.6 collective-permute-start.20
  59.1 1.2 %collective-permute-done.20.received = bf16[64,2048]{1,0:T(8,128)(2,1)S(1)} collective-permute-done((bf16[64,2048]{1,0:T(8,128)(2,1)S(1)}, bf16[64,2048]{1,0:T(8,128)(2,1)S(1)}, u32[]{:S(2)}, u32[]{:S(2)}) %collective-permute-start.20) | collective-permute-done | bytes 262176 | tf_op jit(solution)/shard_map/ppermute | solution.py:506
  60.2 0.1 quarters.1
  60.3 0.6 collective-permute-start.21
  60.9 1.3 %collective-permute-start.22 = (bf16[16,2048]{1,0:T(8,128)(2,1)S(1)}, bf16[16,2048]{1,0:T(8,128)(2,1)S(1)}, u32[]{:S(2)}, u32[]{:S(2)}) collective-permute-start(bf16[16,2048]{1,0:T(8,128)(2,1)S(1)} %get-tuple-element.56), channel_id=1, source_target_pairs={{0,4},{2,6},{4,0},{6,2},{8,12},{10,14},{12,8},{14,10},{1,5},{3,7},... | collective-permute-start | bytes 196616 | tf_op jit(solution)/shard_map/ppermute | solution.py:499
  62.1 1.7 %collective-permute-start.23 = (bf16[16,2048]{1,0:T(8,128)(2,1)S(1)}, bf16[16,2048]{1,0:T(8,128)(2,1)S(1)}, u32[]{:S(2)}, u32[]{:S(2)}) collective-permute-start(bf16[16,2048]{1,0:T(8,128)(2,1)S(1)} %get-tuple-element.57), channel_id=1, source_target_pairs={{0,6},{2,4},{4,2},{6,0},{8,14},{10,12},{12,10},{14,8},{1,7},{3,5},... | collective-permute-start | bytes 196616 | tf_op jit(solution)/shard_map/ppermute | solution.py:499
  63.9 0.9 %collective-permute-done.21.refs_1_ = bf16[16,2048]{1,0:T(8,128)(2,1)S(1)} collective-permute-done((bf16[16,2048]{1,0:T(8,128)(2,1)S(1)}, bf16[16,2048]{1,0:T(8,128)(2,1)S(1)}, u32[]{:S(2)}, u32[]{:S(2)}) %collective-permute-start.21) | collective-permute-done | bytes 65568 | tf_op jit(solution)/shard_map/ppermute | solution.py:499
  64.7 0.4 collective-permute-done.22.refs_2_
  65.1 2.4 %collective-permute-done.23.refs_3_ = bf16[16,2048]{1,0:T(8,128)(2,1)S(1)} collective-permute-done((bf16[16,2048]{1,0:T(8,128)(2,1)S(1)}, bf16[16,2048]{1,0:T(8,128)(2,1)S(1)}, u32[]{:S(2)}, u32[]{:S(2)}) %collective-permute-start.23) | collective-permute-done | bytes 65568 | tf_op jit(solution)/shard_map/ppermute | solution.py:499
  67.5 1.2 %collective-permute-start.24 = (bf16[8,2048]{1,0:T(8,128)(2,1)S(1)}, bf16[8,2048]{1,0:T(8,128)(2,1)S(1)}, u32[]{:S(2)}, u32[]{:S(2)}) collective-permute-start(bf16[8,2048]{1,0:T(8,128)(2,1)S(1)} %get-tuple-element.59), channel_id=1, source_target_pairs={{0,8},{2,10},{4,12},{6,14},{8,0},{10,2},{12,4},{14,6},{1,9},{3,11}... | collective-permute-start | bytes 98312 | tf_op jit(solution)/shard_map/ppermute | solution.py:608
  68.8 3.6 %collective-permute-done.24.refs_1_ = bf16[8,2048]{1,0:T(8,128)(2,1)S(1)} collective-permute-done((bf16[8,2048]{1,0:T(8,128)(2,1)S(1)}, bf16[8,2048]{1,0:T(8,128)(2,1)S(1)}, u32[]{:S(2)}, u32[]{:S(2)}) %collective-permute-start.24) | collective-permute-done | bytes 32800 | tf_op jit(solution)/shard_map/ppermute | solution.py:608
  72.4 0.6 added.1
  (16 shorter events, 0.1 us)
Async XLA Ops:
  0.6 39.3 %copy-start = (bf16[2048]{0:T(1024)(128)(2,1)S(1)}, bf16[2048]{0:T(1024)(128)(2,1)}, u32[]{:S(2)}) copy-start(bf16[2048]{0:T(1024)(128)(2,1)} %param.16) | copy-start | bytes 12292
  0.6 32.8 %collective-permute-start.8 = (bf16[128,2048]{1,0:T(8,128)(2,1)}, bf16[128,2048]{1,0:T(8,128)(2,1)S(1)}, u32[]{:S(2)}, u32[]{:S(2)}) collective-permute-start(bf16[128,2048]{1,0:T(8,128)(2,1)} %refs_3_.1), channel_id=1, source_target_pairs={{0,2},{2,0},{4,6},{6,4},{8,10},{10,8},{12,14},{14,12},{1,3},{3,1},... | collective-permute-start | bytes 1572872 | tf_op jit(solution)/shard_map/ppermute | solution.py:503
  3.7 15.8 %collective-permute-start.3 = (bf16[512,128]{1,0:T(8,128)(2,1)}, bf16[512,128]{1,0:T(8,128)(2,1)S(1)}, u32[]{:S(2)}, u32[]{:S(2)}) collective-permute-start(bf16[512,128]{1,0:T(8,128)(2,1)} %refs_1_.2), channel_id=1, source_target_pairs={{0,2},{2,0},{4,6},{6,4},{8,10},{10,8},{12,14},{14,12},{1,3},{3,1},... | collective-permute-start | bytes 393224 | tf_op jit(solution)/shard_map/ppermute | solution.py:503
  3.8 17.7 %collective-permute-start.4 = (bf16[512,128]{1,0:T(8,128)(2,1)}, bf16[512,128]{1,0:T(8,128)(2,1)S(1)}, u32[]{:S(2)}, u32[]{:S(2)}) collective-permute-start(bf16[512,128]{1,0:T(8,128)(2,1)} %refs_2_.1), channel_id=1, source_target_pairs={{0,2},{2,0},{4,6},{6,4},{8,10},{10,8},{12,14},{14,12},{1,3},{3,1},... | collective-permute-start | bytes 393224 | tf_op jit(solution)/shard_map/ppermute | solution.py:503
  5.7 4.1 %collective-permute-start = (bf16[16,1024]{1,0:T(8,128)(2,1)}, bf16[16,1024]{1,0:T(8,128)(2,1)S(1)}, u32[]{:S(2)}, u32[]{:S(2)}) collective-permute-start(bf16[16,1024]{1,0:T(8,128)(2,1)} %refs_0_.3), channel_id=1, source_target_pairs={{0,4},{2,6},{4,0},{6,2},{8,12},{10,14},{12,8},{14,10},{1,5},{3,7},... | collective-permute-start | bytes 98312 | tf_op jit(solution)/shard_map/ppermute | solution.py:469
  7.3 6.4 %collective-permute-start.2 = (bf16[16,1024]{1,0:T(8,128)(2,1)}, bf16[16,1024]{1,0:T(8,128)(2,1)S(1)}, u32[]{:S(2)}, u32[]{:S(2)}) collective-permute-start(bf16[16,1024]{1,0:T(8,128)(2,1)} %refs_0_.3), channel_id=1, source_target_pairs={{0,12},{2,14},{4,8},{6,10},{8,4},{10,6},{12,0},{14,2},{1,13},{3,15... | collective-permute-start | bytes 98312 | tf_op jit(solution)/shard_map/ppermute | solution.py:469
  9.9 5.0 %collective-permute-start.1 = (bf16[16,1024]{1,0:T(8,128)(2,1)}, bf16[16,1024]{1,0:T(8,128)(2,1)S(1)}, u32[]{:S(2)}, u32[]{:S(2)}) collective-permute-start(bf16[16,1024]{1,0:T(8,128)(2,1)} %refs_0_.3), channel_id=1, source_target_pairs={{0,8},{2,10},{4,12},{6,14},{8,0},{10,2},{12,4},{14,6},{1,9},{3,11}... | collective-permute-start | bytes 98312 | tf_op jit(solution)/shard_map/ppermute | solution.py:469
  23.1 4.5 %collective-permute-start.5 = (bf16[64,384]{1,0:T(8,128)(2,1)S(1)}, bf16[64,384]{1,0:T(8,128)(2,1)S(1)}, u32[]{:S(2)}, u32[]{:S(2)}) collective-permute-start(bf16[64,384]{1,0:T(8,128)(2,1)S(1)} %get-tuple-element.37), channel_id=1, source_target_pairs={{0,4},{2,6},{4,0},{6,2},{8,12},{10,14},{12,8},{14,10},{1,5},{3,7},... | collective-permute-start | bytes 147464 | tf_op jit(solution)/shard_map/ppermute | solution.py:469
  25.0 6.0 %collective-permute-start.6 = (bf16[64,384]{1,0:T(8,128)(2,1)S(1)}, bf16[64,384]{1,0:T(8,128)(2,1)S(1)}, u32[]{:S(2)}, u32[]{:S(2)}) collective-permute-start(bf16[64,384]{1,0:T(8,128)(2,1)S(1)} %get-tuple-element.38), channel_id=1, source_target_pairs={{0,8},{2,10},{4,12},{6,14},{8,0},{10,2},{12,4},{14,6},{1,9},{3,11}... | collective-permute-start | bytes 147464 | tf_op jit(solution)/shard_map/ppermute | solution.py:469
  27.6 5.9 %collective-permute-start.7 = (bf16[64,384]{1,0:T(8,128)(2,1)S(1)}, bf16[64,384]{1,0:T(8,128)(2,1)S(1)}, u32[]{:S(2)}, u32[]{:S(2)}) collective-permute-start(bf16[64,384]{1,0:T(8,128)(2,1)S(1)} %get-tuple-element.39), channel_id=1, source_target_pairs={{0,12},{2,14},{4,8},{6,10},{8,4},{10,6},{12,0},{14,2},{1,13},{3,15... | collective-permute-start | bytes 147464 | tf_op jit(solution)/shard_map/ppermute | solution.py:469
  34.0 1.4 %collective-permute-start.9 = (bf16[32,2048]{1,0:T(8,128)(2,1)S(1)}, bf16[32,2048]{1,0:T(8,128)(2,1)S(1)}, u32[]{:S(2)}, u32[]{:S(2)}) collective-permute-start(bf16[32,2048]{1,0:T(8,128)(2,1)S(1)} %get-tuple-element.42), channel_id=1, source_target_pairs={{0,1},{1,0},{2,3},{3,2},{4,5},{5,4},{6,7},{7,6},{8,9},{9,8},{10,11... | collective-permute-start | bytes 393224 | tf_op jit(solution)/shard_map/ppermute | solution.py:506
  35.5 5.2 %collective-permute-start.10 = (bf16[16,2048]{1,0:T(8,128)(2,1)S(1)}, bf16[16,2048]{1,0:T(8,128)(2,1)S(1)}, u32[]{:S(2)}, u32[]{:S(2)}) collective-permute-start(bf16[16,2048]{1,0:T(8,128)(2,1)S(1)} %get-tuple-element.44), channel_id=1, source_target_pairs={{0,4},{2,6},{4,0},{6,2},{8,12},{10,14},{12,8},{14,10},{1,5},{3,7},... | collective-permute-start | bytes 196616 | tf_op jit(solution)/shard_map/ppermute | solution.py:469
  35.6 8.6 %collective-permute-start.11 = (bf16[16,2048]{1,0:T(8,128)(2,1)S(1)}, bf16[16,2048]{1,0:T(8,128)(2,1)S(1)}, u32[]{:S(2)}, u32[]{:S(2)}) collective-permute-start(bf16[16,2048]{1,0:T(8,128)(2,1)S(1)} %get-tuple-element.45), channel_id=1, source_target_pairs={{0,8},{2,10},{4,12},{6,14},{8,0},{10,2},{12,4},{14,6},{1,9},{3,11}... | collective-permute-start | bytes 196616 | tf_op jit(solution)/shard_map/ppermute | solution.py:469
  36.7 7.5 %collective-permute-start.12 = (bf16[16,2048]{1,0:T(8,128)(2,1)S(1)}, bf16[16,2048]{1,0:T(8,128)(2,1)S(1)}, u32[]{:S(2)}, u32[]{:S(2)}) collective-permute-start(bf16[16,2048]{1,0:T(8,128)(2,1)S(1)} %get-tuple-element.46), channel_id=1, source_target_pairs={{0,12},{2,14},{4,8},{6,10},{8,4},{10,6},{12,0},{14,2},{1,13},{3,15... | collective-permute-start | bytes 196616 | tf_op jit(solution)/shard_map/ppermute | solution.py:469
  44.8 5.2 %collective-permute-start.15 = (bf16[16,2176]{1,0:T(8,128)(2,1)S(1)}, bf16[16,2176]{1,0:T(8,128)(2,1)S(1)}, u32[]{:S(2)}, u32[]{:S(2)}) collective-permute-start(bf16[16,2176]{1,0:T(8,128)(2,1)S(1)} %get-tuple-element.49.refs_0_), channel_id=1, source_target_pairs={{0,6},{2,4},{4,2},{6,0},{8,14},{10,12},{12,10},{14,8},{1,7},{3,5},... | collective-permute-start | bytes 208904 | tf_op jit(solution)/shard_map/ppermute | solution.py:499
  47.1 4.3 %collective-permute-start.14 = (bf16[16,2176]{1,0:T(8,128)(2,1)S(1)}, bf16[16,2176]{1,0:T(8,128)(2,1)S(1)}, u32[]{:S(2)}, u32[]{:S(2)}) collective-permute-start(bf16[16,2176]{1,0:T(8,128)(2,1)S(1)} %get-tuple-element.49.refs_0_), channel_id=1, source_target_pairs={{0,4},{2,6},{4,0},{6,2},{8,12},{10,14},{12,8},{14,10},{1,5},{3,7},... | collective-permute-start | bytes 208904 | tf_op jit(solution)/shard_map/ppermute | solution.py:499
  47.8 4.3 %collective-permute-start.13 = (bf16[16,2176]{1,0:T(8,128)(2,1)S(1)}, bf16[16,2176]{1,0:T(8,128)(2,1)S(1)}, u32[]{:S(2)}, u32[]{:S(2)}) collective-permute-start(bf16[16,2176]{1,0:T(8,128)(2,1)S(1)} %get-tuple-element.49.refs_0_), channel_id=1, source_target_pairs={{0,2},{2,0},{4,6},{6,4},{8,10},{10,8},{12,14},{14,12},{1,3},{3,1},... | collective-permute-start | bytes 208904 | tf_op jit(solution)/shard_map/ppermute | solution.py:499
  48.3 8.6 %collective-permute-start.16 = (bf16[16,2176]{1,0:T(8,128)(2,1)S(1)}, bf16[16,2176]{1,0:T(8,128)(2,1)S(1)}, u32[]{:S(2)}, u32[]{:S(2)}) collective-permute-start(bf16[16,2176]{1,0:T(8,128)(2,1)S(1)} %get-tuple-element.49.refs_0_), channel_id=1, source_target_pairs={{0,1},{1,0},{2,3},{3,2},{4,5},{5,4},{6,7},{7,6},{8,9},{9,8},{10,11... | collective-permute-start | bytes 208904 | tf_op jit(solution)/shard_map/ppermute | solution.py:506
  50.1 6.9 %collective-permute-start.19 = (bf16[16,2176]{1,0:T(8,128)(2,1)S(1)}, bf16[16,2176]{1,0:T(8,128)(2,1)S(1)}, u32[]{:S(2)}, u32[]{:S(2)}) collective-permute-start(bf16[16,2176]{1,0:T(8,128)(2,1)S(1)} %collective-permute-done.15.refs_3_), channel_id=1, source_target_pairs={{0,1},{1,0},{2,3},{3,2},{4,5},{5,4},{6,7},{7,6},{8,9},{9,8},{10,11... | collective-permute-start | bytes 208904 | tf_op jit(solution)/shard_map/ppermute | solution.py:506
  51.4 5.6 %collective-permute-start.18 = (bf16[16,2176]{1,0:T(8,128)(2,1)S(1)}, bf16[16,2176]{1,0:T(8,128)(2,1)S(1)}, u32[]{:S(2)}, u32[]{:S(2)}) collective-permute-start(bf16[16,2176]{1,0:T(8,128)(2,1)S(1)} %collective-permute-done.14.refs_2_), channel_id=1, source_target_pairs={{0,1},{1,0},{2,3},{3,2},{4,5},{5,4},{6,7},{7,6},{8,9},{9,8},{10,11... | collective-permute-start | bytes 208904 | tf_op jit(solution)/shard_map/ppermute | solution.py:506
  52.1 4.8 %collective-permute-start.17 = (bf16[16,2176]{1,0:T(8,128)(2,1)S(1)}, bf16[16,2176]{1,0:T(8,128)(2,1)S(1)}, u32[]{:S(2)}, u32[]{:S(2)}) collective-permute-start(bf16[16,2176]{1,0:T(8,128)(2,1)S(1)} %collective-permute-done.13.refs_1_), channel_id=1, source_target_pairs={{0,1},{1,0},{2,3},{3,2},{4,5},{5,4},{6,7},{7,6},{8,9},{9,8},{10,11... | collective-permute-start | bytes 208904 | tf_op jit(solution)/shard_map/ppermute | solution.py:506
  58.5 1.7 %collective-permute-start.20 = (bf16[64,2048]{1,0:T(8,128)(2,1)S(1)}, bf16[64,2048]{1,0:T(8,128)(2,1)S(1)}, u32[]{:S(2)}, u32[]{:S(2)}) collective-permute-start(bf16[64,2048]{1,0:T(8,128)(2,1)S(1)} %get-tuple-element.53), channel_id=1, source_target_pairs={{0,1},{1,0},{2,3},{3,2},{4,5},{5,4},{6,7},{7,6},{8,9},{9,8},{10,11... | collective-permute-start | bytes 786440 | tf_op jit(solution)/shard_map/ppermute | solution.py:506
  60.3 4.4 %collective-permute-start.21 = (bf16[16,2048]{1,0:T(8,128)(2,1)S(1)}, bf16[16,2048]{1,0:T(8,128)(2,1)S(1)}, u32[]{:S(2)}, u32[]{:S(2)}) collective-permute-start(bf16[16,2048]{1,0:T(8,128)(2,1)S(1)} %get-tuple-element.55), channel_id=1, source_target_pairs={{0,2},{2,0},{4,6},{6,4},{8,10},{10,8},{12,14},{14,12},{1,3},{3,1},... | collective-permute-start | bytes 196616 | tf_op jit(solution)/shard_map/ppermute | solution.py:499
  60.9 4.3 %collective-permute-start.22 = (bf16[16,2048]{1,0:T(8,128)(2,1)S(1)}, bf16[16,2048]{1,0:T(8,128)(2,1)S(1)}, u32[]{:S(2)}, u32[]{:S(2)}) collective-permute-start(bf16[16,2048]{1,0:T(8,128)(2,1)S(1)} %get-tuple-element.56), channel_id=1, source_target_pairs={{0,4},{2,6},{4,0},{6,2},{8,12},{10,14},{12,8},{14,10},{1,5},{3,7},... | collective-permute-start | bytes 196616 | tf_op jit(solution)/shard_map/ppermute | solution.py:499
  62.1 5.4 %collective-permute-start.23 = (bf16[16,2048]{1,0:T(8,128)(2,1)S(1)}, bf16[16,2048]{1,0:T(8,128)(2,1)S(1)}, u32[]{:S(2)}, u32[]{:S(2)}) collective-permute-start(bf16[16,2048]{1,0:T(8,128)(2,1)S(1)} %get-tuple-element.57), channel_id=1, source_target_pairs={{0,6},{2,4},{4,2},{6,0},{8,14},{10,12},{12,10},{14,8},{1,7},{3,5},... | collective-permute-start | bytes 196616 | tf_op jit(solution)/shard_map/ppermute | solution.py:499
  67.5 4.9 %collective-permute-start.24 = (bf16[8,2048]{1,0:T(8,128)(2,1)S(1)}, bf16[8,2048]{1,0:T(8,128)(2,1)S(1)}, u32[]{:S(2)}, u32[]{:S(2)}) collective-permute-start(bf16[8,2048]{1,0:T(8,128)(2,1)S(1)} %get-tuple-element.59), channel_id=1, source_target_pairs={{0,8},{2,10},{4,12},{6,14},{8,0},{10,2},{12,4},{14,6},{1,9},{3,11}... | collective-permute-start | bytes 98312 | tf_op jit(solution)/shard_map/ppermute | solution.py:608

commit v4 on v3

--- a/solution.py
+++ b/solution.py
@@ -464,10 +464,10 @@
     shape_of = jax.ShapeDtypeStruct
 
     def over_far(arrays):
-        moved = []
-        for step in range(far_count - 1, 0, -1):
+        moved = [arrays[0]]
+        for step in range(1, far_count):
             moved.append(lax.ppermute(arrays[step], "blk", far_of(step, blk)))
-        return [arrays[0]] + moved[::-1]
+        return moved
 
     def in_hbm(arrays):
         return [pltpu.with_memory_space_constraint(a, pltpu.HBM) for a in arrays]
@@ -493,11 +493,11 @@
         )(*terms)
 
     def over_close(arrays):
-        moved = []
-        for at, step in ((3, 3), (1, 1), (2, 2)):
+        moved = [arrays[0]]
+        for step in range(1, 4):
             pairs = [(source, source ^ step) for source in range(blk)]
-            moved.append(lax.ppermute(arrays[at], "blk", pairs))
-        return [arrays[0], moved[1], moved[2], moved[0]]
+            moved.append(lax.ppermute(arrays[step], "blk", pairs))
+        return moved
 
     def over_near(array):
         return lax.ppermute(array, "blk", side_of(blk))
@@ -565,13 +565,21 @@
     gate_weight, up_weight = fetched(gate_weight, up_weight)
     attn_proj, normed = pl.pallas_call(
         functools.partial(norm_kernel, far_count),
-        out_shape=[shape_of((own_tokens, width), bf16), shape_of((shared, width + HD), bf16)],
+        out_shape=[pltpu.VMEM((own_tokens, width), bf16), shape_of((shared, width + HD), bf16)],
         in_specs=in_vmem(far_count + 2),
         out_specs=in_vmem(2),
         compiler_params=grant(4),
         name="norm",
     )(*parts, norm_gain.reshape(1, width), routes)
     pieces = over_close([normed] * 4)
+    attn_proj = pl.pallas_call(
+        add_kernel,
+        out_shape=shape_of((own_tokens, width), bf16),
+        in_specs=in_vmem(1),
+        out_specs=pl.BlockSpec(memory_space=pltpu.VMEM),
+        compiler_params=grant(4),
+        name="emit",
+    )(attn_proj)
     pieces = pieces + [over_rows(piece) for piece in pieces]
     keep, send = pl.pallas_call(
         functools.partial(expert_kernel, width, len(pieces)),

time: 73.2 us -> 72.8 us (level)
  no operation moved by 1% of the time
where the time goes in v4:
time: 72.8 us; the launch traced here: 72.6 us
  waiting for transfers between devices  30.9 us (42%)
  starting transfers between devices  29.6 us (41%)
  Pallas kernels  11.3 us (16%)
  between operations  0.78 us (1%)
    ppermute x9, starting transfers between devices, over_far(): moved.append(lax.ppermute(arrays[step], 'blk', far_of(step, blk)))  15.5 us
    ppermute x9, waiting for transfers between devices, over_far(): moved.append(lax.ppermute(arrays[step], 'blk', far_of(step, blk)))  11.3 us
    ppermute x6, waiting for transfers between devices, over_close(): moved.append(lax.ppermute(arrays[step], 'blk', pairs))  7.44 us
    ppermute x6, starting transfers between devices, over_close(): moved.append(lax.ppermute(arrays[step], 'blk', pairs))  7.11 us
    ppermute x3, waiting for transfers between devices, over_near(): return lax.ppermute(array, 'blk', side_of(blk))  6.58 us
    ppermute x3, starting transfers between devices, over_near(): return lax.ppermute(array, 'blk', side_of(blk))  5.09 us
    pallas_call x2, Pallas kernels, fetched(): pl.pallas_call(fetch_kernel, out_shape=[shape_of(a.shape, a.dtype) for a...  4.76 us
    ppermute x1, waiting for transfers between devices, paired_device(): lax.ppermute(term, 'blk', far_of(step, blk))  3.01 us
  transfers between devices with their start and end apart: 25, of which 17 were waited for; matrix products, arithmetic and copies ran while one was open for 0% of the time, Pallas kernels for 11%

profile of v4, /device:TPU:0, one launch (start us, length us, event | category | flops | bytes accessed | tf_op | source)
XLA Modules:
  0.0 72.6 jit_solution(808088084141101820)
XLA Ops:
  0.6 3.1 %collective-permute-start.8 = (bf16[128,2048]{1,0:T(8,128)(2,1)}, bf16[128,2048]{1,0:T(8,128)(2,1)S(1)}, u32[]{:S(2)}, u32[]{:S(2)}) collective-permute-start(bf16[128,2048]{1,0:T(8,128)(2,1)} %refs_3_.1), channel_id=1, source_target_pairs={{0,2},{2,0},{4,6},{6,4},{8,10},{10,8},{12,14},{14,12},{1,3},{3,1},... | collective-permute-start | bytes 1572872 | tf_op jit(solution)/shard_map/ppermute | solution.py:503
  3.7 0.1 collective-permute-start.3
  3.8 1.9 %collective-permute-start.4 = (bf16[512,128]{1,0:T(8,128)(2,1)}, bf16[512,128]{1,0:T(8,128)(2,1)S(1)}, u32[]{:S(2)}, u32[]{:S(2)}) collective-permute-start(bf16[512,128]{1,0:T(8,128)(2,1)} %refs_2_.1), channel_id=1, source_target_pairs={{0,2},{2,0},{4,6},{6,4},{8,10},{10,8},{12,14},{14,12},{1,3},{3,1},... | collective-permute-start | bytes 393224 | tf_op jit(solution)/shard_map/ppermute | solution.py:503
  5.7 1.6 %collective-permute-start = (bf16[16,1024]{1,0:T(8,128)(2,1)}, bf16[16,1024]{1,0:T(8,128)(2,1)S(1)}, u32[]{:S(2)}, u32[]{:S(2)}) collective-permute-start(bf16[16,1024]{1,0:T(8,128)(2,1)} %refs_0_.3), channel_id=1, source_target_pairs={{0,4},{2,6},{4,0},{6,2},{8,12},{10,14},{12,8},{14,10},{1,5},{3,7},... | collective-permute-start | bytes 98312 | tf_op jit(solution)/shard_map/ppermute | solution.py:469
  7.3 2.5 %collective-permute-start.2 = (bf16[16,1024]{1,0:T(8,128)(2,1)}, bf16[16,1024]{1,0:T(8,128)(2,1)S(1)}, u32[]{:S(2)}, u32[]{:S(2)}) collective-permute-start(bf16[16,1024]{1,0:T(8,128)(2,1)} %refs_0_.3), channel_id=1, source_target_pairs={{0,12},{2,14},{4,8},{6,10},{8,4},{10,6},{12,0},{14,2},{1,13},{3,15... | collective-permute-start | bytes 98312 | tf_op jit(solution)/shard_map/ppermute | solution.py:469
  9.8 0.1 collective-permute-done.refs_1_
  9.9 2.6 %collective-permute-start.1 = (bf16[16,1024]{1,0:T(8,128)(2,1)}, bf16[16,1024]{1,0:T(8,128)(2,1)S(1)}, u32[]{:S(2)}, u32[]{:S(2)}) collective-permute-start(bf16[16,1024]{1,0:T(8,128)(2,1)} %refs_0_.3), channel_id=1, source_target_pairs={{0,8},{2,10},{4,12},{6,14},{8,0},{10,2},{12,4},{14,6},{1,9},{3,11}... | collective-permute-start | bytes 98312 | tf_op jit(solution)/shard_map/ppermute | solution.py:469
  12.4 1.3 %prepare.1 = (bf16[16,1024]{1,0:T(8,128)(2,1)S(1)}, bf16[512,128]{1,0:T(8,128)(2,1)S(1)}, bf16[512,128]{1,0:T(8,128)(2,1)S(1)}, bf16[128,2048]{1,0:T(8,128)(2,1)...) custom-call(bf16[16,1024]{1,0:T(8,128)(2,1)} %refs_0_.3, bf16[512,128]{1,0:T(8,128)(2,1)} %refs_1_.2, ...), custom_call_target="tpu_custom_call" | custom-call | tf_op jit(solution)/shard_map/prepare/pallas_call | solution.py:513
  13.7 1.1 %collective-permute-done.1.refs_2_ = bf16[16,1024]{1,0:T(8,128)(2,1)S(1)} collective-permute-done((bf16[16,1024]{1,0:T(8,128)(2,1)}, bf16[16,1024]{1,0:T(8,128)(2,1)S(1)}, u32[]{:S(2)}, u32[]{:S(2)}) %collective-permute-start.1) | collective-permute-done | bytes 32800 | tf_op jit(solution)/shard_map/ppermute | solution.py:469
  14.9 4.6 %collective-permute-done.3.refs_5_ = bf16[512,128]{1,0:T(8,128)(2,1)S(1)} collective-permute-done((bf16[512,128]{1,0:T(8,128)(2,1)}, bf16[512,128]{1,0:T(8,128)(2,1)S(1)}, u32[]{:S(2)}, u32[]{:S(2)}) %collective-permute-start.3) | collective-permute-done | bytes 131104 | tf_op jit(solution)/shard_map/ppermute | solution.py:503
  19.5 2.0 %collective-permute-done.4.refs_7_ = bf16[512,128]{1,0:T(8,128)(2,1)S(1)} collective-permute-done((bf16[512,128]{1,0:T(8,128)(2,1)}, bf16[512,128]{1,0:T(8,128)(2,1)S(1)}, u32[]{:S(2)}, u32[]{:S(2)}) %collective-permute-start.4) | collective-permute-done | bytes 131104 | tf_op jit(solution)/shard_map/ppermute | solution.py:503
  21.5 1.6 %attend.1 = (bf16[64,384]{1,0:T(8,128)(2,1)S(1)}, bf16[64,384]{1,0:T(8,128)(2,1)S(1)}, bf16[64,384]{1,0:T(8,128)(2,1)S(1)}, bf16[64,384]{1,0:T(8,128)(2,1)S(1)}) custom-call(bf16[16,1024]{1,0:T(8,128)(2,1)S(1)} %get-tuple-element.31.refs_0_, bf16[16,1024]{1,0:T(8,128)(2,1)S(1)} %collective-permute-done.refs_1_, ...), custom_call_target="tpu_custom_call" | custom-call | tf_op jit(solution)/shard_map/attend/pallas_call | solution.py:531
  23.1 1.9 %collective-permute-start.5 = (bf16[64,384]{1,0:T(8,128)(2,1)S(1)}, bf16[64,384]{1,0:T(8,128)(2,1)S(1)}, u32[]{:S(2)}, u32[]{:S(2)}) collective-permute-start(bf16[64,384]{1,0:T(8,128)(2,1)S(1)} %get-tuple-element.37), channel_id=1, source_target_pairs={{0,4},{2,6},{4,0},{6,2},{8,12},{10,14},{12,8},{14,10},{1,5},{3,7},... | collective-permute-start | bytes 147464 | tf_op jit(solution)/shard_map/ppermute | solution.py:469
  25.0 2.6 %collective-permute-start.6 = (bf16[64,384]{1,0:T(8,128)(2,1)S(1)}, bf16[64,384]{1,0:T(8,128)(2,1)S(1)}, u32[]{:S(2)}, u32[]{:S(2)}) collective-permute-start(bf16[64,384]{1,0:T(8,128)(2,1)S(1)} %get-tuple-element.38), channel_id=1, source_target_pairs={{0,8},{2,10},{4,12},{6,14},{8,0},{10,2},{12,4},{14,6},{1,9},{3,11}... | collective-permute-start | bytes 147464 | tf_op jit(solution)/shard_map/ppermute | solution.py:469
  27.6 0.0 collective-permute-start.7
  27.6 3.4 %collective-permute-done.6.refs_2_ = bf16[64,384]{1,0:T(8,128)(2,1)S(1)} collective-permute-done((bf16[64,384]{1,0:T(8,128)(2,1)S(1)}, bf16[64,384]{1,0:T(8,128)(2,1)S(1)}, u32[]{:S(2)}, u32[]{:S(2)}) %collective-permute-start.6) | collective-permute-done | bytes 49184 | tf_op jit(solution)/shard_map/ppermute | solution.py:469
  31.0 2.4 %collective-permute-done.7.refs_3_ = bf16[64,384]{1,0:T(8,128)(2,1)S(1)} collective-permute-done((bf16[64,384]{1,0:T(8,128)(2,1)S(1)}, bf16[64,384]{1,0:T(8,128)(2,1)S(1)}, u32[]{:S(2)}, u32[]{:S(2)}) %collective-permute-start.7) | collective-permute-done | bytes 49184 | tf_op jit(solution)/shard_map/ppermute | solution.py:469
  33.4 0.6 project.1
  34.0 0.1 collective-permute-start.9
  34.1 1.3 %collective-permute-done.9.received = bf16[32,2048]{1,0:T(8,128)(2,1)S(1)} collective-permute-done((bf16[32,2048]{1,0:T(8,128)(2,1)S(1)}, bf16[32,2048]{1,0:T(8,128)(2,1)S(1)}, u32[]{:S(2)}, u32[]{:S(2)}) %collective-permute-start.9) | collective-permute-done | bytes 131104 | tf_op jit(solution)/shard_map/ppermute | solution.py:506
  35.5 0.1 collective-permute-start.10
  35.6 1.1 %collective-permute-start.11 = (bf16[16,2048]{1,0:T(8,128)(2,1)S(1)}, bf16[16,2048]{1,0:T(8,128)(2,1)S(1)}, u32[]{:S(2)}, u32[]{:S(2)}) collective-permute-start(bf16[16,2048]{1,0:T(8,128)(2,1)S(1)} %get-tuple-element.45), channel_id=1, source_target_pairs={{0,8},{2,10},{4,12},{6,14},{8,0},{10,2},{12,4},{14,6},{1,9},{3,11}... | collective-permute-start | bytes 196616 | tf_op jit(solution)/shard_map/ppermute | solution.py:469
  36.7 3.3 %collective-permute-start.12 = (bf16[16,2048]{1,0:T(8,128)(2,1)S(1)}, bf16[16,2048]{1,0:T(8,128)(2,1)S(1)}, u32[]{:S(2)}, u32[]{:S(2)}) collective-permute-start(bf16[16,2048]{1,0:T(8,128)(2,1)S(1)} %get-tuple-element.46), channel_id=1, source_target_pairs={{0,12},{2,14},{4,8},{6,10},{8,4},{10,6},{12,0},{14,2},{1,13},{3,15... | collective-permute-start | bytes 196616 | tf_op jit(solution)/shard_map/ppermute | solution.py:469
  40.0 0.8 %collective-permute-done.10.refs_1_ = bf16[16,2048]{1,0:T(8,128)(2,1)S(1)} collective-permute-done((bf16[16,2048]{1,0:T(8,128)(2,1)S(1)}, bf16[16,2048]{1,0:T(8,128)(2,1)S(1)}, u32[]{:S(2)}, u32[]{:S(2)}) %collective-permute-start.10) | collective-permute-done | bytes 65568 | tf_op jit(solution)/shard_map/ppermute | solution.py:469
  40.7 3.5 %collective-permute-done.11.refs_2_ = bf16[16,2048]{1,0:T(8,128)(2,1)S(1)} collective-permute-done((bf16[16,2048]{1,0:T(8,128)(2,1)S(1)}, bf16[16,2048]{1,0:T(8,128)(2,1)S(1)}, u32[]{:S(2)}, u32[]{:S(2)}) %collective-permute-start.11) | collective-permute-done | bytes 65568 | tf_op jit(solution)/shard_map/ppermute | solution.py:469
  44.2 0.1 norm.1
  44.3 2.3 %collective-permute-start.15 = (bf16[16,2176]{1,0:T(8,128)(2,1)S(1)}, bf16[16,2176]{1,0:T(8,128)(2,1)S(1)}, u32[]{:S(2)}, u32[]{:S(2)}) collective-permute-start(bf16[16,2176]{1,0:T(8,128)(2,1)S(1)} %get-tuple-element.49.refs_0_), channel_id=1, source_target_pairs={{0,6},{2,4},{4,2},{6,0},{8,14},{10,12},{12,10},{14,8},{1,7},{3,5},... | collective-permute-start | bytes 208904 | tf_op jit(solution)/shard_map/ppermute | solution.py:499
  46.6 0.8 %collective-permute-start.14 = (bf16[16,2176]{1,0:T(8,128)(2,1)S(1)}, bf16[16,2176]{1,0:T(8,128)(2,1)S(1)}, u32[]{:S(2)}, u32[]{:S(2)}) collective-permute-start(bf16[16,2176]{1,0:T(8,128)(2,1)S(1)} %get-tuple-element.49.refs_0_), channel_id=1, source_target_pairs={{0,4},{2,6},{4,0},{6,2},{8,12},{10,14},{12,8},{14,10},{1,5},{3,7},... | collective-permute-start | bytes 208904 | tf_op jit(solution)/shard_map/ppermute | solution.py:499
  47.4 0.5 collective-permute-start.13
  47.9 1.7 %collective-permute-done.15.refs_3_ = bf16[16,2176]{1,0:T(8,128)(2,1)S(1)} collective-permute-done((bf16[16,2176]{1,0:T(8,128)(2,1)S(1)}, bf16[16,2176]{1,0:T(8,128)(2,1)S(1)}, u32[]{:S(2)}, u32[]{:S(2)}) %collective-permute-start.15) | collective-permute-done | bytes 69664 | tf_op jit(solution)/shard_map/ppermute | solution.py:499
  49.6 1.3 %collective-permute-done.14.refs_2_ = bf16[16,2176]{1,0:T(8,128)(2,1)S(1)} collective-permute-done((bf16[16,2176]{1,0:T(8,128)(2,1)S(1)}, bf16[16,2176]{1,0:T(8,128)(2,1)S(1)}, u32[]{:S(2)}, u32[]{:S(2)}) %collective-permute-start.14) | collective-permute-done | bytes 69664 | tf_op jit(solution)/shard_map/ppermute | solution.py:499
  50.9 0.8 %collective-permute-done.13.refs_1_ = bf16[16,2176]{1,0:T(8,128)(2,1)S(1)} collective-permute-done((bf16[16,2176]{1,0:T(8,128)(2,1)S(1)}, bf16[16,2176]{1,0:T(8,128)(2,1)S(1)}, u32[]{:S(2)}, u32[]{:S(2)}) %collective-permute-start.13) | collective-permute-done | bytes 69664 | tf_op jit(solution)/shard_map/ppermute | solution.py:499
  51.7 1.9 %shard_map.123.refs_10_ = bf16[1,768,2048]{2,1,0:T(8,128)(2,1)S(1)} custom-call(bf16[1,768,2048]{2,1,0:T(8,128)(2,1)} %refs_0_.5), custom_call_target="tpu_custom_call" | custom-call | tf_op jit(solution)/shard_map/pallas_call | solution.py:476
  53.6 2.9 %shard_map.122 = (bf16[1,2048,768]{2,1,0:T(8,128)(2,1)S(1)}, bf16[1,2048,768]{2,1,0:T(8,128)(2,1)S(1)}) custom-call(bf16[1,2048,768]{2,1,0:T(8,128)(2,1)} %refs_0_.4, bf16[1,2048,768]{2,1,0:T(8,128)(2,1)} %refs_1_.3), custom_call_target="tpu_custom_call" | custom-call | tf_op jit(solution)/shard_map/pallas_call | solution.py:476
  56.5 1.5 %experts.1 = (bf16[64,2048]{1,0:T(8,128)(2,1)S(1)}, bf16[64,2048]{1,0:T(8,128)(2,1)S(1)}) custom-call(bf16[16,2176]{1,0:T(8,128)(2,1)S(1)} %get-tuple-element.49.refs_0_, bf16[16,2176]{1,0:T(8,128)(2,1)S(1)} %collective-permute-done.13.refs_1_, bf16[16,2176]{1,0:T(8,128)(2,1)S(1)} %collective-permute-done.14.refs_2_, ...), custom_call_target="tpu_custom_call" | custom-call | tf_op jit(solution)/shard_map/experts/pallas_call | solution.py:584
  58.1 0.6 collective-permute-start.20
  58.6 1.2 %collective-permute-done.20.received = bf16[64,2048]{1,0:T(8,128)(2,1)S(1)} collective-permute-done((bf16[64,2048]{1,0:T(8,128)(2,1)S(1)}, bf16[64,2048]{1,0:T(8,128)(2,1)S(1)}, u32[]{:S(2)}, u32[]{:S(2)}) %collective-permute-start.20) | collective-permute-done | bytes 262176 | tf_op jit(solution)/shard_map/ppermute | solution.py:506
  59.8 0.1 quarters.1
  59.9 0.6 collective-permute-start.21
  60.4 1.3 %collective-permute-start.22 = (bf16[16,2048]{1,0:T(8,128)(2,1)S(1)}, bf16[16,2048]{1,0:T(8,128)(2,1)S(1)}, u32[]{:S(2)}, u32[]{:S(2)}) collective-permute-start(bf16[16,2048]{1,0:T(8,128)(2,1)S(1)} %get-tuple-element.56), channel_id=1, source_target_pairs={{0,4},{2,6},{4,0},{6,2},{8,12},{10,14},{12,8},{14,10},{1,5},{3,7},... | collective-permute-start | bytes 196616 | tf_op jit(solution)/shard_map/ppermute | solution.py:499
  61.7 1.7 %collective-permute-start.23 = (bf16[16,2048]{1,0:T(8,128)(2,1)S(1)}, bf16[16,2048]{1,0:T(8,128)(2,1)S(1)}, u32[]{:S(2)}, u32[]{:S(2)}) collective-permute-start(bf16[16,2048]{1,0:T(8,128)(2,1)S(1)} %get-tuple-element.57), channel_id=1, source_target_pairs={{0,6},{2,4},{4,2},{6,0},{8,14},{10,12},{12,10},{14,8},{1,7},{3,5},... | collective-permute-start | bytes 196616 | tf_op jit(solution)/shard_map/ppermute | solution.py:499
  63.4 0.9 %collective-permute-done.21.refs_1_ = bf16[16,2048]{1,0:T(8,128)(2,1)S(1)} collective-permute-done((bf16[16,2048]{1,0:T(8,128)(2,1)S(1)}, bf16[16,2048]{1,0:T(8,128)(2,1)S(1)}, u32[]{:S(2)}, u32[]{:S(2)}) %collective-permute-start.21) | collective-permute-done | bytes 65568 | tf_op jit(solution)/shard_map/ppermute | solution.py:499
  64.3 0.4 collective-permute-done.22.refs_2_
  64.7 2.4 %collective-permute-done.23.refs_3_ = bf16[16,2048]{1,0:T(8,128)(2,1)S(1)} collective-permute-done((bf16[16,2048]{1,0:T(8,128)(2,1)S(1)}, bf16[16,2048]{1,0:T(8,128)(2,1)S(1)}, u32[]{:S(2)}, u32[]{:S(2)}) %collective-permute-start.23) | collective-permute-done | bytes 65568 | tf_op jit(solution)/shard_map/ppermute | solution.py:499
  67.1 1.2 %collective-permute-start.24 = (bf16[8,2048]{1,0:T(8,128)(2,1)S(1)}, bf16[8,2048]{1,0:T(8,128)(2,1)S(1)}, u32[]{:S(2)}, u32[]{:S(2)}) collective-permute-start(bf16[8,2048]{1,0:T(8,128)(2,1)S(1)} %get-tuple-element.59), channel_id=1, source_target_pairs={{0,8},{2,10},{4,12},{6,14},{8,0},{10,2},{12,4},{14,6},{1,9},{3,11}... | collective-permute-start | bytes 98312 | tf_op jit(solution)/shard_map/ppermute | solution.py:616
  68.3 0.6 emit.1
  69.0 3.0 %collective-permute-done.24.refs_1_ = bf16[8,2048]{1,0:T(8,128)(2,1)S(1)} collective-permute-done((bf16[8,2048]{1,0:T(8,128)(2,1)S(1)}, bf16[8,2048]{1,0:T(8,128)(2,1)S(1)}, u32[]{:S(2)}, u32[]{:S(2)}) %collective-permute-start.24) | collective-permute-done | bytes 32800 | tf_op jit(solution)/shard_map/ppermute | solution.py:616
  72.0 0.6 added.1
  (17 shorter events, 0.1 us)
Async XLA Ops:
  0.6 39.3 %copy-start = (bf16[2048]{0:T(1024)(128)(2,1)S(1)}, bf16[2048]{0:T(1024)(128)(2,1)}, u32[]{:S(2)}) copy-start(bf16[2048]{0:T(1024)(128)(2,1)} %param.16) | copy-start | bytes 12292
  0.6 32.8 %collective-permute-start.8 = (bf16[128,2048]{1,0:T(8,128)(2,1)}, bf16[128,2048]{1,0:T(8,128)(2,1)S(1)}, u32[]{:S(2)}, u32[]{:S(2)}) collective-permute-start(bf16[128,2048]{1,0:T(8,128)(2,1)} %refs_3_.1), channel_id=1, source_target_pairs={{0,2},{2,0},{4,6},{6,4},{8,10},{10,8},{12,14},{14,12},{1,3},{3,1},... | collective-permute-start | bytes 1572872 | tf_op jit(solution)/shard_map/ppermute | solution.py:503
  3.7 15.8 %collective-permute-start.3 = (bf16[512,128]{1,0:T(8,128)(2,1)}, bf16[512,128]{1,0:T(8,128)(2,1)S(1)}, u32[]{:S(2)}, u32[]{:S(2)}) collective-permute-start(bf16[512,128]{1,0:T(8,128)(2,1)} %refs_1_.2), channel_id=1, source_target_pairs={{0,2},{2,0},{4,6},{6,4},{8,10},{10,8},{12,14},{14,12},{1,3},{3,1},... | collective-permute-start | bytes 393224 | tf_op jit(solution)/shard_map/ppermute | solution.py:503
  3.8 17.7 %collective-permute-start.4 = (bf16[512,128]{1,0:T(8,128)(2,1)}, bf16[512,128]{1,0:T(8,128)(2,1)S(1)}, u32[]{:S(2)}, u32[]{:S(2)}) collective-permute-start(bf16[512,128]{1,0:T(8,128)(2,1)} %refs_2_.1), channel_id=1, source_target_pairs={{0,2},{2,0},{4,6},{6,4},{8,10},{10,8},{12,14},{14,12},{1,3},{3,1},... | collective-permute-start | bytes 393224 | tf_op jit(solution)/shard_map/ppermute | solution.py:503
  5.7 4.1 %collective-permute-start = (bf16[16,1024]{1,0:T(8,128)(2,1)}, bf16[16,1024]{1,0:T(8,128)(2,1)S(1)}, u32[]{:S(2)}, u32[]{:S(2)}) collective-permute-start(bf16[16,1024]{1,0:T(8,128)(2,1)} %refs_0_.3), channel_id=1, source_target_pairs={{0,4},{2,6},{4,0},{6,2},{8,12},{10,14},{12,8},{14,10},{1,5},{3,7},... | collective-permute-start | bytes 98312 | tf_op jit(solution)/shard_map/ppermute | solution.py:469
  7.3 6.4 %collective-permute-start.2 = (bf16[16,1024]{1,0:T(8,128)(2,1)}, bf16[16,1024]{1,0:T(8,128)(2,1)S(1)}, u32[]{:S(2)}, u32[]{:S(2)}) collective-permute-start(bf16[16,1024]{1,0:T(8,128)(2,1)} %refs_0_.3), channel_id=1, source_target_pairs={{0,12},{2,14},{4,8},{6,10},{8,4},{10,6},{12,0},{14,2},{1,13},{3,15... | collective-permute-start | bytes 98312 | tf_op jit(solution)/shard_map/ppermute | solution.py:469
  9.9 5.0 %collective-permute-start.1 = (bf16[16,1024]{1,0:T(8,128)(2,1)}, bf16[16,1024]{1,0:T(8,128)(2,1)S(1)}, u32[]{:S(2)}, u32[]{:S(2)}) collective-permute-start(bf16[16,1024]{1,0:T(8,128)(2,1)} %refs_0_.3), channel_id=1, source_target_pairs={{0,8},{2,10},{4,12},{6,14},{8,0},{10,2},{12,4},{14,6},{1,9},{3,11}... | collective-permute-start | bytes 98312 | tf_op jit(solution)/shard_map/ppermute | solution.py:469
  23.1 4.5 %collective-permute-start.5 = (bf16[64,384]{1,0:T(8,128)(2,1)S(1)}, bf16[64,384]{1,0:T(8,128)(2,1)S(1)}, u32[]{:S(2)}, u32[]{:S(2)}) collective-permute-start(bf16[64,384]{1,0:T(8,128)(2,1)S(1)} %get-tuple-element.37), channel_id=1, source_target_pairs={{0,4},{2,6},{4,0},{6,2},{8,12},{10,14},{12,8},{14,10},{1,5},{3,7},... | collective-permute-start | bytes 147464 | tf_op jit(solution)/shard_map/ppermute | solution.py:469
  25.0 6.0 %collective-permute-start.6 = (bf16[64,384]{1,0:T(8,128)(2,1)S(1)}, bf16[64,384]{1,0:T(8,128)(2,1)S(1)}, u32[]{:S(2)}, u32[]{:S(2)}) collective-permute-start(bf16[64,384]{1,0:T(8,128)(2,1)S(1)} %get-tuple-element.38), channel_id=1, source_target_pairs={{0,8},{2,10},{4,12},{6,14},{8,0},{10,2},{12,4},{14,6},{1,9},{3,11}... | collective-permute-start | bytes 147464 | tf_op jit(solution)/shard_map/ppermute | solution.py:469
  27.6 5.9 %collective-permute-start.7 = (bf16[64,384]{1,0:T(8,128)(2,1)S(1)}, bf16[64,384]{1,0:T(8,128)(2,1)S(1)}, u32[]{:S(2)}, u32[]{:S(2)}) collective-permute-start(bf16[64,384]{1,0:T(8,128)(2,1)S(1)} %get-tuple-element.39), channel_id=1, source_target_pairs={{0,12},{2,14},{4,8},{6,10},{8,4},{10,6},{12,0},{14,2},{1,13},{3,15... | collective-permute-start | bytes 147464 | tf_op jit(solution)/shard_map/ppermute | solution.py:469
  34.0 1.4 %collective-permute-start.9 = (bf16[32,2048]{1,0:T(8,128)(2,1)S(1)}, bf16[32,2048]{1,0:T(8,128)(2,1)S(1)}, u32[]{:S(2)}, u32[]{:S(2)}) collective-permute-start(bf16[32,2048]{1,0:T(8,128)(2,1)S(1)} %get-tuple-element.42), channel_id=1, source_target_pairs={{0,1},{1,0},{2,3},{3,2},{4,5},{5,4},{6,7},{7,6},{8,9},{9,8},{10,11... | collective-permute-start | bytes 393224 | tf_op jit(solution)/shard_map/ppermute | solution.py:506
  35.5 5.2 %collective-permute-start.10 = (bf16[16,2048]{1,0:T(8,128)(2,1)S(1)}, bf16[16,2048]{1,0:T(8,128)(2,1)S(1)}, u32[]{:S(2)}, u32[]{:S(2)}) collective-permute-start(bf16[16,2048]{1,0:T(8,128)(2,1)S(1)} %get-tuple-element.44), channel_id=1, source_target_pairs={{0,4},{2,6},{4,0},{6,2},{8,12},{10,14},{12,8},{14,10},{1,5},{3,7},... | collective-permute-start | bytes 196616 | tf_op jit(solution)/shard_map/ppermute | solution.py:469
  35.6 8.6 %collective-permute-start.11 = (bf16[16,2048]{1,0:T(8,128)(2,1)S(1)}, bf16[16,2048]{1,0:T(8,128)(2,1)S(1)}, u32[]{:S(2)}, u32[]{:S(2)}) collective-permute-start(bf16[16,2048]{1,0:T(8,128)(2,1)S(1)} %get-tuple-element.45), channel_id=1, source_target_pairs={{0,8},{2,10},{4,12},{6,14},{8,0},{10,2},{12,4},{14,6},{1,9},{3,11}... | collective-permute-start | bytes 196616 | tf_op jit(solution)/shard_map/ppermute | solution.py:469
  36.7 7.5 %collective-permute-start.12 = (bf16[16,2048]{1,0:T(8,128)(2,1)S(1)}, bf16[16,2048]{1,0:T(8,128)(2,1)S(1)}, u32[]{:S(2)}, u32[]{:S(2)}) collective-permute-start(bf16[16,2048]{1,0:T(8,128)(2,1)S(1)} %get-tuple-element.46), channel_id=1, source_target_pairs={{0,12},{2,14},{4,8},{6,10},{8,4},{10,6},{12,0},{14,2},{1,13},{3,15... | collective-permute-start | bytes 196616 | tf_op jit(solution)/shard_map/ppermute | solution.py:469
  44.3 5.3 %collective-permute-start.15 = (bf16[16,2176]{1,0:T(8,128)(2,1)S(1)}, bf16[16,2176]{1,0:T(8,128)(2,1)S(1)}, u32[]{:S(2)}, u32[]{:S(2)}) collective-permute-start(bf16[16,2176]{1,0:T(8,128)(2,1)S(1)} %get-tuple-element.49.refs_0_), channel_id=1, source_target_pairs={{0,6},{2,4},{4,2},{6,0},{8,14},{10,12},{12,10},{14,8},{1,7},{3,5},... | collective-permute-start | bytes 208904 | tf_op jit(solution)/shard_map/ppermute | solution.py:499
  46.6 4.3 %collective-permute-start.14 = (bf16[16,2176]{1,0:T(8,128)(2,1)S(1)}, bf16[16,2176]{1,0:T(8,128)(2,1)S(1)}, u32[]{:S(2)}, u32[]{:S(2)}) collective-permute-start(bf16[16,2176]{1,0:T(8,128)(2,1)S(1)} %get-tuple-element.49.refs_0_), channel_id=1, source_target_pairs={{0,4},{2,6},{4,0},{6,2},{8,12},{10,14},{12,8},{14,10},{1,5},{3,7},... | collective-permute-start | bytes 208904 | tf_op jit(solution)/shard_map/ppermute | solution.py:499
  47.4 4.3 %collective-permute-start.13 = (bf16[16,2176]{1,0:T(8,128)(2,1)S(1)}, bf16[16,2176]{1,0:T(8,128)(2,1)S(1)}, u32[]{:S(2)}, u32[]{:S(2)}) collective-permute-start(bf16[16,2176]{1,0:T(8,128)(2,1)S(1)} %get-tuple-element.49.refs_0_), channel_id=1, source_target_pairs={{0,2},{2,0},{4,6},{6,4},{8,10},{10,8},{12,14},{14,12},{1,3},{3,1},... | collective-permute-start | bytes 208904 | tf_op jit(solution)/shard_map/ppermute | solution.py:499
  47.9 8.6 %collective-permute-start.16 = (bf16[16,2176]{1,0:T(8,128)(2,1)S(1)}, bf16[16,2176]{1,0:T(8,128)(2,1)S(1)}, u32[]{:S(2)}, u32[]{:S(2)}) collective-permute-start(bf16[16,2176]{1,0:T(8,128)(2,1)S(1)} %get-tuple-element.49.refs_0_), channel_id=1, source_target_pairs={{0,1},{1,0},{2,3},{3,2},{4,5},{5,4},{6,7},{7,6},{8,9},{9,8},{10,11... | collective-permute-start | bytes 208904 | tf_op jit(solution)/shard_map/ppermute | solution.py:506
  49.6 6.9 %collective-permute-start.19 = (bf16[16,2176]{1,0:T(8,128)(2,1)S(1)}, bf16[16,2176]{1,0:T(8,128)(2,1)S(1)}, u32[]{:S(2)}, u32[]{:S(2)}) collective-permute-start(bf16[16,2176]{1,0:T(8,128)(2,1)S(1)} %collective-permute-done.15.refs_3_), channel_id=1, source_target_pairs={{0,1},{1,0},{2,3},{3,2},{4,5},{5,4},{6,7},{7,6},{8,9},{9,8},{10,11... | collective-permute-start | bytes 208904 | tf_op jit(solution)/shard_map/ppermute | solution.py:506
  50.9 5.6 %collective-permute-start.18 = (bf16[16,2176]{1,0:T(8,128)(2,1)S(1)}, bf16[16,2176]{1,0:T(8,128)(2,1)S(1)}, u32[]{:S(2)}, u32[]{:S(2)}) collective-permute-start(bf16[16,2176]{1,0:T(8,128)(2,1)S(1)} %collective-permute-done.14.refs_2_), channel_id=1, source_target_pairs={{0,1},{1,0},{2,3},{3,2},{4,5},{5,4},{6,7},{7,6},{8,9},{9,8},{10,11... | collective-permute-start | bytes 208904 | tf_op jit(solution)/shard_map/ppermute | solution.py:506
  51.7 4.8 %collective-permute-start.17 = (bf16[16,2176]{1,0:T(8,128)(2,1)S(1)}, bf16[16,2176]{1,0:T(8,128)(2,1)S(1)}, u32[]{:S(2)}, u32[]{:S(2)}) collective-permute-start(bf16[16,2176]{1,0:T(8,128)(2,1)S(1)} %collective-permute-done.13.refs_1_), channel_id=1, source_target_pairs={{0,1},{1,0},{2,3},{3,2},{4,5},{5,4},{6,7},{7,6},{8,9},{9,8},{10,11... | collective-permute-start | bytes 208904 | tf_op jit(solution)/shard_map/ppermute | solution.py:506
  58.1 1.7 %collective-permute-start.20 = (bf16[64,2048]{1,0:T(8,128)(2,1)S(1)}, bf16[64,2048]{1,0:T(8,128)(2,1)S(1)}, u32[]{:S(2)}, u32[]{:S(2)}) collective-permute-start(bf16[64,2048]{1,0:T(8,128)(2,1)S(1)} %get-tuple-element.53), channel_id=1, source_target_pairs={{0,1},{1,0},{2,3},{3,2},{4,5},{5,4},{6,7},{7,6},{8,9},{9,8},{10,11... | collective-permute-start | bytes 786440 | tf_op jit(solution)/shard_map/ppermute | solution.py:506
  59.9 4.4 %collective-permute-start.21 = (bf16[16,2048]{1,0:T(8,128)(2,1)S(1)}, bf16[16,2048]{1,0:T(8,128)(2,1)S(1)}, u32[]{:S(2)}, u32[]{:S(2)}) collective-permute-start(bf16[16,2048]{1,0:T(8,128)(2,1)S(1)} %get-tuple-element.55), channel_id=1, source_target_pairs={{0,2},{2,0},{4,6},{6,4},{8,10},{10,8},{12,14},{14,12},{1,3},{3,1},... | collective-permute-start | bytes 196616 | tf_op jit(solution)/shard_map/ppermute | solution.py:499
  60.4 4.3 %collective-permute-start.22 = (bf16[16,2048]{1,0:T(8,128)(2,1)S(1)}, bf16[16,2048]{1,0:T(8,128)(2,1)S(1)}, u32[]{:S(2)}, u32[]{:S(2)}) collective-permute-start(bf16[16,2048]{1,0:T(8,128)(2,1)S(1)} %get-tuple-element.56), channel_id=1, source_target_pairs={{0,4},{2,6},{4,0},{6,2},{8,12},{10,14},{12,8},{14,10},{1,5},{3,7},... | collective-permute-start | bytes 196616 | tf_op jit(solution)/shard_map/ppermute | solution.py:499
  61.7 5.4 %collective-permute-start.23 = (bf16[16,2048]{1,0:T(8,128)(2,1)S(1)}, bf16[16,2048]{1,0:T(8,128)(2,1)S(1)}, u32[]{:S(2)}, u32[]{:S(2)}) collective-permute-start(bf16[16,2048]{1,0:T(8,128)(2,1)S(1)} %get-tuple-element.57), channel_id=1, source_target_pairs={{0,6},{2,4},{4,2},{6,0},{8,14},{10,12},{12,10},{14,8},{1,7},{3,5},... | collective-permute-start | bytes 196616 | tf_op jit(solution)/shard_map/ppermute | solution.py:499
  67.1 4.9 %collective-permute-start.24 = (bf16[8,2048]{1,0:T(8,128)(2,1)S(1)}, bf16[8,2048]{1,0:T(8,128)(2,1)S(1)}, u32[]{:S(2)}, u32[]{:S(2)}) collective-permute-start(bf16[8,2048]{1,0:T(8,128)(2,1)S(1)} %get-tuple-element.59), channel_id=1, source_target_pairs={{0,8},{2,10},{4,12},{6,14},{8,0},{10,2},{12,4},{14,6},{1,9},{3,11}... | collective-permute-start | bytes 98312 | tf_op jit(solution)/shard_map/ppermute | solution.py:616

commit v5 on v4

--- a/solution.py
+++ b/solution.py
@@ -261,43 +261,48 @@
     routes = routes_ref[...]
     lane = lax.broadcasted_iota(jnp.int32, (tokens, HD), 1)
     scale = 1.0 / math.sqrt(HD)
-    for group in range(far_count):
-        rows = group * own_heads * tokens
+    joined = 2
+    for first in range(0, far_count, joined):
+        rows = first * own_heads * tokens
         scores = lax.dot_general(
-            q_all[rows : rows + own_heads * tokens, :],
+            q_all[rows : rows + joined * own_heads * tokens, :],
             keys[...],
             (((1,), (1,)), ((), ())),
             preferred_element_type=jnp.float32,
         )
-        extra = routes
         weights_16 = []
-        for j in range(own_heads):
-            part = jnp.where(visible, scores[j * tokens : (j + 1) * tokens] * scale, NEG_FILL)
-            top = jnp.maximum(jnp.max(part, axis=1, keepdims=True), NEG_FILL / 10)
-            top = top.astype(jnp.bfloat16).astype(jnp.float32)
-            weights = jnp.exp(part - top)
-            total = jnp.sum(weights, axis=1, keepdims=True)
-            total_high = total.astype(jnp.bfloat16).astype(jnp.float32)
-            extra = jnp.where(lane == 3 * j, top, extra)
-            extra = jnp.where(lane == 3 * j + 1, total_high, extra)
-            extra = jnp.where(lane == 3 * j + 2, total - total_high, extra)
-            weights_16.append(weights.astype(jnp.bfloat16))
+        for group in range(first, first + joined):
+            extra = routes
+            for j in range(own_heads):
+                at = (group - first) * own_heads + j
+                part = scores[at * tokens : (at + 1) * tokens] * scale
+                part = jnp.where(visible, part, NEG_FILL)
+                top = jnp.maximum(jnp.max(part, axis=1, keepdims=True), NEG_FILL / 10)
+                top = top.astype(jnp.bfloat16).astype(jnp.float32)
+                weights = jnp.exp(part - top)
+                total = jnp.sum(weights, axis=1, keepdims=True)
+                total_high = total.astype(jnp.bfloat16).astype(jnp.float32)
+                extra = jnp.where(lane == 3 * j, top, extra)
+                extra = jnp.where(lane == 3 * j + 1, total_high, extra)
+                extra = jnp.where(lane == 3 * j + 2, total - total_high, extra)
+                weights_16.append(weights.astype(jnp.bfloat16))
+            staged[group, :, own_heads * HD :] = extra.astype(jnp.bfloat16)
         numerator = jnp.dot(
             jnp.concatenate(weights_16, axis=0), values[...], preferred_element_type=jnp.float32
         ).astype(jnp.bfloat16)
-        for j in range(own_heads):
-            staged[group, :, j * HD : (j + 1) * HD] = numerator[j * tokens : (j + 1) * tokens]
-        staged[group, :, own_heads * HD :] = extra.astype(jnp.bfloat16)
+        for group in range(first, first + joined):
+            for j in range(own_heads):
+                at = (group - first) * own_heads + j
+                staged[group, :, j * HD : (j + 1) * HD] = numerator[at * tokens : (at + 1) * tokens]
     for step in range(far_count):
         outs[step][...] = staged[far ^ step]
 
 
-def project_kernel(sizes, *refs):
+def merge_kernel(sizes, *refs):
     far_count, own_heads, own_tokens = sizes
     messages = refs[:far_count]
-    weight_own, weight_side, keep, send, routes, partial = refs[far_count:]
-    far, near = place_of()
-    row_at = lax.axis_index("rows")
+    weight_own, side, routes, partial = refs[far_count:]
+    _, near = place_of()
     tokens = messages[0].shape[0]
     attended = []
     extras = [m[:, own_heads * HD :].astype(jnp.float32) for m in messages]
@@ -314,10 +319,23 @@
             below += factor * (e[:, 3 * j + 1 : 3 * j + 2] + e[:, 3 * j + 2 : 3 * j + 3])
         attended.append(above / below)
     first = jnp.where(near == 0, attended[0], attended[1]).astype(jnp.bfloat16)
-    second = jnp.where(near == 0, attended[1], attended[0]).astype(jnp.bfloat16)
-    partial[...] = jnp.dot(
-        first, weight_own[...], preferred_element_type=jnp.float32
-    ) + jnp.dot(second, weight_side[...], preferred_element_type=jnp.float32)
+    side[...] = jnp.where(near == 0, attended[1], attended[0]).astype(jnp.bfloat16)
+    partial[...] = jnp.dot(first, weight_own[...], preferred_element_type=jnp.float32)
+    for at, step in enumerate(range(0, far_count, 2)):
+        e = extras[step]
+        routes[at * own_tokens : (at + 1) * own_tokens, :] = (
+            e[:own_tokens] + e[own_tokens : 2 * own_tokens]
+        )
+
+
+def project_kernel(sizes, side, weight_side, merged, keep, send, partial):
+    far_count, own_tokens = sizes
+    far = place_of()[0]
+    row_at = lax.axis_index("rows")
+    tokens = side.shape[0]
+    partial[...] = merged[...] + jnp.dot(
+        side[...], weight_side[...], preferred_element_type=jnp.float32
+    )
     piece = tokens // far_count
     other = 1 - row_at
     mine, theirs = [], []
@@ -328,11 +346,6 @@
         theirs.append(partial[pl.ds(at, own_tokens), :])
     keep[...] = jnp.concatenate(mine, axis=0)
     send[...] = jnp.concatenate(theirs, axis=0).astype(jnp.bfloat16)
-    for at, step in enumerate(range(0, far_count, 2)):
-        e = extras[step]
-        routes[at * own_tokens : (at + 1) * own_tokens, :] = (
-            e[:own_tokens] + e[own_tokens : 2 * own_tokens]
-        )
 
 
 def parts_kernel(keep, received, *outs):
@@ -544,15 +557,23 @@
     )(*q_pieces, keys_own, key_side, values_own, value_side, pos_all, routes)
     messages = over_far(messages)
     (down_weight,) = fetched(down_weight)
-    keep, send, routes = pl.pallas_call(
-        functools.partial(project_kernel, (far_count, own_heads, own_tokens)),
-        out_shape=[shape_of((held, width), f32), shape_of((held, width), bf16), shape_of((shared, HD), f32)],
-        in_specs=in_vmem(far_count + 2),
+    side, routes, merged = pl.pallas_call(
+        functools.partial(merge_kernel, (far_count, own_heads, own_tokens)),
+        out_shape=[shape_of((tokens, HD), bf16), shape_of((shared, HD), f32), shape_of((tokens, width), f32)],
+        in_specs=in_vmem(far_count + 1),
         out_specs=in_vmem(3),
+        compiler_params=grant(4),
+        name="merge",
+    )(*messages, weight_own)
+    keep, send = pl.pallas_call(
+        functools.partial(project_kernel, (far_count, own_tokens)),
+        out_shape=[shape_of((held, width), f32), shape_of((held, width), bf16)],
+        in_specs=in_vmem(3),
+        out_specs=in_vmem(2),
         scratch_shapes=[pltpu.VMEM((tokens, width), f32)],
-        compiler_params=grant(8),
+        compiler_params=grant(6),
         name="project",
-    )(*messages, weight_own, weight_side)
+    )(side, weight_side, merged)
     parts = pl.pallas_call(
         parts_kernel,
         out_shape=[shape_of((shared, width), f32)] + [shape_of((shared, width), bf16)] * (far_count - 1),

time: 72.8 us -> 72.5 us (level)
  transfers between devices with their start and end apart: 25 -> 25, of which waited for: 17 -> 18; matrix products, arithmetic and copies ran while one was open for 0% -> 0% of each run, Pallas kernels for 11% -> 12%
where the time goes in v5:
time: 72.5 us; the launch traced here: 72.3 us
  waiting for transfers between devices  30.9 us (43%)
  starting transfers between devices  29.6 us (41%)
  Pallas kernels  11 us (15%)
  between operations  0.8 us (1%)
    ppermute x9, starting transfers between devices, over_far(): moved.append(lax.ppermute(arrays[step], 'blk', far_of(step, blk)))  15.5 us
    ppermute x9, waiting for transfers between devices, over_far(): moved.append(lax.ppermute(arrays[step], 'blk', far_of(step, blk)))  11.3 us
    ppermute x6, waiting for transfers between devices, over_close(): moved.append(lax.ppermute(arrays[step], 'blk', pairs))  7.44 us
    ppermute x6, starting transfers between devices, over_close(): moved.append(lax.ppermute(arrays[step], 'blk', pairs))  7.11 us
    ppermute x3, waiting for transfers between devices, over_near(): return lax.ppermute(array, 'blk', side_of(blk))  6.58 us
    ppermute x3, starting transfers between devices, over_near(): return lax.ppermute(array, 'blk', side_of(blk))  5.09 us
    pallas_call x2, Pallas kernels, fetched(): pl.pallas_call(fetch_kernel, out_shape=[shape_of(a.shape, a.dtype) for a...  4.76 us
    ppermute x1, waiting for transfers between devices, paired_device(): lax.ppermute(term, 'blk', far_of(step, blk))  3.01 us
  transfers between devices with their start and end apart: 25, of which 18 were waited for; matrix products, arithmetic and copies ran while one was open for 0% of the time, Pallas kernels for 12%

profile of v5, /device:TPU:0, one launch (start us, length us, event | category | flops | bytes accessed | tf_op | source)
XLA Modules:
  0.0 72.3 jit_solution(16126489700840621948)
XLA Ops:
  0.6 3.1 %collective-permute-start.8 = (bf16[128,2048]{1,0:T(8,128)(2,1)}, bf16[128,2048]{1,0:T(8,128)(2,1)S(1)}, u32[]{:S(2)}, u32[]{:S(2)}) collective-permute-start(bf16[128,2048]{1,0:T(8,128)(2,1)} %refs_3_.1), channel_id=1, source_target_pairs={{0,2},{2,0},{4,6},{6,4},{8,10},{10,8},{12,14},{14,12},{1,3},{3,1},... | collective-permute-start | bytes 1572872 | tf_op jit(solution)/shard_map/ppermute | solution.py:516
  3.7 0.1 collective-permute-start.3
  3.8 1.9 %collective-permute-start.4 = (bf16[512,128]{1,0:T(8,128)(2,1)}, bf16[512,128]{1,0:T(8,128)(2,1)S(1)}, u32[]{:S(2)}, u32[]{:S(2)}) collective-permute-start(bf16[512,128]{1,0:T(8,128)(2,1)} %refs_2_.1), channel_id=1, source_target_pairs={{0,2},{2,0},{4,6},{6,4},{8,10},{10,8},{12,14},{14,12},{1,3},{3,1},... | collective-permute-start | bytes 393224 | tf_op jit(solution)/shard_map/ppermute | solution.py:516
  5.7 1.6 %collective-permute-start = (bf16[16,1024]{1,0:T(8,128)(2,1)}, bf16[16,1024]{1,0:T(8,128)(2,1)S(1)}, u32[]{:S(2)}, u32[]{:S(2)}) collective-permute-start(bf16[16,1024]{1,0:T(8,128)(2,1)} %refs_0_.3), channel_id=1, source_target_pairs={{0,4},{2,6},{4,0},{6,2},{8,12},{10,14},{12,8},{14,10},{1,5},{3,7},... | collective-permute-start | bytes 98312 | tf_op jit(solution)/shard_map/ppermute | solution.py:482
  7.3 2.5 %collective-permute-start.2 = (bf16[16,1024]{1,0:T(8,128)(2,1)}, bf16[16,1024]{1,0:T(8,128)(2,1)S(1)}, u32[]{:S(2)}, u32[]{:S(2)}) collective-permute-start(bf16[16,1024]{1,0:T(8,128)(2,1)} %refs_0_.3), channel_id=1, source_target_pairs={{0,12},{2,14},{4,8},{6,10},{8,4},{10,6},{12,0},{14,2},{1,13},{3,15... | collective-permute-start | bytes 98312 | tf_op jit(solution)/shard_map/ppermute | solution.py:482
  9.8 0.1 collective-permute-done.refs_1_
  9.9 2.6 %collective-permute-start.1 = (bf16[16,1024]{1,0:T(8,128)(2,1)}, bf16[16,1024]{1,0:T(8,128)(2,1)S(1)}, u32[]{:S(2)}, u32[]{:S(2)}) collective-permute-start(bf16[16,1024]{1,0:T(8,128)(2,1)} %refs_0_.3), channel_id=1, source_target_pairs={{0,8},{2,10},{4,12},{6,14},{8,0},{10,2},{12,4},{14,6},{1,9},{3,11}... | collective-permute-start | bytes 98312 | tf_op jit(solution)/shard_map/ppermute | solution.py:482
  12.4 1.3 %prepare.1 = (bf16[16,1024]{1,0:T(8,128)(2,1)S(1)}, bf16[512,128]{1,0:T(8,128)(2,1)S(1)}, bf16[512,128]{1,0:T(8,128)(2,1)S(1)}, bf16[128,2048]{1,0:T(8,128)(2,1)...) custom-call(bf16[16,1024]{1,0:T(8,128)(2,1)} %refs_0_.3, bf16[512,128]{1,0:T(8,128)(2,1)} %refs_1_.2, ...), custom_call_target="tpu_custom_call" | custom-call | tf_op jit(solution)/shard_map/prepare/pallas_call | solution.py:526
  13.7 1.1 %collective-permute-done.1.refs_2_ = bf16[16,1024]{1,0:T(8,128)(2,1)S(1)} collective-permute-done((bf16[16,1024]{1,0:T(8,128)(2,1)}, bf16[16,1024]{1,0:T(8,128)(2,1)S(1)}, u32[]{:S(2)}, u32[]{:S(2)}) %collective-permute-start.1) | collective-permute-done | bytes 32800 | tf_op jit(solution)/shard_map/ppermute | solution.py:482
  14.9 4.6 %collective-permute-done.3.refs_5_ = bf16[512,128]{1,0:T(8,128)(2,1)S(1)} collective-permute-done((bf16[512,128]{1,0:T(8,128)(2,1)}, bf16[512,128]{1,0:T(8,128)(2,1)S(1)}, u32[]{:S(2)}, u32[]{:S(2)}) %collective-permute-start.3) | collective-permute-done | bytes 131104 | tf_op jit(solution)/shard_map/ppermute | solution.py:516
  19.5 2.0 %collective-permute-done.4.refs_7_ = bf16[512,128]{1,0:T(8,128)(2,1)S(1)} collective-permute-done((bf16[512,128]{1,0:T(8,128)(2,1)}, bf16[512,128]{1,0:T(8,128)(2,1)S(1)}, u32[]{:S(2)}, u32[]{:S(2)}) %collective-permute-start.4) | collective-permute-done | bytes 131104 | tf_op jit(solution)/shard_map/ppermute | solution.py:516
  21.5 1.2 %attend.1 = (bf16[64,384]{1,0:T(8,128)(2,1)S(1)}, bf16[64,384]{1,0:T(8,128)(2,1)S(1)}, bf16[64,384]{1,0:T(8,128)(2,1)S(1)}, bf16[64,384]{1,0:T(8,128)(2,1)S(1)}) custom-call(bf16[16,1024]{1,0:T(8,128)(2,1)S(1)} %get-tuple-element.33.refs_0_, bf16[16,1024]{1,0:T(8,128)(2,1)S(1)} %collective-permute-done.refs_1_, ...), custom_call_target="tpu_custom_call" | custom-call | tf_op jit(solution)/shard_map/attend/pallas_call | solution.py:544
  22.7 1.9 %collective-permute-start.5 = (bf16[64,384]{1,0:T(8,128)(2,1)S(1)}, bf16[64,384]{1,0:T(8,128)(2,1)S(1)}, u32[]{:S(2)}, u32[]{:S(2)}) collective-permute-start(bf16[64,384]{1,0:T(8,128)(2,1)S(1)} %get-tuple-element.39), channel_id=1, source_target_pairs={{0,4},{2,6},{4,0},{6,2},{8,12},{10,14},{12,8},{14,10},{1,5},{3,7},... | collective-permute-start | bytes 147464 | tf_op jit(solution)/shard_map/ppermute | solution.py:482
  24.6 2.6 %collective-permute-start.6 = (bf16[64,384]{1,0:T(8,128)(2,1)S(1)}, bf16[64,384]{1,0:T(8,128)(2,1)S(1)}, u32[]{:S(2)}, u32[]{:S(2)}) collective-permute-start(bf16[64,384]{1,0:T(8,128)(2,1)S(1)} %get-tuple-element.40), channel_id=1, source_target_pairs={{0,8},{2,10},{4,12},{6,14},{8,0},{10,2},{12,4},{14,6},{1,9},{3,11}... | collective-permute-start | bytes 147464 | tf_op jit(solution)/shard_map/ppermute | solution.py:482
  27.2 0.2 collective-permute-done.5.refs_1_
  27.3 3.3 %collective-permute-done.6.refs_2_ = bf16[64,384]{1,0:T(8,128)(2,1)S(1)} collective-permute-done((bf16[64,384]{1,0:T(8,128)(2,1)S(1)}, bf16[64,384]{1,0:T(8,128)(2,1)S(1)}, u32[]{:S(2)}, u32[]{:S(2)}) %collective-permute-start.6) | collective-permute-done | bytes 49184 | tf_op jit(solution)/shard_map/ppermute | solution.py:482
  30.6 2.4 %collective-permute-done.7.refs_3_ = bf16[64,384]{1,0:T(8,128)(2,1)S(1)} collective-permute-done((bf16[64,384]{1,0:T(8,128)(2,1)S(1)}, bf16[64,384]{1,0:T(8,128)(2,1)S(1)}, u32[]{:S(2)}, u32[]{:S(2)}) %collective-permute-start.7) | collective-permute-done | bytes 49184 | tf_op jit(solution)/shard_map/ppermute | solution.py:482
  33.0 0.5 merge.1
  33.5 0.2 project.1
  33.8 0.1 collective-permute-start.9
  33.9 1.3 %collective-permute-done.9.received = bf16[32,2048]{1,0:T(8,128)(2,1)S(1)} collective-permute-done((bf16[32,2048]{1,0:T(8,128)(2,1)S(1)}, bf16[32,2048]{1,0:T(8,128)(2,1)S(1)}, u32[]{:S(2)}, u32[]{:S(2)}) %collective-permute-start.9) | collective-permute-done | bytes 131104 | tf_op jit(solution)/shard_map/ppermute | solution.py:519
  35.2 0.1 collective-permute-start.10
  35.3 1.1 %collective-permute-start.11 = (bf16[16,2048]{1,0:T(8,128)(2,1)S(1)}, bf16[16,2048]{1,0:T(8,128)(2,1)S(1)}, u32[]{:S(2)}, u32[]{:S(2)}) collective-permute-start(bf16[16,2048]{1,0:T(8,128)(2,1)S(1)} %get-tuple-element.49), channel_id=1, source_target_pairs={{0,8},{2,10},{4,12},{6,14},{8,0},{10,2},{12,4},{14,6},{1,9},{3,11}... | collective-permute-start | bytes 196616 | tf_op jit(solution)/shard_map/ppermute | solution.py:482
  36.4 3.2 %collective-permute-start.12 = (bf16[16,2048]{1,0:T(8,128)(2,1)S(1)}, bf16[16,2048]{1,0:T(8,128)(2,1)S(1)}, u32[]{:S(2)}, u32[]{:S(2)}) collective-permute-start(bf16[16,2048]{1,0:T(8,128)(2,1)S(1)} %get-tuple-element.50), channel_id=1, source_target_pairs={{0,12},{2,14},{4,8},{6,10},{8,4},{10,6},{12,0},{14,2},{1,13},{3,15... | collective-permute-start | bytes 196616 | tf_op jit(solution)/shard_map/ppermute | solution.py:482
  39.7 0.8 %collective-permute-done.10.refs_1_ = bf16[16,2048]{1,0:T(8,128)(2,1)S(1)} collective-permute-done((bf16[16,2048]{1,0:T(8,128)(2,1)S(1)}, bf16[16,2048]{1,0:T(8,128)(2,1)S(1)}, u32[]{:S(2)}, u32[]{:S(2)}) %collective-permute-start.10) | collective-permute-done | bytes 65568 | tf_op jit(solution)/shard_map/ppermute | solution.py:482
  40.4 3.5 %collective-permute-done.11.refs_2_ = bf16[16,2048]{1,0:T(8,128)(2,1)S(1)} collective-permute-done((bf16[16,2048]{1,0:T(8,128)(2,1)S(1)}, bf16[16,2048]{1,0:T(8,128)(2,1)S(1)}, u32[]{:S(2)}, u32[]{:S(2)}) %collective-permute-start.11) | collective-permute-done | bytes 65568 | tf_op jit(solution)/shard_map/ppermute | solution.py:482
  43.9 0.1 norm.1
  44.1 2.3 %collective-permute-start.15 = (bf16[16,2176]{1,0:T(8,128)(2,1)S(1)}, bf16[16,2176]{1,0:T(8,128)(2,1)S(1)}, u32[]{:S(2)}, u32[]{:S(2)}) collective-permute-start(bf16[16,2176]{1,0:T(8,128)(2,1)S(1)} %get-tuple-element.53.refs_0_), channel_id=1, source_target_pairs={{0,6},{2,4},{4,2},{6,0},{8,14},{10,12},{12,10},{14,8},{1,7},{3,5},... | collective-permute-start | bytes 208904 | tf_op jit(solution)/shard_map/ppermute | solution.py:512
  46.4 0.8 %collective-permute-start.14 = (bf16[16,2176]{1,0:T(8,128)(2,1)S(1)}, bf16[16,2176]{1,0:T(8,128)(2,1)S(1)}, u32[]{:S(2)}, u32[]{:S(2)}) collective-permute-start(bf16[16,2176]{1,0:T(8,128)(2,1)S(1)} %get-tuple-element.53.refs_0_), channel_id=1, source_target_pairs={{0,4},{2,6},{4,0},{6,2},{8,12},{10,14},{12,8},{14,10},{1,5},{3,7},... | collective-permute-start | bytes 208904 | tf_op jit(solution)/shard_map/ppermute | solution.py:512
  47.1 0.5 collective-permute-start.13
  47.6 1.7 %collective-permute-done.15.refs_3_ = bf16[16,2176]{1,0:T(8,128)(2,1)S(1)} collective-permute-done((bf16[16,2176]{1,0:T(8,128)(2,1)S(1)}, bf16[16,2176]{1,0:T(8,128)(2,1)S(1)}, u32[]{:S(2)}, u32[]{:S(2)}) %collective-permute-start.15) | collective-permute-done | bytes 69664 | tf_op jit(solution)/shard_map/ppermute | solution.py:512
  49.4 1.3 %collective-permute-done.14.refs_2_ = bf16[16,2176]{1,0:T(8,128)(2,1)S(1)} collective-permute-done((bf16[16,2176]{1,0:T(8,128)(2,1)S(1)}, bf16[16,2176]{1,0:T(8,128)(2,1)S(1)}, u32[]{:S(2)}, u32[]{:S(2)}) %collective-permute-start.14) | collective-permute-done | bytes 69664 | tf_op jit(solution)/shard_map/ppermute | solution.py:512
  50.7 0.8 %collective-permute-done.13.refs_1_ = bf16[16,2176]{1,0:T(8,128)(2,1)S(1)} collective-permute-done((bf16[16,2176]{1,0:T(8,128)(2,1)S(1)}, bf16[16,2176]{1,0:T(8,128)(2,1)S(1)}, u32[]{:S(2)}, u32[]{:S(2)}) %collective-permute-start.13) | collective-permute-done | bytes 69664 | tf_op jit(solution)/shard_map/ppermute | solution.py:512
  51.4 1.9 %shard_map.123.refs_10_ = bf16[1,768,2048]{2,1,0:T(8,128)(2,1)S(1)} custom-call(bf16[1,768,2048]{2,1,0:T(8,128)(2,1)} %refs_0_.5), custom_call_target="tpu_custom_call" | custom-call | tf_op jit(solution)/shard_map/pallas_call | solution.py:489
  53.4 2.9 %shard_map.122 = (bf16[1,2048,768]{2,1,0:T(8,128)(2,1)S(1)}, bf16[1,2048,768]{2,1,0:T(8,128)(2,1)S(1)}) custom-call(bf16[1,2048,768]{2,1,0:T(8,128)(2,1)} %refs_0_.4, bf16[1,2048,768]{2,1,0:T(8,128)(2,1)} %refs_1_.3), custom_call_target="tpu_custom_call" | custom-call | tf_op jit(solution)/shard_map/pallas_call | solution.py:489
  56.3 1.5 %experts.1 = (bf16[64,2048]{1,0:T(8,128)(2,1)S(1)}, bf16[64,2048]{1,0:T(8,128)(2,1)S(1)}) custom-call(bf16[16,2176]{1,0:T(8,128)(2,1)S(1)} %get-tuple-element.53.refs_0_, bf16[16,2176]{1,0:T(8,128)(2,1)S(1)} %collective-permute-done.13.refs_1_, bf16[16,2176]{1,0:T(8,128)(2,1)S(1)} %collective-permute-done.14.refs_2_, ...), custom_call_target="tpu_custom_call" | custom-call | tf_op jit(solution)/shard_map/experts/pallas_call | solution.py:605
  57.8 0.6 collective-permute-start.20
  58.4 1.2 %collective-permute-done.20.received = bf16[64,2048]{1,0:T(8,128)(2,1)S(1)} collective-permute-done((bf16[64,2048]{1,0:T(8,128)(2,1)S(1)}, bf16[64,2048]{1,0:T(8,128)(2,1)S(1)}, u32[]{:S(2)}, u32[]{:S(2)}) %collective-permute-start.20) | collective-permute-done | bytes 262176 | tf_op jit(solution)/shard_map/ppermute | solution.py:519
  59.6 0.6 collective-permute-start.21
  60.2 1.3 %collective-permute-start.22 = (bf16[16,2048]{1,0:T(8,128)(2,1)S(1)}, bf16[16,2048]{1,0:T(8,128)(2,1)S(1)}, u32[]{:S(2)}, u32[]{:S(2)}) collective-permute-start(bf16[16,2048]{1,0:T(8,128)(2,1)S(1)} %get-tuple-element.60), channel_id=1, source_target_pairs={{0,4},{2,6},{4,0},{6,2},{8,12},{10,14},{12,8},{14,10},{1,5},{3,7},... | collective-permute-start | bytes 196616 | tf_op jit(solution)/shard_map/ppermute | solution.py:512
  61.4 1.7 %collective-permute-start.23 = (bf16[16,2048]{1,0:T(8,128)(2,1)S(1)}, bf16[16,2048]{1,0:T(8,128)(2,1)S(1)}, u32[]{:S(2)}, u32[]{:S(2)}) collective-permute-start(bf16[16,2048]{1,0:T(8,128)(2,1)S(1)} %get-tuple-element.61), channel_id=1, source_target_pairs={{0,6},{2,4},{4,2},{6,0},{8,14},{10,12},{12,10},{14,8},{1,7},{3,5},... | collective-permute-start | bytes 196616 | tf_op jit(solution)/shard_map/ppermute | solution.py:512
  63.2 0.9 %collective-permute-done.21.refs_1_ = bf16[16,2048]{1,0:T(8,128)(2,1)S(1)} collective-permute-done((bf16[16,2048]{1,0:T(8,128)(2,1)S(1)}, bf16[16,2048]{1,0:T(8,128)(2,1)S(1)}, u32[]{:S(2)}, u32[]{:S(2)}) %collective-permute-start.21) | collective-permute-done | bytes 65568 | tf_op jit(solution)/shard_map/ppermute | solution.py:512
  64.0 0.4 collective-permute-done.22.refs_2_
  64.4 2.4 %collective-permute-done.23.refs_3_ = bf16[16,2048]{1,0:T(8,128)(2,1)S(1)} collective-permute-done((bf16[16,2048]{1,0:T(8,128)(2,1)S(1)}, bf16[16,2048]{1,0:T(8,128)(2,1)S(1)}, u32[]{:S(2)}, u32[]{:S(2)}) %collective-permute-start.23) | collective-permute-done | bytes 65568 | tf_op jit(solution)/shard_map/ppermute | solution.py:512
  66.8 1.3 %collective-permute-start.24 = (bf16[8,2048]{1,0:T(8,128)(2,1)S(1)}, bf16[8,2048]{1,0:T(8,128)(2,1)S(1)}, u32[]{:S(2)}, u32[]{:S(2)}) collective-permute-start(bf16[8,2048]{1,0:T(8,128)(2,1)S(1)} %get-tuple-element.63), channel_id=1, source_target_pairs={{0,8},{2,10},{4,12},{6,14},{8,0},{10,2},{12,4},{14,6},{1,9},{3,11}... | collective-permute-start | bytes 98312 | tf_op jit(solution)/shard_map/ppermute | solution.py:637
  68.1 0.6 emit.1
  68.7 3.0 %collective-permute-done.24.refs_1_ = bf16[8,2048]{1,0:T(8,128)(2,1)S(1)} collective-permute-done((bf16[8,2048]{1,0:T(8,128)(2,1)S(1)}, bf16[8,2048]{1,0:T(8,128)(2,1)S(1)}, u32[]{:S(2)}, u32[]{:S(2)}) %collective-permute-start.24) | collective-permute-done | bytes 32800 | tf_op jit(solution)/shard_map/ppermute | solution.py:637
  71.7 0.6 added.1
  (18 shorter events, 0.2 us)
Async XLA Ops:
  0.6 39.0 %copy-start = (bf16[2048]{0:T(1024)(128)(2,1)S(1)}, bf16[2048]{0:T(1024)(128)(2,1)}, u32[]{:S(2)}) copy-start(bf16[2048]{0:T(1024)(128)(2,1)} %param.16) | copy-start | bytes 12292
  0.6 32.9 %collective-permute-start.8 = (bf16[128,2048]{1,0:T(8,128)(2,1)}, bf16[128,2048]{1,0:T(8,128)(2,1)S(1)}, u32[]{:S(2)}, u32[]{:S(2)}) collective-permute-start(bf16[128,2048]{1,0:T(8,128)(2,1)} %refs_3_.1), channel_id=1, source_target_pairs={{0,2},{2,0},{4,6},{6,4},{8,10},{10,8},{12,14},{14,12},{1,3},{3,1},... | collective-permute-start | bytes 1572872 | tf_op jit(solution)/shard_map/ppermute | solution.py:516
  3.7 15.8 %collective-permute-start.3 = (bf16[512,128]{1,0:T(8,128)(2,1)}, bf16[512,128]{1,0:T(8,128)(2,1)S(1)}, u32[]{:S(2)}, u32[]{:S(2)}) collective-permute-start(bf16[512,128]{1,0:T(8,128)(2,1)} %refs_1_.2), channel_id=1, source_target_pairs={{0,2},{2,0},{4,6},{6,4},{8,10},{10,8},{12,14},{14,12},{1,3},{3,1},... | collective-permute-start | bytes 393224 | tf_op jit(solution)/shard_map/ppermute | solution.py:516
  3.8 17.7 %collective-permute-start.4 = (bf16[512,128]{1,0:T(8,128)(2,1)}, bf16[512,128]{1,0:T(8,128)(2,1)S(1)}, u32[]{:S(2)}, u32[]{:S(2)}) collective-permute-start(bf16[512,128]{1,0:T(8,128)(2,1)} %refs_2_.1), channel_id=1, source_target_pairs={{0,2},{2,0},{4,6},{6,4},{8,10},{10,8},{12,14},{14,12},{1,3},{3,1},... | collective-permute-start | bytes 393224 | tf_op jit(solution)/shard_map/ppermute | solution.py:516
  5.7 4.1 %collective-permute-start = (bf16[16,1024]{1,0:T(8,128)(2,1)}, bf16[16,1024]{1,0:T(8,128)(2,1)S(1)}, u32[]{:S(2)}, u32[]{:S(2)}) collective-permute-start(bf16[16,1024]{1,0:T(8,128)(2,1)} %refs_0_.3), channel_id=1, source_target_pairs={{0,4},{2,6},{4,0},{6,2},{8,12},{10,14},{12,8},{14,10},{1,5},{3,7},... | collective-permute-start | bytes 98312 | tf_op jit(solution)/shard_map/ppermute | solution.py:482
  7.3 6.4 %collective-permute-start.2 = (bf16[16,1024]{1,0:T(8,128)(2,1)}, bf16[16,1024]{1,0:T(8,128)(2,1)S(1)}, u32[]{:S(2)}, u32[]{:S(2)}) collective-permute-start(bf16[16,1024]{1,0:T(8,128)(2,1)} %refs_0_.3), channel_id=1, source_target_pairs={{0,12},{2,14},{4,8},{6,10},{8,4},{10,6},{12,0},{14,2},{1,13},{3,15... | collective-permute-start | bytes 98312 | tf_op jit(solution)/shard_map/ppermute | solution.py:482
  9.9 5.0 %collective-permute-start.1 = (bf16[16,1024]{1,0:T(8,128)(2,1)}, bf16[16,1024]{1,0:T(8,128)(2,1)S(1)}, u32[]{:S(2)}, u32[]{:S(2)}) collective-permute-start(bf16[16,1024]{1,0:T(8,128)(2,1)} %refs_0_.3), channel_id=1, source_target_pairs={{0,8},{2,10},{4,12},{6,14},{8,0},{10,2},{12,4},{14,6},{1,9},{3,11}... | collective-permute-start | bytes 98312 | tf_op jit(solution)/shard_map/ppermute | solution.py:482
  22.7 4.6 %collective-permute-start.5 = (bf16[64,384]{1,0:T(8,128)(2,1)S(1)}, bf16[64,384]{1,0:T(8,128)(2,1)S(1)}, u32[]{:S(2)}, u32[]{:S(2)}) collective-permute-start(bf16[64,384]{1,0:T(8,128)(2,1)S(1)} %get-tuple-element.39), channel_id=1, source_target_pairs={{0,4},{2,6},{4,0},{6,2},{8,12},{10,14},{12,8},{14,10},{1,5},{3,7},... | collective-permute-start | bytes 147464 | tf_op jit(solution)/shard_map/ppermute | solution.py:482
  24.6 6.0 %collective-permute-start.6 = (bf16[64,384]{1,0:T(8,128)(2,1)S(1)}, bf16[64,384]{1,0:T(8,128)(2,1)S(1)}, u32[]{:S(2)}, u32[]{:S(2)}) collective-permute-start(bf16[64,384]{1,0:T(8,128)(2,1)S(1)} %get-tuple-element.40), channel_id=1, source_target_pairs={{0,8},{2,10},{4,12},{6,14},{8,0},{10,2},{12,4},{14,6},{1,9},{3,11}... | collective-permute-start | bytes 147464 | tf_op jit(solution)/shard_map/ppermute | solution.py:482
  27.1 5.9 %collective-permute-start.7 = (bf16[64,384]{1,0:T(8,128)(2,1)S(1)}, bf16[64,384]{1,0:T(8,128)(2,1)S(1)}, u32[]{:S(2)}, u32[]{:S(2)}) collective-permute-start(bf16[64,384]{1,0:T(8,128)(2,1)S(1)} %get-tuple-element.41), channel_id=1, source_target_pairs={{0,12},{2,14},{4,8},{6,10},{8,4},{10,6},{12,0},{14,2},{1,13},{3,15... | collective-permute-start | bytes 147464 | tf_op jit(solution)/shard_map/ppermute | solution.py:482
  33.8 1.4 %collective-permute-start.9 = (bf16[32,2048]{1,0:T(8,128)(2,1)S(1)}, bf16[32,2048]{1,0:T(8,128)(2,1)S(1)}, u32[]{:S(2)}, u32[]{:S(2)}) collective-permute-start(bf16[32,2048]{1,0:T(8,128)(2,1)S(1)} %get-tuple-element.46), channel_id=1, source_target_pairs={{0,1},{1,0},{2,3},{3,2},{4,5},{5,4},{6,7},{7,6},{8,9},{9,8},{10,11... | collective-permute-start | bytes 393224 | tf_op jit(solution)/shard_map/ppermute | solution.py:519
  35.2 5.2 %collective-permute-start.10 = (bf16[16,2048]{1,0:T(8,128)(2,1)S(1)}, bf16[16,2048]{1,0:T(8,128)(2,1)S(1)}, u32[]{:S(2)}, u32[]{:S(2)}) collective-permute-start(bf16[16,2048]{1,0:T(8,128)(2,1)S(1)} %get-tuple-element.48), channel_id=1, source_target_pairs={{0,4},{2,6},{4,0},{6,2},{8,12},{10,14},{12,8},{14,10},{1,5},{3,7},... | collective-permute-start | bytes 196616 | tf_op jit(solution)/shard_map/ppermute | solution.py:482
  35.3 8.6 %collective-permute-start.11 = (bf16[16,2048]{1,0:T(8,128)(2,1)S(1)}, bf16[16,2048]{1,0:T(8,128)(2,1)S(1)}, u32[]{:S(2)}, u32[]{:S(2)}) collective-permute-start(bf16[16,2048]{1,0:T(8,128)(2,1)S(1)} %get-tuple-element.49), channel_id=1, source_target_pairs={{0,8},{2,10},{4,12},{6,14},{8,0},{10,2},{12,4},{14,6},{1,9},{3,11}... | collective-permute-start | bytes 196616 | tf_op jit(solution)/shard_map/ppermute | solution.py:482
  36.4 7.5 %collective-permute-start.12 = (bf16[16,2048]{1,0:T(8,128)(2,1)S(1)}, bf16[16,2048]{1,0:T(8,128)(2,1)S(1)}, u32[]{:S(2)}, u32[]{:S(2)}) collective-permute-start(bf16[16,2048]{1,0:T(8,128)(2,1)S(1)} %get-tuple-element.50), channel_id=1, source_target_pairs={{0,12},{2,14},{4,8},{6,10},{8,4},{10,6},{12,0},{14,2},{1,13},{3,15... | collective-permute-start | bytes 196616 | tf_op jit(solution)/shard_map/ppermute | solution.py:482
  44.1 5.3 %collective-permute-start.15 = (bf16[16,2176]{1,0:T(8,128)(2,1)S(1)}, bf16[16,2176]{1,0:T(8,128)(2,1)S(1)}, u32[]{:S(2)}, u32[]{:S(2)}) collective-permute-start(bf16[16,2176]{1,0:T(8,128)(2,1)S(1)} %get-tuple-element.53.refs_0_), channel_id=1, source_target_pairs={{0,6},{2,4},{4,2},{6,0},{8,14},{10,12},{12,10},{14,8},{1,7},{3,5},... | collective-permute-start | bytes 208904 | tf_op jit(solution)/shard_map/ppermute | solution.py:512
  46.4 4.3 %collective-permute-start.14 = (bf16[16,2176]{1,0:T(8,128)(2,1)S(1)}, bf16[16,2176]{1,0:T(8,128)(2,1)S(1)}, u32[]{:S(2)}, u32[]{:S(2)}) collective-permute-start(bf16[16,2176]{1,0:T(8,128)(2,1)S(1)} %get-tuple-element.53.refs_0_), channel_id=1, source_target_pairs={{0,4},{2,6},{4,0},{6,2},{8,12},{10,14},{12,8},{14,10},{1,5},{3,7},... | collective-permute-start | bytes 208904 | tf_op jit(solution)/shard_map/ppermute | solution.py:512
  47.1 4.3 %collective-permute-start.13 = (bf16[16,2176]{1,0:T(8,128)(2,1)S(1)}, bf16[16,2176]{1,0:T(8,128)(2,1)S(1)}, u32[]{:S(2)}, u32[]{:S(2)}) collective-permute-start(bf16[16,2176]{1,0:T(8,128)(2,1)S(1)} %get-tuple-element.53.refs_0_), channel_id=1, source_target_pairs={{0,2},{2,0},{4,6},{6,4},{8,10},{10,8},{12,14},{14,12},{1,3},{3,1},... | collective-permute-start | bytes 208904 | tf_op jit(solution)/shard_map/ppermute | solution.py:512
  47.6 8.6 %collective-permute-start.16 = (bf16[16,2176]{1,0:T(8,128)(2,1)S(1)}, bf16[16,2176]{1,0:T(8,128)(2,1)S(1)}, u32[]{:S(2)}, u32[]{:S(2)}) collective-permute-start(bf16[16,2176]{1,0:T(8,128)(2,1)S(1)} %get-tuple-element.53.refs_0_), channel_id=1, source_target_pairs={{0,1},{1,0},{2,3},{3,2},{4,5},{5,4},{6,7},{7,6},{8,9},{9,8},{10,11... | collective-permute-start | bytes 208904 | tf_op jit(solution)/shard_map/ppermute | solution.py:519
  49.3 6.9 %collective-permute-start.19 = (bf16[16,2176]{1,0:T(8,128)(2,1)S(1)}, bf16[16,2176]{1,0:T(8,128)(2,1)S(1)}, u32[]{:S(2)}, u32[]{:S(2)}) collective-permute-start(bf16[16,2176]{1,0:T(8,128)(2,1)S(1)} %collective-permute-done.15.refs_3_), channel_id=1, source_target_pairs={{0,1},{1,0},{2,3},{3,2},{4,5},{5,4},{6,7},{7,6},{8,9},{9,8},{10,11... | collective-permute-start | bytes 208904 | tf_op jit(solution)/shard_map/ppermute | solution.py:519
  50.7 5.6 %collective-permute-start.18 = (bf16[16,2176]{1,0:T(8,128)(2,1)S(1)}, bf16[16,2176]{1,0:T(8,128)(2,1)S(1)}, u32[]{:S(2)}, u32[]{:S(2)}) collective-permute-start(bf16[16,2176]{1,0:T(8,128)(2,1)S(1)} %collective-permute-done.14.refs_2_), channel_id=1, source_target_pairs={{0,1},{1,0},{2,3},{3,2},{4,5},{5,4},{6,7},{7,6},{8,9},{9,8},{10,11... | collective-permute-start | bytes 208904 | tf_op jit(solution)/shard_map/ppermute | solution.py:519
  51.4 4.8 %collective-permute-start.17 = (bf16[16,2176]{1,0:T(8,128)(2,1)S(1)}, bf16[16,2176]{1,0:T(8,128)(2,1)S(1)}, u32[]{:S(2)}, u32[]{:S(2)}) collective-permute-start(bf16[16,2176]{1,0:T(8,128)(2,1)S(1)} %collective-permute-done.13.refs_1_), channel_id=1, source_target_pairs={{0,1},{1,0},{2,3},{3,2},{4,5},{5,4},{6,7},{7,6},{8,9},{9,8},{10,11... | collective-permute-start | bytes 208904 | tf_op jit(solution)/shard_map/ppermute | solution.py:519
  57.8 1.7 %collective-permute-start.20 = (bf16[64,2048]{1,0:T(8,128)(2,1)S(1)}, bf16[64,2048]{1,0:T(8,128)(2,1)S(1)}, u32[]{:S(2)}, u32[]{:S(2)}) collective-permute-start(bf16[64,2048]{1,0:T(8,128)(2,1)S(1)} %get-tuple-element.57), channel_id=1, source_target_pairs={{0,1},{1,0},{2,3},{3,2},{4,5},{5,4},{6,7},{7,6},{8,9},{9,8},{10,11... | collective-permute-start | bytes 786440 | tf_op jit(solution)/shard_map/ppermute | solution.py:519
  59.6 4.4 %collective-permute-start.21 = (bf16[16,2048]{1,0:T(8,128)(2,1)S(1)}, bf16[16,2048]{1,0:T(8,128)(2,1)S(1)}, u32[]{:S(2)}, u32[]{:S(2)}) collective-permute-start(bf16[16,2048]{1,0:T(8,128)(2,1)S(1)} %get-tuple-element.59), channel_id=1, source_target_pairs={{0,2},{2,0},{4,6},{6,4},{8,10},{10,8},{12,14},{14,12},{1,3},{3,1},... | collective-permute-start | bytes 196616 | tf_op jit(solution)/shard_map/ppermute | solution.py:512
  60.2 4.3 %collective-permute-start.22 = (bf16[16,2048]{1,0:T(8,128)(2,1)S(1)}, bf16[16,2048]{1,0:T(8,128)(2,1)S(1)}, u32[]{:S(2)}, u32[]{:S(2)}) collective-permute-start(bf16[16,2048]{1,0:T(8,128)(2,1)S(1)} %get-tuple-element.60), channel_id=1, source_target_pairs={{0,4},{2,6},{4,0},{6,2},{8,12},{10,14},{12,8},{14,10},{1,5},{3,7},... | collective-permute-start | bytes 196616 | tf_op jit(solution)/shard_map/ppermute | solution.py:512
  61.4 5.4 %collective-permute-start.23 = (bf16[16,2048]{1,0:T(8,128)(2,1)S(1)}, bf16[16,2048]{1,0:T(8,128)(2,1)S(1)}, u32[]{:S(2)}, u32[]{:S(2)}) collective-permute-start(bf16[16,2048]{1,0:T(8,128)(2,1)S(1)} %get-tuple-element.61), channel_id=1, source_target_pairs={{0,6},{2,4},{4,2},{6,0},{8,14},{10,12},{12,10},{14,8},{1,7},{3,5},... | collective-permute-start | bytes 196616 | tf_op jit(solution)/shard_map/ppermute | solution.py:512
  66.8 4.9 %collective-permute-start.24 = (bf16[8,2048]{1,0:T(8,128)(2,1)S(1)}, bf16[8,2048]{1,0:T(8,128)(2,1)S(1)}, u32[]{:S(2)}, u32[]{:S(2)}) collective-permute-start(bf16[8,2048]{1,0:T(8,128)(2,1)S(1)} %get-tuple-element.63), channel_id=1, source_target_pairs={{0,8},{2,10},{4,12},{6,14},{8,0},{10,2},{12,4},{14,6},{1,9},{3,11}... | collective-permute-start | bytes 98312 | tf_op jit(solution)/shard_map/ppermute | solution.py:637
